TPU v7x, 32 devices: a whole 2x2x4 slice. The times are simulated.
32 devices in a mesh: dp: 8 (over z, y), mp: 4 (over x, core).
Axes of the slice: x: 2, y: 2, z: 4, core: 2. Of those that a mesh axis runs over, the one named last changes fastest.
Arguments:
- latents: float32 [10240, 1024], P(('dp', 'mp')), may hold values from -6 to 6
- cotangent: float32 [10240, 1024], P(('dp', 'mp')), may hold values from -6 to 6
- text_embed: bfloat16 [4, 77, 1024], replicated, may hold values from -6 to 6
- text_mask: int32 [4, 77], replicated, may hold values 0 or 1
- band_ids: int32 [4], replicated, may hold values from 0 to 3, as said below
- rel_index_s: int32 [256, 256], replicated, may hold values from 0 to 1023
- rel_index_t: int32 [320, 320], replicated, may hold values from 0 to 2047
- modulation: float32 [4, 18, 1024], replicated, may hold values from -3 to 3
- qkv_master: float32 [2, 1024, 3072], P(None, 'dp', 'mp'), may hold values from -0.1875 to 0.1875
- out_master: float32 [2, 1024, 1024], P(None, 'mp', 'dp'), may hold values from -0.75 to 0.75
- cq_master: float32 [2, 1024, 1024], P(None, 'dp', 'mp'), may hold values from -0.1875 to 0.1875
- ckv_master: float32 [2, 1024, 2048], P(None, 'dp', 'mp'), may hold values from -0.1875 to 0.1875
- cout_master: float32 [2, 1024, 1024], P(None, 'mp', 'dp'), may hold values from -0.5 to 0.5
- up_master: float32 [2, 1024, 4096], P(None, 'dp', 'mp'), may hold values from -0.1875 to 0.1875
- down_master: float32 [2, 4096, 1024], P(None, 'mp', 'dp'), may hold values from -0.09375 to 0.09375
- rel_s_master: float32 [16, 1024], P('mp', 'dp'), may hold values from -4 to 4
- rel_t_master: float32 [16, 2048], P('mp', 'dp'), may hold values from -4 to 4
- qkv_first: float32 [2, 1024, 3072], P(None, 'dp', 'mp'), may hold values from -32 to 32
- out_first: float32 [2, 1024, 1024], P(None, 'mp', 'dp'), may hold values from -16 to 16
- cq_first: float32 [2, 1024, 1024], P(None, 'dp', 'mp'), may hold values from -96 to 96
- ckv_first: float32 [2, 1024, 2048], P(None, 'dp', 'mp'), may hold values from -80 to 80
- cout_first: float32 [2, 1024, 1024], P(None, 'mp', 'dp'), may hold values from -24 to 24
- up_first: float32 [2, 1024, 4096], P(None, 'dp', 'mp'), may hold values from -20 to 20
- down_first: float32 [2, 4096, 1024], P(None, 'mp', 'dp'), may hold values from -40 to 40
- rel_s_first: float32 [16, 1024], P('mp', 'dp'), may hold values from -12 to 12
- rel_t_first: float32 [16, 2048], P('mp', 'dp'), may hold values from -4 to 4
- qkv_second: float32 [2, 1024, 3072], P(None, 'dp', 'mp'), may hold values from 153.6 to 616
- out_second: float32 [2, 1024, 1024], P(None, 'mp', 'dp'), may hold values from 38.4 to 153.6
- cq_second: float32 [2, 1024, 1024], P(None, 'dp', 'mp'), may hold values from 1140.48 to 4567.2
- ckv_second: float32 [2, 1024, 2048], P(None, 'dp', 'mp'), may hold values from 792 to 3168
- cout_second: float32 [2, 1024, 1024], P(None, 'mp', 'dp'), may hold values from 71.28 to 285.12
- up_second: float32 [2, 1024, 4096], P(None, 'dp', 'mp'), may hold values from 55.296 to 221.184
- down_second: float32 [2, 4096, 1024], P(None, 'mp', 'dp'), may hold values from 221.184 to 884.736
- rel_s_second: float32 [16, 1024], P('mp', 'dp'), may hold values from 17.28 to 69.2
- rel_t_second: float32 [16, 2048], P('mp', 'dp'), may hold values from 8.64 to 34.6
Outputs:
- outputs: float32 [10240, 1024], P(('dp', 'mp'))
- grad_latents: float32 [10240, 1024], P(('dp', 'mp'))
- grad_modulation: float32 [4, 18, 1024], replicated
- qkv_new: float32 [2, 1024, 3072], P(None, 'dp', 'mp')
- qkv_first_new: float32 [2, 1024, 3072], P(None, 'dp', 'mp')
- qkv_second_new: float32 [2, 1024, 3072], P(None, 'dp', 'mp')
- qkv_low: bfloat16 [2, 1024, 3072], P(None, 'dp', 'mp')
- out_new: float32 [2, 1024, 1024], P(None, 'mp', 'dp')
- out_first_new: float32 [2, 1024, 1024], P(None, 'mp', 'dp')
- out_second_new: float32 [2, 1024, 1024], P(None, 'mp', 'dp')
- out_low: bfloat16 [2, 1024, 1024], P(None, 'mp', 'dp')
- cq_new: float32 [2, 1024, 1024], P(None, 'dp', 'mp')
- cq_first_new: float32 [2, 1024, 1024], P(None, 'dp', 'mp')
- cq_second_new: float32 [2, 1024, 1024], P(None, 'dp', 'mp')
- cq_low: bfloat16 [2, 1024, 1024], P(None, 'dp', 'mp')
- ckv_new: float32 [2, 1024, 2048], P(None, 'dp', 'mp')
- ckv_first_new: float32 [2, 1024, 2048], P(None, 'dp', 'mp')
- ckv_second_new: float32 [2, 1024, 2048], P(None, 'dp', 'mp')
- ckv_low: bfloat16 [2, 1024, 2048], P(None, 'dp', 'mp')
- cout_new: float32 [2, 1024, 1024], P(None, 'mp', 'dp')
- cout_first_new: float32 [2, 1024, 1024], P(None, 'mp', 'dp')
- cout_second_new: float32 [2, 1024, 1024], P(None, 'mp', 'dp')
- cout_low: bfloat16 [2, 1024, 1024], P(None, 'mp', 'dp')
- up_new: float32 [2, 1024, 4096], P(None, 'dp', 'mp')
- up_first_new: float32 [2, 1024, 4096], P(None, 'dp', 'mp')
- up_second_new: float32 [2, 1024, 4096], P(None, 'dp', 'mp')
- up_low: bfloat16 [2, 1024, 4096], P(None, 'dp', 'mp')
- down_new: float32 [2, 4096, 1024], P(None, 'mp', 'dp')
- down_first_new: float32 [2, 4096, 1024], P(None, 'mp', 'dp')
- down_second_new: float32 [2, 4096, 1024], P(None, 'mp', 'dp')
- down_low: bfloat16 [2, 4096, 1024], P(None, 'mp', 'dp')
- rel_s_new: float32 [16, 1024], P('mp', 'dp')
- rel_s_first_new: float32 [16, 1024], P('mp', 'dp')
- rel_s_second_new: float32 [16, 1024], P('mp', 'dp')
- rel_s_low: bfloat16 [16, 1024], P('mp', 'dp')
- rel_t_new: float32 [16, 2048], P('mp', 'dp')
- rel_t_first_new: float32 [16, 2048], P('mp', 'dp')
- rel_t_second_new: float32 [16, 2048], P('mp', 'dp')
- rel_t_low: bfloat16 [16, 2048], P('mp', 'dp')
Inputs may be any that keep to these rules, and one draw needn't show every extreme that they name: `band_ids`: the first and the last clip share one band; clip 1 lies in another band.
All inputs are finite; a program needn't handle non-finite values.
Results may differ from a plain program's by a relative error of at most 0.028.
Values may be sent and summed in bfloat16 or wider, within the bound.
No kernel may reach another device: no remote copies, remote signals or barrier semaphores. Data moves between devices by JAX's collectives and lax.ppermute only.
A program may use at most 320 MiB of HBM per device.

v0:
```python
import jax
import jax.numpy as jnp
from jax import lax
from jax.sharding import PartitionSpec as P

D = 1024
HD = 64
FF = 4096
FRAMES = 5
SIDE = 16
LAYERS = 2
STEP = 10


BETA_ONE = 0.9
BETA_TWO = 0.95
ADAM_EPS = 1e-08
DECAY_RATE = 0.1


def learning_rates():
    inverse_root = D ** (-0.5)
    return (
        1.5 * inverse_root,
        6.0 * inverse_root,
        1.5 * inverse_root,
        1.5 * inverse_root,
        4.2 * inverse_root,
        1.5 * inverse_root,
        1.5 * FF ** (-0.5),
        1.5,
        1.5,
    )


def layer_norm(tensor):
    center = tensor - jnp.mean(tensor, axis=-1, keepdims=True)
    inverse = lax.rsqrt(jnp.mean(center * center, axis=-1, keepdims=True) + 1e-06)
    return (center * inverse, inverse)


def norm_back(grad_norm, normed, inverse):
    return inverse * (
        grad_norm
        - jnp.mean(grad_norm, axis=-1, keepdims=True)
        - normed * jnp.mean(grad_norm * normed, axis=-1, keepdims=True)
    )


def modulate_back(grad_latent, grad_input, normed, inverse, scaling):
    grad_norm = grad_input * (1.0 + scaling)
    return (
        grad_latent + norm_back(grad_norm, normed, inverse),
        jnp.sum(grad_input, axis=0),
        jnp.sum(grad_input * normed, axis=0),
    )


def contract_last(matrix, weight):
    return lax.dot_general(
        matrix, weight, (((1,), (1,)), ((), ())), preferred_element_type=jnp.float32
    )


def contract_first(matrix, weight):
    return lax.dot_general(
        matrix, weight, (((0,), (0,)), ((), ())), preferred_element_type=jnp.float32
    )


def gelu_tanh(tensor):
    return jax.nn.gelu(tensor, approximate=True)


def to_windows(tensor, window_kind):
    trailing = tensor.shape[1:]
    if window_kind == 0:
        return tensor.reshape((FRAMES, SIDE * SIDE) + trailing)
    halfway = SIDE // 2
    tensor = tensor.reshape((FRAMES, 2, halfway, 2, halfway) + trailing)
    tensor = jnp.transpose(tensor, (1, 3, 0, 2, 4) + tuple(range(5, 5 + len(trailing))))
    return tensor.reshape((4, FRAMES * halfway * halfway) + trailing)


def from_windows(tensor, window_kind):
    trailing = tensor.shape[2:]
    if window_kind == 0:
        return tensor.reshape((FRAMES * SIDE * SIDE,) + trailing)
    halfway = SIDE // 2
    tensor = tensor.reshape((2, 2, FRAMES, halfway, halfway) + trailing)
    tensor = jnp.transpose(tensor, (2, 0, 3, 1, 4) + tuple(range(5, 5 + len(trailing))))
    return tensor.reshape((FRAMES * SIDE * SIDE,) + trailing)


def gather_rows(sending):
    return lax.all_gather(sending, "mp", axis=0, tiled=True)


def gather_grads(sending):
    return lax.all_gather(sending, "mp", axis=0, tiled=True)


def branch_sum(matrix, weight):
    return lax.psum_scatter(
        jnp.dot(matrix, weight, preferred_element_type=jnp.float32).astype(jnp.bfloat16),
        "mp",
        scatter_dimension=0,
        tiled=True,
    ).astype(jnp.float32)


def project_heads(mixed, weight):
    return branch_sum(mixed, weight)


def input_grad_sum(matrix, weight):
    return lax.psum_scatter(
        contract_last(matrix, weight).astype(jnp.bfloat16), "mp", scatter_dimension=0, tiled=True
    ).astype(jnp.float32)


def fetch_weights(masters, layer_index):
    return (
        lax.all_gather(masters[0][layer_index].astype(jnp.bfloat16), "dp", axis=0, tiled=True),
        lax.all_gather(masters[1][layer_index].astype(jnp.bfloat16), "dp", axis=1, tiled=True),
        lax.all_gather(masters[2][layer_index].astype(jnp.bfloat16), "dp", axis=0, tiled=True),
        lax.all_gather(masters[3][layer_index].astype(jnp.bfloat16), "dp", axis=0, tiled=True),
        lax.all_gather(masters[4][layer_index].astype(jnp.bfloat16), "dp", axis=1, tiled=True),
        lax.all_gather(masters[5][layer_index].astype(jnp.bfloat16), "dp", axis=0, tiled=True),
        lax.all_gather(masters[6][layer_index].astype(jnp.bfloat16), "dp", axis=1, tiled=True),
        lax.all_gather(masters[7 + layer_index].astype(jnp.bfloat16), "dp", axis=1, tiled=True),
    )


def window_parts(qkv, window_kind):
    heads_local = qkv.shape[1] // (3 * HD)
    windows = to_windows(qkv.reshape(qkv.shape[0], heads_local, 3, HD), window_kind)
    return (windows[:, :, :, 0], windows[:, :, :, 1], windows[:, :, :, 2])


def self_scores(queries, key_rows, table, index_table):
    bias = table.astype(jnp.float32)[:, index_table]
    return (
        jnp.einsum("wnhe,wmhe->whnm", queries, key_rows, preferred_element_type=jnp.float32)
        * HD ** (-0.5)
        + bias[None]
    )


def self_forward(gathered, w_qkv, table, index_table, window_kind):
    qkv = jnp.dot(gathered, w_qkv, preferred_element_type=jnp.float32).astype(jnp.bfloat16)
    queries, key_rows, values = window_parts(qkv, window_kind)
    scores = self_scores(queries, key_rows, table, index_table)
    log_total = jax.nn.logsumexp(scores, axis=-1, keepdims=True)
    probs = jnp.exp(scores - log_total).astype(jnp.bfloat16)
    mixed = jnp.einsum("whnm,wmhe->wnhe", probs, values, preferred_element_type=jnp.float32)
    mixed = from_windows(mixed, window_kind)
    return (qkv, log_total, mixed.reshape(mixed.shape[0], -1).astype(jnp.bfloat16))


def self_backward(
    gathered, w_out, table, index_table, window_kind, qkv, log_total, mixed, grad_rows
):
    grad_mixed = contract_last(grad_rows, w_out).astype(jnp.bfloat16)
    grad_out_w = contract_first(mixed, grad_rows)
    queries, key_rows, values = window_parts(qkv, window_kind)
    heads_local = queries.shape[2]
    grad_windows = to_windows(grad_mixed.reshape(grad_mixed.shape[0], heads_local, HD), window_kind)
    scores = self_scores(queries, key_rows, table, index_table)
    probs = jnp.exp(scores - log_total)
    grad_probs = jnp.einsum(
        "wnhe,wmhe->whnm", grad_windows, values, preferred_element_type=jnp.float32
    )
    row_dot = jnp.sum(probs * grad_probs, axis=-1, keepdims=True)
    grad_scores = (probs * (grad_probs - row_dot)).astype(jnp.bfloat16)
    scaling = HD ** (-0.5)
    grad_query = (
        jnp.einsum("whnm,wmhe->wnhe", grad_scores, key_rows, preferred_element_type=jnp.float32)
        * scaling
    )
    grad_key = (
        jnp.einsum("whnm,wnhe->wmhe", grad_scores, queries, preferred_element_type=jnp.float32)
        * scaling
    )
    grad_value = jnp.einsum(
        "whnm,wnhe->wmhe",
        probs.astype(jnp.bfloat16),
        grad_windows,
        preferred_element_type=jnp.float32,
    )
    grad_qkv = from_windows(jnp.stack([grad_query, grad_key, grad_value], axis=3), window_kind)
    grad_qkv = grad_qkv.reshape(grad_qkv.shape[0], -1).astype(jnp.bfloat16)
    summed = jnp.sum(grad_scores, axis=0, dtype=jnp.float32).reshape(heads_local, -1)
    grad_table = jax.ops.segment_sum(
        summed.T, index_table.reshape(-1), num_segments=table.shape[1]
    ).T
    grad_qkv_w = contract_first(gathered, grad_qkv)
    return (grad_qkv, grad_qkv_w, grad_out_w, grad_table)


def cross_split(query_flat, keyval):
    heads_local = query_flat.shape[1] // HD
    return (
        query_flat.reshape(query_flat.shape[0], heads_local, HD),
        keyval.reshape(keyval.shape[0], heads_local, 2, HD),
    )


def cross_scores(queries, key_rows, valid_bias):
    return (
        jnp.einsum("nhe,mhe->hnm", queries, key_rows, preferred_element_type=jnp.float32)
        * HD ** (-0.5)
        + valid_bias
    )


def cross_forward(gathered, w_cq, w_ckv, text_rows, valid_bias):
    query_flat = jnp.dot(gathered, w_cq, preferred_element_type=jnp.float32).astype(jnp.bfloat16)
    keyval = jnp.dot(text_rows, w_ckv, preferred_element_type=jnp.float32).astype(jnp.bfloat16)
    queries, paired = cross_split(query_flat, keyval)
    scores = cross_scores(queries, paired[:, :, 0], valid_bias)
    log_total = jax.nn.logsumexp(scores, axis=-1, keepdims=True)
    probs = jnp.exp(scores - log_total).astype(jnp.bfloat16)
    mixed = jnp.einsum("hnm,mhe->nhe", probs, paired[:, :, 1], preferred_element_type=jnp.float32)
    return (query_flat, keyval, log_total, mixed.reshape(mixed.shape[0], -1).astype(jnp.bfloat16))


def cross_backward(
    gathered, w_cout, text_rows, valid_bias, query_flat, keyval, log_total, mixed, grad_rows
):
    grad_mixed = contract_last(grad_rows, w_cout).astype(jnp.bfloat16)
    grad_cout_w = contract_first(mixed, grad_rows)
    queries, paired = cross_split(query_flat, keyval)
    grad_heads = grad_mixed.reshape(queries.shape)
    scores = cross_scores(queries, paired[:, :, 0], valid_bias)
    probs = jnp.exp(scores - log_total)
    grad_probs = jnp.einsum(
        "nhe,mhe->hnm", grad_heads, paired[:, :, 1], preferred_element_type=jnp.float32
    )
    row_dot = jnp.sum(probs * grad_probs, axis=-1, keepdims=True)
    grad_scores = (probs * (grad_probs - row_dot)).astype(jnp.bfloat16)
    scaling = HD ** (-0.5)
    grad_query = (
        jnp.einsum("hnm,mhe->nhe", grad_scores, paired[:, :, 0], preferred_element_type=jnp.float32)
        * scaling
    )
    grad_query = grad_query.reshape(query_flat.shape).astype(jnp.bfloat16)
    grad_key = (
        jnp.einsum("hnm,nhe->mhe", grad_scores, queries, preferred_element_type=jnp.float32)
        * scaling
    )
    grad_value = jnp.einsum(
        "hnm,nhe->mhe", probs.astype(jnp.bfloat16), grad_heads, preferred_element_type=jnp.float32
    )
    grad_keyval = (
        jnp.stack([grad_key, grad_value], axis=2).reshape(keyval.shape).astype(jnp.bfloat16)
    )
    grad_cq_w = contract_first(gathered, grad_query)
    grad_ckv_w = contract_first(text_rows, grad_keyval)
    return (grad_query, grad_cq_w, grad_ckv_w, grad_cout_w)


def adam_update(master, first, second, grad, rate):
    first_new = BETA_ONE * first + (1.0 - BETA_ONE) * grad
    second_new = BETA_TWO * second + (1.0 - BETA_TWO) * grad * grad
    step_size = (
        first_new
        / (1.0 - BETA_ONE**STEP)
        / (jnp.sqrt(second_new / (1.0 - BETA_TWO**STEP)) + ADAM_EPS)
    )
    master_new = master - rate * (step_size + DECAY_RATE * master)
    return (master_new, first_new, second_new, master_new.astype(jnp.bfloat16))


def body(
    latents,
    cotangent,
    text_embed,
    text_mask,
    band_ids,
    rel_index_s,
    rel_index_t,
    modulation,
    qkv_master,
    out_master,
    cq_master,
    ckv_master,
    cout_master,
    up_master,
    down_master,
    rel_s_master,
    rel_t_master,
    qkv_first,
    out_first,
    cq_first,
    ckv_first,
    cout_first,
    up_first,
    down_first,
    rel_s_first,
    rel_t_first,
    qkv_second,
    out_second,
    cq_second,
    ckv_second,
    cout_second,
    up_second,
    down_second,
    rel_s_second,
    rel_t_second,
):
    masters = (
        qkv_master,
        out_master,
        cq_master,
        ckv_master,
        cout_master,
        up_master,
        down_master,
        rel_s_master,
        rel_t_master,
    )
    firsts = (
        qkv_first,
        out_first,
        cq_first,
        ckv_first,
        cout_first,
        up_first,
        down_first,
        rel_s_first,
        rel_t_first,
    )
    seconds = (
        qkv_second,
        out_second,
        cq_second,
        ckv_second,
        cout_second,
        up_second,
        down_second,
        rel_s_second,
        rel_t_second,
    )
    rates = learning_rates()
    clip_index = lax.axis_index("dp") // 2
    text_rows = lax.dynamic_index_in_dim(text_embed, clip_index, 0, keepdims=False)
    mask_row = lax.dynamic_index_in_dim(text_mask, clip_index, 0, keepdims=False)
    first_token = (jnp.arange(mask_row.shape[0], dtype=jnp.int32) == 0).astype(jnp.int32)
    valid_bias = (jnp.maximum(mask_row, first_token).astype(jnp.float32) - 1.0) * 1000000000.0
    band_now = lax.dynamic_index_in_dim(band_ids, clip_index, 0, keepdims=False)
    selector = (jnp.arange(modulation.shape[0], dtype=jnp.int32) == band_now).astype(jnp.float32)
    mod_rows = jnp.sum(selector[:, None, None] * modulation, axis=0)
    index_tables = (rel_index_s, rel_index_t)
    latent = latents
    saved = []
    gathered_weights = []
    for layer_index in range(LAYERS):
        weights_now = fetch_weights(masters, layer_index)
        gathered_weights.append(weights_now)
        w_qkv, w_out, w_cq, w_ckv, w_cout, w_up, w_down, table = weights_now
        base = 9 * layer_index
        record = {}
        normed, inverse = layer_norm(latent)
        record["norm_a"] = (normed, inverse)
        gathered = gather_rows(
            (normed * (1.0 + mod_rows[base + 1]) + mod_rows[base]).astype(jnp.bfloat16)
        )
        qkv, log_total, mixed = self_forward(
            gathered, w_qkv, table, index_tables[layer_index], layer_index
        )
        branch = project_heads(mixed, w_out)
        record["self"] = (gathered, qkv, log_total, mixed, branch)
        latent = latent + mod_rows[base + 2] * branch
        normed, inverse = layer_norm(latent)
        record["norm_c"] = (normed, inverse)
        gathered = gather_rows(
            (normed * (1.0 + mod_rows[base + 4]) + mod_rows[base + 3]).astype(jnp.bfloat16)
        )
        query_flat, keyval, log_total, mixed = cross_forward(
            gathered, w_cq, w_ckv, text_rows, valid_bias
        )
        branch = project_heads(mixed, w_cout)
        record["cross"] = (gathered, query_flat, keyval, log_total, mixed, branch)
        latent = latent + mod_rows[base + 5] * branch
        normed, inverse = layer_norm(latent)
        record["norm_m"] = (normed, inverse)
        gathered = gather_rows(
            (normed * (1.0 + mod_rows[base + 7]) + mod_rows[base + 6]).astype(jnp.bfloat16)
        )
        hidden = jnp.dot(gathered, w_up, preferred_element_type=jnp.float32)
        active = gelu_tanh(hidden).astype(jnp.bfloat16)
        branch = branch_sum(active, w_down)
        record["feed"] = (gathered, hidden, active, branch)
        latent = latent + mod_rows[base + 8] * branch
        saved.append(record)
    grad_latent = cotangent
    mod_grads = [None, None]
    weight_grads = [None, None]
    reduced = [None, None]
    for layer_index in reversed(range(LAYERS)):
        w_qkv, w_out, w_cq, w_ckv, w_cout, w_up, w_down, table = gathered_weights[layer_index]
        base = 9 * layer_index
        record = saved[layer_index]
        gathered, hidden, active, branch = record["feed"]
        gate_m = jnp.sum(grad_latent * branch, axis=0)
        grad_rows = gather_grads((mod_rows[base + 8] * grad_latent).astype(jnp.bfloat16))
        grad_active = contract_last(grad_rows, w_down)
        unused, pullback = jax.vjp(gelu_tanh, hidden)
        grad_hidden = pullback(grad_active)[0].astype(jnp.bfloat16)
        grad_down_w = contract_first(active, grad_rows)
        grad_up_w = contract_first(gathered, grad_hidden)
        grad_input = input_grad_sum(grad_hidden, w_up)
        normed, inverse = record["norm_m"]
        grad_latent, shift_m, scale_m = modulate_back(
            grad_latent, grad_input, normed, inverse, mod_rows[base + 7]
        )
        gathered, query_flat, keyval, log_total, mixed, branch = record["cross"]
        gate_c = jnp.sum(grad_latent * branch, axis=0)
        grad_rows = gather_grads((mod_rows[base + 5] * grad_latent).astype(jnp.bfloat16))
        grad_query, grad_cq_w, grad_ckv_w, grad_cout_w = cross_backward(
            gathered, w_cout, text_rows, valid_bias, query_flat, keyval, log_total, mixed, grad_rows
        )
        grad_input = input_grad_sum(grad_query, w_cq)
        normed, inverse = record["norm_c"]
        grad_latent, shift_c, scale_c = modulate_back(
            grad_latent, grad_input, normed, inverse, mod_rows[base + 4]
        )
        gathered, qkv, log_total, mixed, branch = record["self"]
        gate_a = jnp.sum(grad_latent * branch, axis=0)
        grad_rows = gather_grads((mod_rows[base + 2] * grad_latent).astype(jnp.bfloat16))
        grad_qkv, grad_qkv_w, grad_out_w, grad_table = self_backward(
            gathered,
            w_out,
            table,
            index_tables[layer_index],
            layer_index,
            qkv,
            log_total,
            mixed,
            grad_rows,
        )
        grad_input = input_grad_sum(grad_qkv, w_qkv)
        normed, inverse = record["norm_a"]
        grad_latent, shift_a, scale_a = modulate_back(
            grad_latent, grad_input, normed, inverse, mod_rows[base + 1]
        )
        mod_grads[layer_index] = [
            shift_a,
            scale_a,
            gate_a,
            shift_c,
            scale_c,
            gate_c,
            shift_m,
            scale_m,
            gate_m,
        ]
        weight_grads[layer_index] = (
            grad_qkv_w,
            grad_out_w,
            grad_cq_w,
            grad_ckv_w,
            grad_cout_w,
            grad_up_w,
            grad_down_w,
            grad_table,
        )
    lower_set = weight_grads[0]
    upper_set = weight_grads[1]
    summed_all = (
        lax.psum_scatter(lower_set[0], "dp", scatter_dimension=0, tiled=True),
        lax.psum_scatter(lower_set[1], "dp", scatter_dimension=1, tiled=True),
        lax.psum_scatter(lower_set[2], "dp", scatter_dimension=0, tiled=True),
        lax.psum_scatter(lower_set[3], "dp", scatter_dimension=0, tiled=True),
        lax.psum_scatter(lower_set[4], "dp", scatter_dimension=1, tiled=True),
        lax.psum_scatter(lower_set[5], "dp", scatter_dimension=0, tiled=True),
        lax.psum_scatter(lower_set[6], "dp", scatter_dimension=1, tiled=True),
        lax.psum_scatter(lower_set[7], "dp", scatter_dimension=1, tiled=True),
        lax.psum_scatter(upper_set[0], "dp", scatter_dimension=0, tiled=True),
        lax.psum_scatter(upper_set[1], "dp", scatter_dimension=1, tiled=True),
        lax.psum_scatter(upper_set[2], "dp", scatter_dimension=0, tiled=True),
        lax.psum_scatter(upper_set[3], "dp", scatter_dimension=0, tiled=True),
        lax.psum_scatter(upper_set[4], "dp", scatter_dimension=1, tiled=True),
        lax.psum_scatter(upper_set[5], "dp", scatter_dimension=0, tiled=True),
        lax.psum_scatter(upper_set[6], "dp", scatter_dimension=1, tiled=True),
        lax.psum_scatter(upper_set[7], "dp", scatter_dimension=1, tiled=True),
    )
    reduced = [summed_all[:8], summed_all[8:]]
    mod_local = jnp.stack(mod_grads[0] + mod_grads[1], axis=0)
    grad_modulation = lax.psum(selector[:, None, None] * mod_local[None], ("dp", "mp"))
    grads = [jnp.stack([reduced[0][item], reduced[1][item]], axis=0) for item in range(7)]
    grads.append(reduced[0][7])
    grads.append(reduced[1][7])
    results = [latent, grad_latent, grad_modulation]
    for item in range(9):
        results.extend(
            adam_update(masters[item], firsts[item], seconds[item], grads[item], rates[item])
        )
    return tuple(results)


def solution(mesh):
    in_specs = (
        P(("dp", "mp"), None),
        P(("dp", "mp"), None),
        P(),
        P(),
        P(),
        P(),
        P(),
        P(),
        P(None, "dp", "mp"),
        P(None, "mp", "dp"),
        P(None, "dp", "mp"),
        P(None, "dp", "mp"),
        P(None, "mp", "dp"),
        P(None, "dp", "mp"),
        P(None, "mp", "dp"),
        P("mp", "dp"),
        P("mp", "dp"),
        P(None, "dp", "mp"),
        P(None, "mp", "dp"),
        P(None, "dp", "mp"),
        P(None, "dp", "mp"),
        P(None, "mp", "dp"),
        P(None, "dp", "mp"),
        P(None, "mp", "dp"),
        P("mp", "dp"),
        P("mp", "dp"),
        P(None, "dp", "mp"),
        P(None, "mp", "dp"),
        P(None, "dp", "mp"),
        P(None, "dp", "mp"),
        P(None, "mp", "dp"),
        P(None, "dp", "mp"),
        P(None, "mp", "dp"),
        P("mp", "dp"),
        P("mp", "dp"),
    )
    out_specs = (
        P(("dp", "mp"), None),
        P(("dp", "mp"), None),
        P(),
        P(None, "dp", "mp"),
        P(None, "dp", "mp"),
        P(None, "dp", "mp"),
        P(None, "dp", "mp"),
        P(None, "mp", "dp"),
        P(None, "mp", "dp"),
        P(None, "mp", "dp"),
        P(None, "mp", "dp"),
        P(None, "dp", "mp"),
        P(None, "dp", "mp"),
        P(None, "dp", "mp"),
        P(None, "dp", "mp"),
        P(None, "dp", "mp"),
        P(None, "dp", "mp"),
        P(None, "dp", "mp"),
        P(None, "dp", "mp"),
        P(None, "mp", "dp"),
        P(None, "mp", "dp"),
        P(None, "mp", "dp"),
        P(None, "mp", "dp"),
        P(None, "dp", "mp"),
        P(None, "dp", "mp"),
        P(None, "dp", "mp"),
        P(None, "dp", "mp"),
        P(None, "mp", "dp"),
        P(None, "mp", "dp"),
        P(None, "mp", "dp"),
        P(None, "mp", "dp"),
        P("mp", "dp"),
        P("mp", "dp"),
        P("mp", "dp"),
        P("mp", "dp"),
        P("mp", "dp"),
        P("mp", "dp"),
        P("mp", "dp"),
        P("mp", "dp"),
    )
    return jax.shard_map(body, mesh=mesh, in_specs=in_specs, out_specs=out_specs, check_vma=False)
```

profile of v0, /device:TPU:0, one launch (start us, length us, event | category | flops | bytes accessed | tf_op | source)
XLA Modules:
  0.0 3843.9 jit_solution(6554763601456340581)
XLA Ops:
  36.2 215.9 %gather_fusion = f32[65536,4]{1,0:T(8,128)} fusion(f32[4,1024]{0,1:T(8,128)S(1)} %copy.387, s32[65536]{0:T(1024)S(1)} %broadcast_clamp_fusion.1), kind=kCustom, calls=%fused_computation | custom fusion | bytes 2359296 | tf_op jit(solution)/shard_map/gather | solution.py:142
  397.1 32.2 all-gather.3
  475.1 32.7 reduce-scatter.35.cloned.1.call-done
  512.1 47.7 %all-gather.63.cloned.1.call-done = bf16[1,1024,1024]{2,1,0:T(8,128)(2,1)} async-done(((bf16[1,128,1024]{2,1,0:T(8,128)(2,1)}), bf16[1,1024,1024]{2,1,0:T(8,128)(2,1)}) %all-gather.63.cloned.1.call-update) | async-done | bytes 2097168 | tf_op jit(solution)/shard_map/all_gather | solution.py:129
  593.8 46.0 %all-gather.65.cloned.1.call-done = bf16[1,1024,1024]{2,1,0:T(8,128)(2,1)} async-done(((bf16[1,1024,128]{2,1,0:T(8,128)(2,1)}), bf16[1,1024,1024]{2,1,0:T(8,128)(2,1)}) %all-gather.65.cloned.1.call-update) | async-done | bytes 2097168 | tf_op jit(solution)/shard_map/all_gather | solution.py:130
  648.5 32.2 reduce-scatter.37.cloned.1.call-done
  711.4 337.0 %gather_fusion.1 = f32[102400,4]{1,0:T(8,128)} fusion(f32[4,2048]{0,1:T(8,128)S(1)} %copy.398, s32[102400]{0:T(1024)S(1)} %broadcast_clamp_fusion), kind=kCustom, calls=%fused_computation.1 | custom fusion | bytes 3686400 | tf_op jit(solution)/shard_map/gather | solution.py:142
  1048.3 32.2 copy.399
  1180.6 34.4 all-gather.10
  1256.9 34.2 reduce-scatter.41.cloned.1.call-done
  1295.9 47.3 %all-gather.71.cloned.1.call-done = bf16[1,1024,1024]{2,1,0:T(8,128)(2,1)} async-done(((bf16[1,128,1024]{2,1,0:T(8,128)(2,1)}), bf16[1,1024,1024]{2,1,0:T(8,128)(2,1)}) %all-gather.71.cloned.1.call-update) | async-done | bytes 2097168 | tf_op jit(solution)/shard_map/all_gather | solution.py:129
  1376.9 46.4 %all-gather.73.cloned.1.call-done = bf16[1,1024,1024]{2,1,0:T(8,128)(2,1)} async-done(((bf16[1,1024,128]{2,1,0:T(8,128)(2,1)}), bf16[1,1024,1024]{2,1,0:T(8,128)(2,1)}) %all-gather.73.cloned.1.call-update) | async-done | bytes 2097168 | tf_op jit(solution)/shard_map/all_gather | solution.py:130
  1431.4 32.9 reduce-scatter.43.cloned.1.call-done
  1508.2 34.8 reduce-scatter.45.cloned.1.call-done
  1586.4 34.8 reduce-scatter.47.cloned.1.call-done
  1707.6 34.8 reduce-scatter.49.cloned.1.call-done
  1789.0 34.8 reduce-scatter.51.cloned.1.call-done
  1863.7 34.8 reduce-scatter.53.cloned.1.call-done
  1936.6 543.4 %scatter_custom_fusion.1 = f32[2048,4]{1,0:T(8,128)} fusion(s32[102400]{0:T(1024)S(1)} %reshape.412, f32[102400,4]{1,0:T(8,128)} %copy.428, f32[]{:T(128)} %constant.67.clone.1), kind=kCustom, calls=%fused_computation.289 | custom fusion | flops 409600 | bytes 33280 | tf_op jit(solution)/shard_map/scatter-add | solution.py:194
  2578.6 348.3 %scatter_custom_fusion = f32[1024,4]{1,0:T(8,128)} fusion(s32[65536]{0:T(1024)S(1)} %bitcast.434, f32[65536,4]{1,0:T(8,128)} %copy.425, f32[]{:T(128)} %constant.67.clone.1), kind=kCustom, calls=%fused_computation.304 | custom fusion | flops 262144 | bytes 16896 | tf_op jit(solution)/shard_map/scatter-add | solution.py:194
  2976.8 66.6 %reduce-scatter.73.cloned.1.call-done = f32[256,128]{1,0:T(8,128)} async-done(((f32[256,1024]{1,0:T(8,128)}), f32[256,128]{1,0:T(8,128)}) %reduce-scatter.73.cloned.1.call-update) | async-done | bytes 131088 | tf_op jit(solution)/shard_map/reduce_scatter | solution.py:476
  3045.5 63.6 %reduce-scatter.67.cloned.1.call-done = f32[128,256]{1,0:T(8,128)} async-done(((f32[1024,256]{1,0:T(8,128)}), f32[128,256]{1,0:T(8,128)}) %reduce-scatter.67.cloned.1.call-update) | async-done | bytes 131088 | tf_op jit(solution)/shard_map/reduce_scatter | solution.py:482
  3109.1 66.2 %reduce-scatter.65.cloned.1.call-done = f32[128,256]{1,0:T(8,128)} async-done(((f32[1024,256]{1,0:T(8,128)}), f32[128,256]{1,0:T(8,128)}) %reduce-scatter.65.cloned.1.call-update) | async-done | bytes 131088 | tf_op jit(solution)/shard_map/reduce_scatter | solution.py:474
  3177.3 68.1 %reduce-scatter.71.cloned.1.call-done = f32[128,512]{1,0:T(8,128)} async-done(((f32[1024,512]{1,0:T(8,128)}), f32[128,512]{1,0:T(8,128)}) %reduce-scatter.71.cloned.1.call-update) | async-done | bytes 262160 | tf_op jit(solution)/shard_map/reduce_scatter | solution.py:483
  3245.5 70.3 %reduce-scatter.69.cloned.1.call-done = f32[128,512]{1,0:T(8,128)} async-done(((f32[1024,512]{1,0:T(8,128)}), f32[128,512]{1,0:T(8,128)}) %reduce-scatter.69.cloned.1.call-update) | async-done | bytes 262160 | tf_op jit(solution)/shard_map/reduce_scatter | solution.py:475
  3318.5 61.9 %reduce-scatter.85.cloned.1.call-done = f32[128,4]{1,0:T(8,128)} async-done(((f32[1024,4]{1,0:T(8,128)}), f32[128,4]{1,0:T(8,128)}) %reduce-scatter.85.cloned.1.call-update) | async-done | bytes 2064
  3382.0 65.1 %reduce-scatter.63.cloned.1.call-done = f32[256,128]{1,0:T(8,128)} async-done(((f32[256,1024]{1,0:T(8,128)}), f32[256,128]{1,0:T(8,128)}) %reduce-scatter.63.cloned.1.call-update) | async-done | bytes 131088 | tf_op jit(solution)/shard_map/reduce_scatter | solution.py:481
  3447.1 66.2 %reduce-scatter.61.cloned.1.call-done = f32[256,128]{1,0:T(8,128)} async-done(((f32[256,1024]{1,0:T(8,128)}), f32[256,128]{1,0:T(8,128)}) %reduce-scatter.61.cloned.1.call-update) | async-done | bytes 131088 | tf_op jit(solution)/shard_map/reduce_scatter | solution.py:473
  3515.6 33.9 reduce-scatter.55.cloned.1.call-done
  3555.1 72.4 %reduce-scatter.59.cloned.1.call-done = f32[128,768]{1,0:T(8,128)} async-done(((f32[1024,768]{1,0:T(8,128)}), f32[128,768]{1,0:T(8,128)}) %reduce-scatter.59.cloned.1.call-update) | async-done | bytes 393232 | tf_op jit(solution)/shard_map/reduce_scatter | solution.py:480
  3627.5 77.0 %reduce-scatter.57.cloned.1.call-done = f32[128,768]{1,0:T(8,128)} async-done(((f32[1024,768]{1,0:T(8,128)}), f32[128,768]{1,0:T(8,128)}) %reduce-scatter.57.cloned.1.call-update) | async-done | bytes 393232 | tf_op jit(solution)/shard_map/reduce_scatter | solution.py:472
  3708.4 126.7 %all-reduce.2.cloned.1.call-done = f32[4,18,1024]{2,0,1:T(4,128)} async-done(((f32[4,18,1024]{2,0,1:T(4,128)}), f32[4,18,1024]{2,0,1:T(4,128)}) %all-reduce.2.cloned.1.call-update) | async-done | bytes 294928 | tf_op jit(solution)/shard_map/psum | solution.py:491
  (714 shorter events, 951.6 us)
Async XLA Ops:
  7.3 292.6 %all-gather.59.cloned.1.call-start = ((), (), s32[]{:S(2)}) async-start(), calls=%async_computation.67 | async-start | bytes 1769472 | tf_op jit(solution)/shard_map/all_gather | solution.py:124
  9.4 290.4 %all-gather.35.cloned.1.call-start = ((), (), s32[]{:S(2)}) async-start(), calls=%async_computation.28 | async-start | bytes 3276800 | tf_op jit(solution)/shard_map/all_gather | solution.py:96
  13.4 378.9 %reduce-scatter.33.cloned.1.call-start = ((), (), s32[]{:S(2)}) async-start(), calls=%async_computation.29 | async-start | bytes 3276800 | tf_op jit(solution)/shard_map/reduce_scatter | solution.py:104
  395.9 111.9 %reduce-scatter.35.cloned.1.call-start = ((), (), s32[]{:S(2)}) async-start(), calls=%async_computation.31 | async-start | bytes 3276800 | tf_op jit(solution)/shard_map/reduce_scatter | solution.py:104
  510.7 129.0 %all-gather.65.cloned.1.call-start = ((), (), s32[]{:S(2)}) async-start(), calls=%async_computation.70 | async-start | bytes 2359296 | tf_op jit(solution)/shard_map/all_gather | solution.py:130
  512.1 168.7 %reduce-scatter.37.cloned.1.call-start = ((), (), s32[]{:S(2)}) async-start(), calls=%async_computation.33 | async-start | bytes 3276800 | tf_op jit(solution)/shard_map/reduce_scatter | solution.py:104
  647.7 460.6 %all-gather.67.cloned.1.call-start = ((), (), s32[]{:S(2)}) async-start(), calls=%async_computation.71 | async-start | bytes 1769472 | tf_op jit(solution)/shard_map/all_gather | solution.py:124
  648.5 459.8 %all-gather.41.cloned.1.call-start = ((), (), s32[]{:S(2)}) async-start(), calls=%async_computation.34 | async-start | bytes 3276800 | tf_op jit(solution)/shard_map/all_gather | solution.py:96
  684.3 492.2 %reduce-scatter.39.cloned.1.call-start = ((), (), s32[]{:S(2)}) async-start(), calls=%async_computation.35 | async-start | bytes 3276800 | tf_op jit(solution)/shard_map/reduce_scatter | solution.py:104
  1256.9 112.5 %all-gather.45.cloned.1.call-start = ((), (), s32[]{:S(2)}) async-start(), calls=%async_computation.38 | async-start | bytes 3276800 | tf_op jit(solution)/shard_map/all_gather | solution.py:96
  1295.1 128.2 %all-gather.73.cloned.1.call-start = ((), (), s32[]{:S(2)}) async-start(), calls=%async_computation.74 | async-start | bytes 2359296 | tf_op jit(solution)/shard_map/all_gather | solution.py:130
  1295.8 168.5 %reduce-scatter.43.cloned.1.call-start = ((), (), s32[]{:S(2)}) async-start(), calls=%async_computation.39 | async-start | bytes 3276800 | tf_op jit(solution)/shard_map/reduce_scatter | solution.py:104
  1628.9 113.4 %reduce-scatter.49.cloned.1.call-start = ((), (), s32[]{:S(2)}) async-start(), calls=%async_computation.45 | async-start | bytes 3276800 | tf_op jit(solution)/shard_map/reduce_scatter | solution.py:117
  1863.7 676.6 %all-gather.57.cloned.1.call-start = ((), (), s32[]{:S(2)}) async-start(), calls=%async_computation.50 | async-start | bytes 3276800 | tf_op jit(solution)/shard_map/all_gather | solution.py:100
  1905.2 1057.6 %reduce-scatter.87.cloned.1.call-start = ((), (), s32[]{:S(2)}) async-start(), calls=%async_computation.76 | async-start | bytes 1179648
  2480.0 484.4 %reduce-scatter.83.cloned.1.call-start = ((), (), s32[]{:S(2)}) async-start(), calls=%async_computation.66 | async-start | bytes 4718592 | tf_op jit(solution)/shard_map/reduce_scatter | solution.py:486
  2488.8 475.6 %reduce-scatter.81.cloned.1.call-start = ((), (), s32[]{:S(2)}) async-start(), calls=%async_computation.65 | async-start | bytes 4718592 | tf_op jit(solution)/shard_map/reduce_scatter | solution.py:478
  2497.6 471.1 %reduce-scatter.79.cloned.1.call-start = ((), (), s32[]{:S(2)}) async-start(), calls=%async_computation.64 | async-start | bytes 4718592 | tf_op jit(solution)/shard_map/reduce_scatter | solution.py:485
  2505.6 463.2 %reduce-scatter.77.cloned.1.call-start = ((), (), s32[]{:S(2)}) async-start(), calls=%async_computation.63 | async-start | bytes 4718592 | tf_op jit(solution)/shard_map/reduce_scatter | solution.py:477
  2513.1 463.7 %reduce-scatter.75.cloned.1.call-start = ((), (), s32[]{:S(2)}) async-start(), calls=%async_computation.62 | async-start | bytes 1179648 | tf_op jit(solution)/shard_map/reduce_scatter | solution.py:484
  2517.0 526.4 %reduce-scatter.73.cloned.1.call-start = ((), (), s32[]{:S(2)}) async-start(), calls=%async_computation.61 | async-start | bytes 1179648 | tf_op jit(solution)/shard_map/reduce_scatter | solution.py:476
  2520.7 588.3 %reduce-scatter.67.cloned.1.call-start = ((), (), s32[]{:S(2)}) async-start(), calls=%async_computation.58 | async-start | bytes 1179648 | tf_op jit(solution)/shard_map/reduce_scatter | solution.py:482
  2524.6 650.7 %reduce-scatter.65.cloned.1.call-start = ((), (), s32[]{:S(2)}) async-start(), calls=%async_computation.57 | async-start | bytes 1179648 | tf_op jit(solution)/shard_map/reduce_scatter | solution.py:474
  2528.5 717.0 %reduce-scatter.71.cloned.1.call-start = ((), (), s32[]{:S(2)}) async-start(), calls=%async_computation.60 | async-start | bytes 2359296 | tf_op jit(solution)/shard_map/reduce_scatter | solution.py:483
  2534.3 781.5 %reduce-scatter.69.cloned.1.call-start = ((), (), s32[]{:S(2)}) async-start(), calls=%async_computation.59 | async-start | bytes 2359296 | tf_op jit(solution)/shard_map/reduce_scatter | solution.py:475
  2539.6 840.9 %reduce-scatter.85.cloned.1.call-start = ((), (), s32[]{:S(2)}) async-start(), calls=%async_computation.75 | async-start | bytes 589824
  2926.9 520.2 %reduce-scatter.63.cloned.1.call-start = ((), (), s32[]{:S(2)}) async-start(), calls=%async_computation.56 | async-start | bytes 1179648 | tf_op jit(solution)/shard_map/reduce_scatter | solution.py:481
  2930.7 582.6 %reduce-scatter.61.cloned.1.call-start = ((), (), s32[]{:S(2)}) async-start(), calls=%async_computation.55 | async-start | bytes 1179648 | tf_op jit(solution)/shard_map/reduce_scatter | solution.py:473
  2934.5 615.0 %reduce-scatter.55.cloned.1.call-start = ((), (), s32[]{:S(2)}) async-start(), calls=%async_computation.51 | async-start | bytes 3276800 | tf_op jit(solution)/shard_map/reduce_scatter | solution.py:117
  2948.0 679.6 %reduce-scatter.59.cloned.1.call-start = ((), (), s32[]{:S(2)}) async-start(), calls=%async_computation.54 | async-start | bytes 3538944 | tf_op jit(solution)/shard_map/reduce_scatter | solution.py:480
  2955.2 749.3 %reduce-scatter.57.cloned.1.call-start = ((), (), s32[]{:S(2)}) async-start(), calls=%async_computation.53 | async-start | bytes 3538944 | tf_op jit(solution)/shard_map/reduce_scatter | solution.py:472
  2962.5 872.6 %all-reduce.2.cloned.1.call-start = ((), (), s32[]{:S(2)}) async-start(), calls=%async_computation.52 | async-start | bytes 589824 | tf_op jit(solution)/shard_map/psum | solution.py:491
  (193 other events, 10564.5 us)
Sparse Core Ops, SparseCore 0:
  10.9 46.9 all-gather.58
  395.1 42.9 all-gather.60
  473.1 34.6 reduce-scatter.34
  510.5 49.2 all-gather.62
  588.6 51.0 all-gather.64
  683.7 44.2 all-gather.66
  1179.1 42.5 all-gather.68
  1256.4 34.6 reduce-scatter.40
  1293.9 49.2 all-gather.70
  1372.1 51.0 all-gather.72
  1508.2 34.6 reduce-scatter.44
  1586.4 34.6 reduce-scatter.46
  1707.7 34.6 reduce-scatter.48
  1789.1 34.6 reduce-scatter.50
  1863.8 34.6 reduce-scatter.52
  2480.1 63.3 reduce-scatter.86
  2547.0 87.3 reduce-scatter.82
  2638.5 88.2 reduce-scatter.80
  2730.4 87.8 reduce-scatter.78
  2822.2 87.6 reduce-scatter.76
  2913.2 63.5 reduce-scatter.74
  2980.6 62.8 reduce-scatter.72
  3046.7 62.3 reduce-scatter.66
  3112.9 62.3 reduce-scatter.64
  3178.8 66.5 reduce-scatter.70
  3249.0 66.7 reduce-scatter.68
  3319.6 60.8 reduce-scatter.84
  3384.3 62.8 reduce-scatter.62
  3450.4 62.8 reduce-scatter.60
  3553.0 74.4 reduce-scatter.58
  3631.0 73.5 reduce-scatter.56
  3710.4 124.6 all-reduce.1
  (17 shorter events, 460.8 us)
where the time goes:
time: 3850 us; the launch traced here: 3840 us
  waiting for transfers between devices  1590 us (41%)
  other arithmetic  988 us (26%)
  local copies, waits for them, and re-layouts  796 us (21%)
  blocking collectives  227 us (6%)
  matrix products  225 us (6%)
    scatter-add x2, other arithmetic, self_backward(): jax.ops.segment_sum(summed.T, index_table.reshape(-1), num_segments=table...  892 us
    gather x4, local copies, waits for them, and re-layouts, self_scores(): bias = table.astype(jnp.float32)[:, index_table]  604 us
    reduce_scatter x6, waiting for transfers between devices, input_grad_sum(): lax.psum_scatter(contract_last(matrix, weight).astype(jnp.bfloat16), 'mp'...  208 us
    reduce_scatter x6, waiting for transfers between devices, branch_sum(): lax.psum_scatter(jnp.dot(matrix, weight, preferred_element_type=jnp.float...  193 us
    all_gather x6, waiting for transfers between devices, gather_grads(): return lax.all_gather(sending, 'mp', axis=0, tiled=True)  128 us
    psum x1, waiting for transfers between devices, body(): lax.psum(selector[:, None, None] * mod_local[None], ('dp', 'mp'))  127 us
    all_gather x2, waiting for transfers between devices, fetch_weights(): lax.all_gather(masters[5][layer_index].astype(jnp.bfloat16), 'dp', axis=0...  95 us
    all_gather x2, waiting for transfers between devices, fetch_weights(): lax.all_gather(masters[6][layer_index].astype(jnp.bfloat16), 'dp', axis=1...  92.4 us
  transfers between devices with their start and end apart: 49, of which 37 were waited for; matrix products, arithmetic and copies ran while one was open for 45% of the time, Pallas kernels for 0%

commit v1 on v0

v1 whole, which is shorter than its diff:
```python
import functools

import jax
import jax.numpy as jnp
from jax import lax
from jax.experimental import pallas as pl
from jax.experimental.pallas import tpu as pltpu
from jax.sharding import PartitionSpec as P

D = 1024
HD = 64
FF = 4096
FRAMES = 5
LAYERS = 2
STEP = 10
LANES = 128

BETA_ONE = 0.9
BETA_TWO = 0.95
ADAM_EPS = 1e-08
DECAY_RATE = 0.1


def learning_rates():
    inverse_root = D ** (-0.5)
    return (
        1.5 * inverse_root,
        6.0 * inverse_root,
        1.5 * inverse_root,
        1.5 * inverse_root,
        4.2 * inverse_root,
        1.5 * inverse_root,
        1.5 * FF ** (-0.5),
        1.5,
        1.5,
    )


def layer_norm(tensor):
    center = tensor - jnp.mean(tensor, axis=-1, keepdims=True)
    inverse = lax.rsqrt(jnp.mean(center * center, axis=-1, keepdims=True) + 1e-06)
    return (center * inverse, inverse)


def norm_back(grad_norm, normed, inverse):
    return inverse * (
        grad_norm
        - jnp.mean(grad_norm, axis=-1, keepdims=True)
        - normed * jnp.mean(grad_norm * normed, axis=-1, keepdims=True)
    )


def modulate_back(grad_latent, grad_input, normed, inverse, scaling):
    grad_norm = grad_input * (1.0 + scaling)
    return (
        grad_latent + norm_back(grad_norm, normed, inverse),
        jnp.sum(grad_input, axis=0),
        jnp.sum(grad_input * normed, axis=0),
    )


VM=pltpu.CompilerParams(vmem_limit_bytes=56*1024*1024)

def bias_kernel(table_ref, index_ref, out_ref):
    heads, groups, _ = table_ref.shape
    rows, cols = index_ref.shape
    def step(i, carry):
        r0 = pl.multiple_of(i * 16, 16)
        for c in range(cols // LANES):
            parts = [[] for _ in range(heads)]
            for half in range(2):
                idx = index_ref[pl.ds(r0 + half * 8, 8), pl.ds(c * LANES, LANES)]
                lo = idx & (LANES - 1)
                hi = idx >> 7
                for h in range(heads):
                    acc = jnp.zeros((8, LANES), jnp.float32)
                    for g in range(groups):
                        row = jnp.broadcast_to(table_ref[h, pl.ds(g, 1), :], (8, LANES))
                        val = jnp.take_along_axis(row, lo, axis=1, mode="promise_in_bounds")
                        acc = jnp.where(hi == g, val, acc)
                    parts[h].append(acc)
            for h in range(heads):
                out_ref[h, pl.ds(r0, 16), pl.ds(c * LANES, LANES)] = jnp.concatenate(parts[h], 0).astype(jnp.bfloat16)
        return carry
    lax.fori_loop(0, rows // 16, step, 0)

def make_bias(table, index):
    heads, reach = table.shape
    n = index.shape[0]
    pad = -n % LANES
    index = jnp.pad(index, ((0, 0), (0, pad)))
    return pl.pallas_call(bias_kernel,
        out_shape=jax.ShapeDtypeStruct((heads, n, n + pad), jnp.bfloat16),
        compiler_params=VM)(table.astype(jnp.float32).reshape(heads, reach // LANES, LANES), index)

LOW=64
def bucket_kernel(sum_ref, index_ref, out_ref):
    heads, rows, cols = sum_ref.shape
    high = out_ref.shape[0] // heads
    out_ref[...] = jnp.zeros_like(out_ref)
    hi_iota = lax.broadcasted_iota(jnp.int32, (high, cols), 0)
    lo_iota = lax.broadcasted_iota(jnp.int32, (LOW, cols), 0)
    def step(i, acc):
        r0 = pl.multiple_of(i * 8, 8)
        idx8 = index_ref[pl.ds(r0, 8), :]
        s8 = [sum_ref[h, pl.ds(r0, 8), :] for h in range(heads)]
        for r in range(8):
            idx = idx8[r:r+1]
            hot_hi = hi_iota == (idx >> 6)
            hot_lo = jnp.where(lo_iota == (idx & (LOW-1)), 1.0, 0.0).astype(jnp.bfloat16)
            left = jnp.concatenate([jnp.where(hot_hi, s8[h][r:r+1], 0.0) for h in range(heads)], 0).astype(jnp.bfloat16)
            acc = acc + lax.dot_general(left, hot_lo, (((1,),(1,)),((),())), preferred_element_type=jnp.float32)
        return acc
    out_ref[...] = lax.fori_loop(0, rows // 8, step, jnp.zeros(out_ref.shape, jnp.float32))

def bucket_sum(summed, index, reach):
    heads = summed.shape[0]
    out = pl.pallas_call(bucket_kernel,
        out_shape=jax.ShapeDtypeStruct((heads * (reach // LOW), LOW), jnp.float32),
        compiler_params=VM)(summed, index)
    return out.reshape(heads, reach)
QUARTER=64
NT=(((1,),(1,)),((),()))
TN=(((0,),(0,)),((),()))
def dot(a,b,dims=(((1,),(0,)),((),()))):
    return lax.dot_general(a,b,dims,preferred_element_type=jnp.float32)

def row_start(position, part):
    share = part // FRAMES
    return pl.multiple_of((position ^ share) * (FRAMES * QUARTER) + (part % FRAMES) * QUARTER, QUARTER)

def load_windows(ref, position, kind, step, cols):
    if kind == 0:
        return [jnp.concatenate([ref[pl.ds(row_start(position, 4 * step + t), QUARTER), cols] for t in range(4)], 0)]
    both = [[], []]
    for f in range(FRAMES):
        for k in range(2):
            block = ref[pl.ds(row_start(position, 4 * f + 2 * step + k), QUARTER), cols].astype(jnp.float32)
            block = block.reshape(4, 2, 8, block.shape[-1])
            for c in range(2):
                both[c].append(block[:, c].reshape(32, block.shape[-1]))
    return [jnp.concatenate(b, 0).astype(jnp.bfloat16) for b in both]

def store_windows(ref, position, kind, step, cols, values):
    if kind == 0:
        for t in range(4):
            ref[pl.ds(row_start(position, 4 * step + t), QUARTER), cols] = values[0][t * QUARTER:(t + 1) * QUARTER].astype(ref.dtype)
        return
    for f in range(FRAMES):
        for k in range(2):
            at = (2 * f + k) * 32
            block = jnp.stack([v[at:at + 32].reshape(4, 8, v.shape[-1]) for v in values], axis=1)
            ref[pl.ds(row_start(position, 4 * f + 2 * step + k), QUARTER), cols] = block.reshape(QUARTER, block.shape[-1]).astype(ref.dtype)

def self_forward_kernel(kind, position_ref, qkv_ref, bias_ref, out_ref, probs_ref):
    step = pl.program_id(0)
    position = position_ref[0]
    width = out_ref.shape[1]
    heads = width // HD
    size = probs_ref.shape[2]
    q, k, v = [load_windows(qkv_ref, position, kind, step, pl.ds(j * width, width)) for j in range(3)]
    lane = lax.broadcasted_iota(jnp.int32, (size, width), 1) // HD
    results = []
    for w in range(len(q)):
        total = jnp.zeros((size, width), jnp.float32)
        scaled = q[w] * jnp.bfloat16(HD ** -0.5)
        for h in range(heads):
            s = dot(jnp.where(lane == h, scaled, jnp.bfloat16(0)), k[w], NT) + bias_ref[h, :, pl.ds(0, size)].astype(jnp.float32)
            s = s - jnp.max(s, axis=-1, keepdims=True)
            e = jnp.exp(s)
            p = (e * (1.0 / jnp.sum(e, axis=-1, keepdims=True))).astype(jnp.bfloat16)
            probs_ref[w, h] = p
            total = total + dot(p, jnp.where(lane == h, v[w], jnp.bfloat16(0)))
        results.append(total)
    store_windows(out_ref, position, kind, step, pl.ds(0, width), results)

def self_forward_call(kind, position, qkv, bias):
    rows, width = qkv.shape
    width //= 3
    heads = width // HD
    size = 256 if kind == 0 else 320
    per = 1 if kind == 0 else 2
    steps = rows // size // per
    return pl.pallas_call(
        functools.partial(self_forward_kernel, kind),
        out_shape=(jax.ShapeDtypeStruct((rows, width), jnp.bfloat16),
                   jax.ShapeDtypeStruct((steps * per, heads, size, size), jnp.bfloat16)),
        grid_spec=pltpu.PrefetchScalarGridSpec(
            num_scalar_prefetch=1, grid=(steps,),
            in_specs=[pl.BlockSpec(qkv.shape, lambda i, p: (0, 0)),
                      pl.BlockSpec(bias.shape, lambda i, p: (0, 0, 0))],
            out_specs=[pl.BlockSpec((rows, width), lambda i, p: (0, 0)),
                       pl.BlockSpec((per, heads, size, size), lambda i, p: (i, 0, 0, 0))]),
        compiler_params=VM,
        name="self_forward",
    )(position, qkv, bias)

def self_backward_kernel(kind, position_ref, qkv_ref, probs_ref, grad_ref, dqkv_ref, sum_ref):
    step = pl.program_id(0)
    position = position_ref[0]
    width = grad_ref.shape[1]
    heads = width // HD
    size = probs_ref.shape[2]
    q, k, v = [load_windows(qkv_ref, position, kind, step, pl.ds(j * width, width)) for j in range(3)]
    g = load_windows(grad_ref, position, kind, step, pl.ds(0, width))
    lane = lax.broadcasted_iota(jnp.int32, (size, width), 1) // HD
    zero = jnp.bfloat16(0)
    @pl.when(step == 0)
    def _():
        sum_ref[...] = jnp.zeros_like(sum_ref)
    outs = [[], [], []]
    for w in range(len(q)):
        dq = jnp.zeros((size, width), jnp.float32)
        dk = jnp.zeros((size, width), jnp.float32)
        dv = jnp.zeros((size, width), jnp.float32)
        scaled = q[w] * jnp.bfloat16(HD ** -0.5)
        kscaled = k[w] * jnp.bfloat16(HD ** -0.5)
        for h in range(heads):
            mine = lane == h
            gh = jnp.where(mine, g[w], zero)
            p16 = probs_ref[w, h]
            p = p16.astype(jnp.float32)
            dp = dot(gh, v[w], NT)
            ds = p * (dp - jnp.sum(p * dp, axis=-1, keepdims=True))
            ds16 = ds.astype(jnp.bfloat16)
            sum_ref[h] += ds16.astype(jnp.float32)
            dq = dq + dot(ds16, jnp.where(mine, kscaled, zero))
            dk = dk + dot(ds16, jnp.where(mine, scaled, zero), TN)
            dv = dv + dot(p16, gh, TN)
        outs[0].append(dq); outs[1].append(dk); outs[2].append(dv)
    for j in range(3):
        store_windows(dqkv_ref, position, kind, step, pl.ds(j * width, width), outs[j])

def self_backward_call(kind, position, qkv, probs, grad):
    rows, width = grad.shape
    heads = width // HD
    size = probs.shape[2]
    per = 1 if kind == 0 else 2
    steps = rows // size // per
    return pl.pallas_call(
        functools.partial(self_backward_kernel, kind),
        out_shape=(jax.ShapeDtypeStruct(qkv.shape, jnp.bfloat16),
                   jax.ShapeDtypeStruct((heads, size, size), jnp.float32)),
        grid_spec=pltpu.PrefetchScalarGridSpec(
            num_scalar_prefetch=1, grid=(steps,),
            in_specs=[pl.BlockSpec(qkv.shape, lambda i, p: (0, 0)),
                      pl.BlockSpec((per, heads, size, size), lambda i, p: (i, 0, 0, 0)),
                      pl.BlockSpec(grad.shape, lambda i, p: (0, 0))],
            out_specs=[pl.BlockSpec(qkv.shape, lambda i, p: (0, 0)),
                       pl.BlockSpec((heads, size, size), lambda i, p: (0, 0, 0))]),
        compiler_params=VM,
        name="self_backward",
    )(position, qkv, probs, grad)
PAD=128

def cross_forward_kernel(q_ref, k_ref, v_ref, bias_ref, out_ref, probs_ref):
    rows = q_ref.shape[0]
    first = lax.broadcasted_iota(jnp.int32, (rows, LANES), 1) < HD
    vfirst = lax.broadcasted_iota(jnp.int32, (PAD, LANES), 1) < HD
    zero = jnp.bfloat16(0)
    q = q_ref[...] * jnp.bfloat16(HD ** -0.5)
    total = jnp.zeros((rows, LANES), jnp.float32)
    for half in range(2):
        s = dot(jnp.where(first == (half == 0), q, zero), k_ref[...], NT) + bias_ref[...]
        s = s - jnp.max(s, axis=-1, keepdims=True)
        e = jnp.exp(s)
        p = (e * (1.0 / jnp.sum(e, axis=-1, keepdims=True))).astype(jnp.bfloat16)
        probs_ref[half] = p
        total = total + dot(p, jnp.where(vfirst == (half == 0), v_ref[...], zero))
    out_ref[...] = total.astype(jnp.bfloat16)

def cross_forward_call(q, k, v, bias):
    rows, width = q.shape
    pairs = width // LANES
    col = lambda i: (0, i)
    return pl.pallas_call(
        cross_forward_kernel, grid=(pairs,),
        in_specs=[pl.BlockSpec((rows, LANES), col), pl.BlockSpec((PAD, LANES), col), pl.BlockSpec((PAD, LANES), col),
                  pl.BlockSpec((1, PAD), lambda i: (0, 0))],
        out_specs=[pl.BlockSpec((rows, LANES), col), pl.BlockSpec((2, rows, PAD), lambda i: (i, 0, 0))],
        out_shape=[jax.ShapeDtypeStruct((rows, width), jnp.bfloat16), jax.ShapeDtypeStruct((2 * pairs, rows, PAD), jnp.bfloat16)],
        compiler_params=VM, name="cross_forward")(q, k, v, bias)

def cross_backward_kernel(q_ref, k_ref, v_ref, probs_ref, grad_ref, dq_ref, dk_ref, dv_ref):
    rows = q_ref.shape[0]
    first = lax.broadcasted_iota(jnp.int32, (rows, LANES), 1) < HD
    kfirst = lax.broadcasted_iota(jnp.int32, (PAD, LANES), 1) < HD
    zero = jnp.bfloat16(0)
    q = q_ref[...] * jnp.bfloat16(HD ** -0.5)
    k = k_ref[...] * jnp.bfloat16(HD ** -0.5)
    dq = jnp.zeros((rows, LANES), jnp.float32)
    dk = jnp.zeros((PAD, LANES), jnp.float32)
    dv = jnp.zeros((PAD, LANES), jnp.float32)
    for half in range(2):
        mine = first == (half == 0)
        g = jnp.where(mine, grad_ref[...], zero)
        p16 = probs_ref[half]
        p = p16.astype(jnp.float32)
        dp = dot(g, v_ref[...], NT)
        ds = (p * (dp - jnp.sum(p * dp, axis=-1, keepdims=True))).astype(jnp.bfloat16)
        dq = dq + dot(ds, jnp.where(kfirst == (half == 0), k, zero))
        dk = dk + dot(ds, jnp.where(mine, q, zero), TN)
        dv = dv + dot(p16, g, TN)
    dq_ref[...] = dq.astype(jnp.bfloat16)
    dk_ref[...] = dk
    dv_ref[...] = dv

def cross_backward_call(q, k, v, probs, grad):
    rows, width = q.shape
    pairs = width // LANES
    col = lambda i: (0, i)
    tok = pl.BlockSpec((rows, LANES), col); txt = pl.BlockSpec((PAD, LANES), col)
    return pl.pallas_call(
        cross_backward_kernel, grid=(pairs,),
        in_specs=[tok, txt, txt, pl.BlockSpec((2, rows, PAD), lambda i: (i, 0, 0)), tok],
        out_specs=[tok, txt, txt],
        out_shape=[jax.ShapeDtypeStruct((rows, width), jnp.bfloat16), jax.ShapeDtypeStruct((PAD, width), jnp.float32), jax.ShapeDtypeStruct((PAD, width), jnp.float32)],
        compiler_params=VM, name="cross_backward")(q, k, v, probs, grad)

def gelu_parts(u):
    inner = 0.7978845608028654 * (u + 0.044715 * u * u * u)
    th = jnp.tanh(inner)
    slope = 0.5 * (1.0 + th) + 0.5 * u * (1.0 - th * th) * (0.7978845608028654 * (1.0 + 3.0 * 0.044715 * u * u))
    return 0.5 * u * (1.0 + th), slope


def feed_forward_kernel(a_ref, b_ref, up_ref, down_ref, hidden_ref, active_ref, pa_ref, pb_ref, acc_ref):
    step = pl.program_id(0)
    rows = a_ref.shape[0]
    for at, ref in ((0, a_ref), (rows, b_ref)):
        u = dot(ref[...], up_ref[...])
        hidden_ref[pl.ds(at, rows), :] = u.astype(jnp.bfloat16)
        active = jax.nn.gelu(u, approximate=True).astype(jnp.bfloat16)
        active_ref[pl.ds(at, rows), :] = active
        part = dot(active, down_ref[...], NT)

        @pl.when(step == 0)
        def _():
            acc_ref[pl.ds(at, rows), :] = part

        @pl.when(step > 0)
        def _():
            acc_ref[pl.ds(at, rows), :] += part

    @pl.when(step == pl.num_programs(0) - 1)
    def _():
        pa_ref[...] = acc_ref[pl.ds(0, rows), :].astype(jnp.bfloat16)
        pb_ref[...] = acc_ref[pl.ds(rows, rows), :].astype(jnp.bfloat16)


FF_TILE = 256


def feed_forward_call(a, b, weights):
    rows, width = a.shape
    hidden = weights.shape[1] // 2
    tiles = hidden // FF_TILE
    whole = pl.BlockSpec((rows, width), lambda i: (0, 0))
    strip = pl.BlockSpec((2 * rows, FF_TILE), lambda i: (0, i))
    return pl.pallas_call(
        feed_forward_kernel,
        grid=(tiles,),
        in_specs=[
            whole,
            whole,
            pl.BlockSpec((width, FF_TILE), lambda i: (0, i)),
            pl.BlockSpec((width, FF_TILE), lambda i: (0, tiles + i)),
        ],
        out_specs=[strip, strip, whole, whole],
        out_shape=[
            jax.ShapeDtypeStruct((2 * rows, hidden), jnp.bfloat16),
            jax.ShapeDtypeStruct((2 * rows, hidden), jnp.bfloat16),
            jax.ShapeDtypeStruct((rows, width), jnp.bfloat16),
            jax.ShapeDtypeStruct((rows, width), jnp.bfloat16),
        ],
        scratch_shapes=[pltpu.VMEM((2 * rows, width), jnp.float32)],
        compiler_params=VM,
        cost_estimate=pl.CostEstimate(
            flops=8 * rows * width * hidden, bytes_accessed=4 * width * hidden + 12 * rows * width, transcendentals=2 * rows * hidden
        ),
        name="feed_forward",
    )(a, b, weights, weights)


def feed_backward_kernel(a_ref, b_ref, hidden_ref, up_ref, down_ref, grad_ref, pa_ref, pb_ref, acc_ref):
    step = pl.program_id(0)
    rows = a_ref.shape[0]
    for at, ref in ((0, a_ref), (rows, b_ref)):
        slope = gelu_parts(hidden_ref[pl.ds(at, rows), :].astype(jnp.float32))[1]
        grad = (dot(ref[...], down_ref[...]) * slope).astype(jnp.bfloat16)
        grad_ref[pl.ds(at, rows), :] = grad
        part = dot(grad, up_ref[...], NT)

        @pl.when(step == 0)
        def _():
            acc_ref[pl.ds(at, rows), :] = part

        @pl.when(step > 0)
        def _():
            acc_ref[pl.ds(at, rows), :] += part

    @pl.when(step == pl.num_programs(0) - 1)
    def _():
        pa_ref[...] = acc_ref[pl.ds(0, rows), :].astype(jnp.bfloat16)
        pb_ref[...] = acc_ref[pl.ds(rows, rows), :].astype(jnp.bfloat16)


def feed_backward_call(a, b, hidden, weights):
    rows, width = a.shape
    units = weights.shape[1] // 2
    tiles = units // FF_TILE
    whole = pl.BlockSpec((rows, width), lambda i: (0, 0))
    strip = pl.BlockSpec((2 * rows, FF_TILE), lambda i: (0, i))
    return pl.pallas_call(
        feed_backward_kernel,
        grid=(tiles,),
        in_specs=[
            whole,
            whole,
            strip,
            pl.BlockSpec((width, FF_TILE), lambda i: (0, i)),
            pl.BlockSpec((width, FF_TILE), lambda i: (0, tiles + i)),
        ],
        out_specs=[strip, whole, whole],
        out_shape=[
            jax.ShapeDtypeStruct((2 * rows, units), jnp.bfloat16),
            jax.ShapeDtypeStruct((rows, width), jnp.bfloat16),
            jax.ShapeDtypeStruct((rows, width), jnp.bfloat16),
        ],
        scratch_shapes=[pltpu.VMEM((2 * rows, width), jnp.float32)],
        compiler_params=VM,
        cost_estimate=pl.CostEstimate(
            flops=8 * rows * width * units, bytes_accessed=4 * width * units + 10 * rows * width, transcendentals=2 * rows * units
        ),
        name="feed_backward",
    )(a, b, hidden, weights, weights)

def adam_update(master, first, second, grad, rate):
    first_new = BETA_ONE * first + (1.0 - BETA_ONE) * grad
    second_new = BETA_TWO * second + (1.0 - BETA_TWO) * grad * grad
    step_size = (
        first_new
        / (1.0 - BETA_ONE**STEP)
        / (jnp.sqrt(second_new / (1.0 - BETA_TWO**STEP)) + ADAM_EPS)
    )
    master_new = master - rate * (step_size + DECAY_RATE * master)
    return (master_new, first_new, second_new, master_new.astype(jnp.bfloat16))


def exchange(value, axis, bit, size):
    return lax.ppermute(value, axis, [(i, i ^ bit) for i in range(size)])


def share_rows(own):
    near = exchange(own, "mp", 1, 4)
    far = exchange(own, "mp", 2, 4)
    return (own, near, far, exchange(far, "mp", 1, 4))


def collect_parts(parts):
    beside = exchange(parts[3], "mp", 1, 4)
    crossing = (parts[2].astype(jnp.float32) + beside.astype(jnp.float32)).astype(jnp.bfloat16)
    far = exchange(crossing, "mp", 2, 4)
    near = exchange(parts[1], "mp", 1, 4)
    return parts[0].astype(jnp.float32) + near.astype(jnp.float32) + far.astype(jnp.float32)


def bits_of(size):
    return [1 << n for n in range(size.bit_length() - 1)]


def halve_rows(total, size):
    me = lax.axis_index("dp")
    width = total.shape[1]
    rows = total.shape[0] // size
    blocks = total.reshape(size, rows, width)
    for n, bit in enumerate(bits_of(size)):
        pairs = blocks.reshape(blocks.shape[0] // 2, 2, rows, width)
        mine = (me >> n) & 1
        keep = lax.dynamic_index_in_dim(pairs, mine, 1, keepdims=False)
        send = lax.dynamic_index_in_dim(pairs, 1 - mine, 1, keepdims=False)
        got = exchange(send, "dp", bit, size)
        total = keep.astype(jnp.float32) + got.astype(jnp.float32)
        blocks = total.astype(jnp.bfloat16)
    return total.reshape(rows, width)


def gather_small(own, size):
    me = lax.axis_index("dp")
    slots = own[None]
    for n, bit in enumerate(bits_of(size)):
        got = exchange(slots, "dp", bit, size)
        slots = jnp.where(((me >> n) & 1) == 0, jnp.concatenate([slots, got]), jnp.concatenate([got, slots]))
    return slots


def modulate(latent, scale, shift):
    normed, inverse = layer_norm(latent)
    return (normed * (1.0 + scale) + shift).astype(jnp.bfloat16)


def split_heads(columns, parts):
    rows = columns.shape[0]
    return columns.reshape(rows, -1, parts, HD).swapaxes(1, 2).reshape(rows, -1)


def join_heads(columns, parts):
    rows = columns.shape[0]
    return columns.reshape(rows, parts, -1, HD).swapaxes(1, 2).reshape(rows, -1)


def narrow(value):
    return value.astype(jnp.bfloat16)


def gather_group(shards):
    return lax.all_gather(jnp.concatenate(shards, axis=1), "dp", axis=0, tiled=True)


def mm(a, b, dims=(((1,), (0,)), ((), ()))):
    return lax.dot_general(a, b, dims, preferred_element_type=jnp.float32)


def body(*args):
    (latents, cotangent, text_embed, text_mask, band_ids, rel_index_s, rel_index_t, modulation) = args[:8]
    masters, firsts, seconds = args[8:17], args[17:26], args[26:35]
    groups = lax.axis_size("dp")
    rates = learning_rates()
    position = lax.axis_index("mp").astype(jnp.int32)[None]
    clip_index = lax.axis_index("dp") // 2
    text_rows = lax.dynamic_index_in_dim(text_embed, clip_index, 0, keepdims=False)
    texts = text_rows.shape[0]
    text_rows = jnp.pad(text_rows, ((0, PAD - texts), (0, 0)))
    mask_row = lax.dynamic_index_in_dim(text_mask, clip_index, 0, keepdims=False)
    column = jnp.arange(PAD, dtype=jnp.int32)
    valid = jnp.maximum(jnp.pad(mask_row, (0, PAD - texts)), (column == 0).astype(jnp.int32)).astype(jnp.float32)
    valid_bias = jnp.where(column < texts, (valid - 1.0) * 1000000000.0, -1e30)[None]
    band_now = lax.dynamic_index_in_dim(band_ids, clip_index, 0, keepdims=False)
    selector = (jnp.arange(modulation.shape[0], dtype=jnp.int32) == band_now).astype(jnp.float32)
    mod_rows = lax.dynamic_index_in_dim(modulation, band_now, 0, keepdims=False)

    tables = gather_small(jnp.concatenate([narrow(masters[7]), narrow(masters[8])], axis=1), groups)
    tables = tables.swapaxes(0, 1)
    cut = masters[7].shape[1]
    table_s = tables[:, :, :cut].reshape(tables.shape[0], -1)
    table_t = tables[:, :, cut:].reshape(tables.shape[0], -1)
    biases = (make_bias(table_s, rel_index_s), make_bias(table_t, rel_index_t))
    index_tables = (rel_index_s, rel_index_t)
    reaches = (table_s.shape[1], table_t.shape[1])

    weights = []
    for layer in range(LAYERS):
        self_group = gather_group([split_heads(narrow(masters[0][layer]), 3), narrow(masters[1][layer]).T])
        cross_group = gather_group(
            [narrow(masters[2][layer]), narrow(masters[4][layer]).T, split_heads(narrow(masters[3][layer]), 2)]
        )
        feed_group = gather_group([narrow(masters[5][layer]), narrow(masters[6][layer]).T])
        weights.append((self_group, cross_group, feed_group))

    latent = latents
    saved = []
    wide = masters[1].shape[1]
    for layer in range(LAYERS):
        self_w, cross_w, feed_w = weights[layer]
        base = 9 * layer
        record = {"in": latent}
        rows = share_rows(modulate(latent, mod_rows[base + 1], mod_rows[base]))
        qkv = jnp.concatenate([narrow(mm(item, self_w[:, : 3 * wide])) for item in rows], axis=0)
        mixed, probs = self_forward_call(layer, position, qkv, biases[layer])
        w_out = self_w[:, 3 * wide :]
        own = latents.shape[0]
        parts = [narrow(mm(mixed[k * own : (k + 1) * own], w_out, NT)) for k in range(4)]
        branch = collect_parts(parts)
        record["self"] = (rows, qkv, probs, mixed, branch)
        latent = latent + mod_rows[base + 2] * branch
        record["mid"] = latent
        normed = modulate(latent, mod_rows[base + 4], mod_rows[base + 3])
        keyval = share_rows(narrow(mm(text_rows, cross_w[:, 2 * wide :])))
        keys = jnp.concatenate([item[:, :wide] for item in keyval], axis=1)
        values = jnp.concatenate([item[:, wide:] for item in keyval], axis=1)
        cross_all = share_rows(cross_w[:, : 2 * wide])
        w_cq = jnp.concatenate([item[:, :wide] for item in cross_all], axis=1)
        w_cout = jnp.concatenate([item[:, wide:] for item in cross_all], axis=1)
        queries = narrow(mm(normed, w_cq))
        mixed, probs = cross_forward_call(queries, keys, values, valid_bias)
        branch = mm(mixed, w_cout, NT)
        record["cross"] = (normed, queries, keys, values, probs, mixed, branch, w_cq, w_cout)
        latent = latent + mod_rows[base + 5] * branch
        record["late"] = latent
        rows = share_rows(modulate(latent, mod_rows[base + 7], mod_rows[base + 6]))
        hidden_near, active_near, p0, p1 = feed_forward_call(rows[0], rows[1], feed_w)
        hidden_far, active_far, p2, p3 = feed_forward_call(rows[2], rows[3], feed_w)
        branch = collect_parts([p0, p1, p2, p3])
        record["feed"] = (rows, (hidden_near, hidden_far), (active_near, active_far), branch)
        latent = latent + mod_rows[base + 8] * branch
        saved.append(record)

    grad_latent = cotangent
    mod_grads = [None, None]
    reduced = [None, None]
    for layer in reversed(range(LAYERS)):
        self_w, cross_w, feed_w = weights[layer]
        base = 9 * layer
        record = saved[layer]
        rows, hiddens, actives, branch = record["feed"]
        gate_m = jnp.sum(grad_latent * branch, axis=0)
        grads = share_rows(narrow(mod_rows[base + 8] * grad_latent))
        dh_near, p0, p1 = feed_backward_call(grads[0], grads[1], hiddens[0], feed_w)
        dh_far, p2, p3 = feed_backward_call(grads[2], grads[3], hiddens[1], feed_w)
        grad_input = collect_parts([p0, p1, p2, p3])
        grad_hidden = jnp.concatenate([dh_near, dh_far], axis=0)
        active = jnp.concatenate(actives, axis=0)
        all_rows = jnp.concatenate(rows, axis=0)
        all_grads = jnp.concatenate(grads, axis=0)
        feed_g = jnp.concatenate([narrow(mm(all_rows, grad_hidden, TN)), narrow(mm(all_grads, active, TN))], axis=1)
        feed_sum = halve_rows(feed_g, groups)
        normed, inverse = layer_norm(record["late"])
        grad_latent, shift_m, scale_m = modulate_back(grad_latent, grad_input, normed, inverse, mod_rows[base + 7])

        hidden, queries, keys, values, probs, mixed, branch, w_cq, w_cout = record["cross"]
        gate_c = jnp.sum(grad_latent * branch, axis=0)
        grad_rows = narrow(mod_rows[base + 5] * grad_latent)
        grad_mixed = narrow(mm(grad_rows, w_cout))
        grad_query, grad_key, grad_value = cross_backward_call(queries, keys, values, probs, grad_mixed)
        grad_input = mm(grad_query, w_cq, NT)
        grad_cq = narrow(mm(hidden, grad_query, TN))
        grad_cout = narrow(mm(grad_rows, mixed, TN))
        cross_parts = [
            jnp.concatenate([grad_cq[:, k * wide : (k + 1) * wide], grad_cout[:, k * wide : (k + 1) * wide]], axis=1) for k in range(4)
        ]
        cross_g = collect_parts(cross_parts)
        kv_parts = [
            narrow(jnp.concatenate([grad_key[:, k * wide : (k + 1) * wide], grad_value[:, k * wide : (k + 1) * wide]], axis=1))
            for k in range(4)
        ]
        grad_kv = narrow(collect_parts(kv_parts))
        cross_g = jnp.concatenate([narrow(cross_g), narrow(mm(text_rows, grad_kv, TN))], axis=1)
        cross_sum = halve_rows(cross_g, groups)
        normed, inverse = layer_norm(record["mid"])
        grad_latent, shift_c, scale_c = modulate_back(grad_latent, grad_input, normed, inverse, mod_rows[base + 4])

        rows, qkv, probs, mixed, branch = record["self"]
        gate_a = jnp.sum(grad_latent * branch, axis=0)
        grads = share_rows(narrow(mod_rows[base + 2] * grad_latent))
        w_out = self_w[:, 3 * wide :]
        grad_mixed = jnp.concatenate([narrow(mm(item, w_out)) for item in grads], axis=0)
        grad_qkv, summed = self_backward_call(layer, position, qkv, probs, grad_mixed)
        parts = [narrow(mm(grad_qkv[k * own : (k + 1) * own], self_w[:, : 3 * wide], NT)) for k in range(4)]
        grad_input = collect_parts(parts)
        all_rows = jnp.concatenate(rows, axis=0)
        all_grads = jnp.concatenate(grads, axis=0)
        self_g = jnp.concatenate([narrow(mm(all_rows, grad_qkv, TN)), narrow(mm(all_grads, mixed, TN))], axis=1)
        self_sum = halve_rows(self_g, groups)
        table_g = bucket_sum(summed, index_tables[layer], reaches[layer])
        table_g = table_g.reshape(table_g.shape[0], groups, -1).swapaxes(0, 1).reshape(-1, reaches[layer] // groups)
        table_sum = halve_rows(narrow(table_g), groups)
        normed, inverse = layer_norm(record["in"])
        grad_latent, shift_a, scale_a = modulate_back(grad_latent, grad_input, normed, inverse, mod_rows[base + 1])
        mod_grads[layer] = [shift_a, scale_a, gate_a, shift_c, scale_c, gate_c, shift_m, scale_m, gate_m]
        reduced[layer] = (
            join_heads(self_sum[:, : 3 * wide], 3),
            self_sum[:, 3 * wide :].T,
            cross_sum[:, :wide],
            join_heads(cross_sum[:, 2 * wide :], 2),
            cross_sum[:, wide : 2 * wide].T,
            feed_sum[:, : masters[5].shape[2]],
            feed_sum[:, masters[5].shape[2] :].T,
            table_sum,
        )
    mod_local = jnp.stack(mod_grads[0] + mod_grads[1], axis=0)
    for bit in (1, 2):
        mod_local = mod_local + exchange(mod_local, "mp", bit, 4)
    grad_modulation = selector[:, None, None] * mod_local[None]
    for bit in bits_of(groups):
        grad_modulation = grad_modulation + exchange(grad_modulation, "dp", bit, groups)
    results = [latent, grad_latent, grad_modulation]
    for item in range(9):
        if item < 7:
            grad = jnp.stack([reduced[0][item], reduced[1][item]], axis=0)
        else:
            grad = reduced[item - 7][7]
        results.extend(adam_update(masters[item], firsts[item], seconds[item], grad, rates[item]))
    return tuple(results)


def solution(mesh):
    in_specs = (
        P(("dp", "mp"), None),
        P(("dp", "mp"), None),
        P(),
        P(),
        P(),
        P(),
        P(),
        P(),
        P(None, "dp", "mp"),
        P(None, "mp", "dp"),
        P(None, "dp", "mp"),
        P(None, "dp", "mp"),
        P(None, "mp", "dp"),
        P(None, "dp", "mp"),
        P(None, "mp", "dp"),
        P("mp", "dp"),
        P("mp", "dp"),
        P(None, "dp", "mp"),
        P(None, "mp", "dp"),
        P(None, "dp", "mp"),
        P(None, "dp", "mp"),
        P(None, "mp", "dp"),
        P(None, "dp", "mp"),
        P(None, "mp", "dp"),
        P("mp", "dp"),
        P("mp", "dp"),
        P(None, "dp", "mp"),
        P(None, "mp", "dp"),
        P(None, "dp", "mp"),
        P(None, "dp", "mp"),
        P(None, "mp", "dp"),
        P(None, "dp", "mp"),
        P(None, "mp", "dp"),
        P("mp", "dp"),
        P("mp", "dp"),
    )
    out_specs = (
        P(("dp", "mp"), None),
        P(("dp", "mp"), None),
        P(),
        P(None, "dp", "mp"),
        P(None, "dp", "mp"),
        P(None, "dp", "mp"),
        P(None, "dp", "mp"),
        P(None, "mp", "dp"),
        P(None, "mp", "dp"),
        P(None, "mp", "dp"),
        P(None, "mp", "dp"),
        P(None, "dp", "mp"),
        P(None, "dp", "mp"),
        P(None, "dp", "mp"),
        P(None, "dp", "mp"),
        P(None, "dp", "mp"),
        P(None, "dp", "mp"),
        P(None, "dp", "mp"),
        P(None, "dp", "mp"),
        P(None, "mp", "dp"),
        P(None, "mp", "dp"),
        P(None, "mp", "dp"),
        P(None, "mp", "dp"),
        P(None, "dp", "mp"),
        P(None, "dp", "mp"),
        P(None, "dp", "mp"),
        P(None, "dp", "mp"),
        P(None, "mp", "dp"),
        P(None, "mp", "dp"),
        P(None, "mp", "dp"),
        P(None, "mp", "dp"),
        P("mp", "dp"),
        P("mp", "dp"),
        P("mp", "dp"),
        P("mp", "dp"),
        P("mp", "dp"),
        P("mp", "dp"),
        P("mp", "dp"),
        P("mp", "dp"),
    )
    return jax.shard_map(body, mesh=mesh, in_specs=in_specs, out_specs=out_specs, check_vma=False)
```

time: 3850 us -> 1050 us (0.27)
  waiting for transfers between devices: 1590 us -> 263 us
  other arithmetic: 988 us -> 113 us
  local copies, waits for them, and re-layouts: 796 us -> 264 us
  blocking collectives: 227 us -> 0 us
  Pallas kernels: 0 us -> 205 us
  matrix products: 225 us -> 104 us
  starting transfers between devices: 3.61 us -> 76 us
    reduce_scatter x26 -> x0, waiting for transfers between devices: 1020 us -> none  [the longest x6 208 us: input_grad_sum(): lax.psum_scatter(contract_last(matrix, weight).astype(jnp.bfloat16), 'mp'...]
    scatter-add x2 -> x0, other arithmetic: 892 us -> none  [self_backward(): jax.ops.segment_sum(summed.T, index_table.reshape(-1), num_segments=table...]
    gather x4 -> x0, local copies, waits for them, and re-layouts: 604 us -> none  [self_scores(): bias = table.astype(jnp.float32)[:, index_table]]
    all_gather x20 -> x6, waiting for transfers between devices: 375 us -> 90.7 us  [gather_group(): lax.all_gather(jnp.concatenate(shards, axis=1), 'dp', axis=0, tiled=True)]
    all_gather x8 -> x0, blocking collectives: 227 us -> none  [the longest x2 66.6 us: fetch_weights(): lax.all_gather(masters[2][layer_index].astype(jnp.bfloat16), 'dp', axis=0...]
    pallas_call x0 -> x20, Pallas kernels: none -> 205 us  [the longest x4 46.9 us: feed_backward_call(): pl.pallas_call(feed_backward_kernel, grid=(tiles,), in_specs=[whole, whol...]
    ppermute x0 -> x104, waiting for transfers between devices: none -> 172 us  [exchange(): return lax.ppermute(value, axis, [(i, i ^ bit) for i in range(size)])]
    psum x1 -> x0, waiting for transfers between devices: 127 us -> none  [body(): lax.psum(selector[:, None, None] * mod_local[None], ('dp', 'mp'))]
  transfers between devices with their start and end apart: 49 -> 110, of which waited for: 37 -> 30; matrix products, arithmetic and copies ran while one was open for 45% -> 44% of each run, Pallas kernels for 0% -> 20%
where the time goes in v1:
time: 1050 us; the launch traced here: 1040 us
  local copies, waits for them, and re-layouts  264 us (25%)
  waiting for transfers between devices  263 us (25%)
  Pallas kernels  205 us (20%)
  other arithmetic  113 us (11%)
  matrix products  104 us (10%)
  starting transfers between devices  76 us (7%)
  between operations  20.3 us (2%)
    ppermute x104, waiting for transfers between devices, exchange(): return lax.ppermute(value, axis, [(i, i ^ bit) for i in range(size)])  172 us
    unnamed x532, local copies, waits for them, and re-layouts  141 us
    dot_general x56, matrix products, mm(): return lax.dot_general(a, b, dims, preferred_element_type=jnp.float32)  104 us
    all_gather x6, waiting for transfers between devices, gather_group(): lax.all_gather(jnp.concatenate(shards, axis=1), 'dp', axis=0, tiled=True)  90.7 us
    ppermute x104, starting transfers between devices, exchange(): return lax.ppermute(value, axis, [(i, i ^ bit) for i in range(size)])  75.7 us
    dynamic_slice x7, local copies, waits for them, and re-layouts, halve_rows(): keep = lax.dynamic_index_in_dim(pairs, mine, 1, keepdims=False)  52.7 us
    pallas_call x4, Pallas kernels, feed_backward_call(): pl.pallas_call(feed_backward_kernel, grid=(tiles,), in_specs=[whole, whol...  46.9 us
    pallas_call x4, Pallas kernels, feed_forward_call(): pl.pallas_call(feed_forward_kernel, grid=(tiles,), in_specs=[whole, whole...  45.5 us
  transfers between devices with their start and end apart: 110, of which 30 were waited for; matrix products, arithmetic and copies ran while one was open for 44% of the time, Pallas kernels for 20%

profile of v1, /device:TPU:0, one launch (start us, length us, event | category | flops | bytes accessed | tf_op | source)
XLA Modules:
  0.0 1043.7 jit_solution(11065897710550515729)
XLA Ops:
  43.6 20.9 %all-gather.9.cloned.1.call-done = bf16[1024,1024]{0,1:T(8,128)(2,1)} async-done(((bf16[128,1024]{0,1:T(8,128)(2,1)}), bf16[1024,1024]{0,1:T(8,128)(2,1)}) %all-gather.9.cloned.1.call-update) | async-done | bytes 2097168 | tf_op jit(solution)/shard_map/all_gather | solution.py:517
  70.1 46.0 %all-gather.7.cloned.1.call-done = bf16[1024,1024]{0,1:T(8,128)(2,1)} async-done(((bf16[128,1024]{0,1:T(8,128)(2,1)}), bf16[1024,1024]{0,1:T(8,128)(2,1)}) %all-gather.7.cloned.1.call-update) | async-done | bytes 2097168 | tf_op jit(solution)/shard_map/all_gather | solution.py:517
  145.1 11.2 %collective-permute-done.8 = bf16[320,1024]{1,0:T(8,128)(2,1)S(1)} collective-permute-done((bf16[320,1024]{1,0:T(8,128)(2,1)S(1)}, bf16[320,1024]{1,0:T(8,128)(2,1)S(1)}, u32[]{:S(2)}, u32[]{:S(2)}) %collective-permute-start.8) | collective-permute-done | bytes 655392 | tf_op jit(solution)/shard_map/ppermute | solution.py:451
  173.3 14.5 %collective-permute-done.17.a_ref = bf16[320,1024]{1,0:T(8,128)(2,1)S(1)} collective-permute-done((bf16[320,1024]{1,0:T(8,128)(2,1)S(1)}, bf16[320,1024]{1,0:T(8,128)(2,1)S(1)}, u32[]{:S(2)}, u32[]{:S(2)}) %collective-permute-start.17) | collective-permute-done | bytes 655392 | tf_op jit(solution)/shard_map/ppermute | solution.py:451
  190.4 11.2 %feed_forward.5 = (bf16[640,1024]{1,0:T(8,128)(2,1)}, bf16[640,1024]{1,0:T(8,128)(2,1)}, bf16[320,1024]{1,0:T(8,128)(2,1)}, bf16[320,1024]{1,0:T(8,128)(2,1)}) custom-call(bf16[320,1024]{1,0:T(8,128)(2,1)} %copy-done.224, bf16[320,1024]{1,0:T(8,128)(2,1)} %collective-permute-done.18.b_ref, bf16[1024,2048]{1,0:T(8,128)(2,1)} %all-gather.11.cloned.1.call-done.up_ref.down_ref, ...), custom_call_target="tpu_custom_call" | custom-call | flops 2684354560 | bytes 8126464 | tf_op jit(solution)/shard_map/feed_forward/pallas_call | solution.py:360
  201.8 11.4 %feed_forward.4 = (bf16[640,1024]{1,0:T(8,128)(2,1)}, bf16[640,1024]{1,0:T(8,128)(2,1)}, bf16[320,1024]{1,0:T(8,128)(2,1)}, bf16[320,1024]{1,0:T(8,128)(2,1)}) custom-call(bf16[320,1024]{1,0:T(8,128)(2,1)} %copy-done.110, bf16[320,1024]{1,0:T(8,128)(2,1)} %collective-permute-done.15.b_ref, bf16[1024,2048]{1,0:T(8,128)(2,1)} %all-gather.11.cloned.1.call-done.up_ref.down_ref, ...), custom_call_target="tpu_custom_call" | custom-call | flops 2684354560 | bytes 8126464 | tf_op jit(solution)/shard_map/feed_forward/pallas_call | solution.py:360
  226.5 15.8 %all-gather.15.cloned.1.call-done = bf16[1024,1024]{0,1:T(8,128)(2,1)} async-done(((bf16[128,1024]{0,1:T(8,128)(2,1)}), bf16[1024,1024]{0,1:T(8,128)(2,1)}) %all-gather.15.cloned.1.call-update) | async-done | bytes 2097168 | tf_op jit(solution)/shard_map/all_gather | solution.py:517
  254.4 19.4 %collective-permute-done.31 = bf16[128,512]{1,0:T(8,128)(2,1)S(1)} collective-permute-done((bf16[128,512]{1,0:T(8,128)(2,1)S(1)}, bf16[128,512]{1,0:T(8,128)(2,1)S(1)}, u32[]{:S(2)}, u32[]{:S(2)}) %collective-permute-start.31) | collective-permute-done | bytes 131104 | tf_op jit(solution)/shard_map/ppermute | solution.py:451
  273.8 12.4 %collective-permute-done.22 = bf16[320,1024]{1,0:T(8,128)(2,1)} collective-permute-done((bf16[320,1024]{1,0:T(8,128)(2,1)S(1)}, bf16[320,1024]{1,0:T(8,128)(2,1)}, u32[]{:S(2)}, u32[]{:S(2)}) %collective-permute-start.22) | collective-permute-done | bytes 655392 | tf_op jit(solution)/shard_map/ppermute | solution.py:451
  323.3 9.9 collective-permute-done.26
  352.6 14.5 %collective-permute-done.35.a_ref = bf16[320,1024]{1,0:T(8,128)(2,1)} collective-permute-done((bf16[320,1024]{1,0:T(8,128)(2,1)}, bf16[320,1024]{1,0:T(8,128)(2,1)}, u32[]{:S(2)}, u32[]{:S(2)}) %collective-permute-start.35) | collective-permute-done | bytes 655392 | tf_op jit(solution)/shard_map/ppermute | solution.py:451
  388.5 11.3 %feed_forward.6 = (bf16[640,1024]{1,0:T(8,128)(2,1)}, bf16[640,1024]{1,0:T(8,128)(2,1)}, bf16[320,1024]{1,0:T(8,128)(2,1)}, bf16[320,1024]{1,0:T(8,128)(2,1)}) custom-call(bf16[320,1024]{1,0:T(8,128)(2,1)} %add_convert_fusion.9.a_ref, bf16[320,1024]{1,0:T(8,128)(2,1)} %collective-permute-done.33.b_ref, ...), custom_call_target="tpu_custom_call" | custom-call | flops 2684354560 | bytes 8126464 | tf_op jit(solution)/shard_map/feed_forward/pallas_call | solution.py:360
  399.9 11.6 %feed_backward.4 = (bf16[640,1024]{1,0:T(8,128)(2,1)}, bf16[320,1024]{1,0:T(8,128)(2,1)}, bf16[320,1024]{1,0:T(8,128)(2,1)}) custom-call(bf16[320,1024]{1,0:T(8,128)(2,1)} %multiply_convert_fusion.5.a_ref, bf16[320,1024]{1,0:T(8,128)(2,1)} %collective-permute-done.39.b_ref, bf16[640,1024]{1,0:T(8,128)(2,1)} %get-tuple-element.97.hidden_ref, ...), custom_call_target="tpu_custom_call" | custom-call | flops 2684354560 | bytes 7471104 | tf_op jit(solution)/shard_map/feed_backward/pallas_call | solution.py:414
  412.0 11.6 %feed_forward.7 = (bf16[640,1024]{1,0:T(8,128)(2,1)}, bf16[640,1024]{1,0:T(8,128)(2,1)}, bf16[320,1024]{1,0:T(8,128)(2,1)}, bf16[320,1024]{1,0:T(8,128)(2,1)}) custom-call(bf16[320,1024]{1,0:T(8,128)(2,1)} %collective-permute-done.35.a_ref, bf16[320,1024]{1,0:T(8,128)(2,1)} %collective-permute-done.36.b_ref, ...), custom_call_target="tpu_custom_call" | custom-call | flops 2684354560 | bytes 8126464 | tf_op jit(solution)/shard_map/feed_forward/pallas_call | solution.py:360
  423.7 11.8 %feed_backward.5 = (bf16[640,1024]{1,0:T(8,128)(2,1)}, bf16[320,1024]{1,0:T(8,128)(2,1)}, bf16[320,1024]{1,0:T(8,128)(2,1)}) custom-call(bf16[320,1024]{1,0:T(8,128)(2,1)} %collective-permute-done.41.a_ref, bf16[320,1024]{1,0:T(8,128)(2,1)} %collective-permute-done.42.b_ref, bf16[640,1024]{1,0:T(8,128)(2,1)} %get-tuple-element.100.hidden_ref, ...), custom_call_target="tpu_custom_call" | custom-call | flops 2684354560 | bytes 7471104 | tf_op jit(solution)/shard_map/feed_backward/pallas_call | solution.py:414
  459.5 11.3 %constant_dynamic-slice_fusion.31 = (bf16[4,1,128,2048]{2,1,0,3:T(2,128)(2,1)}, bf16[4,1,128,2048]{2,1,0,3:T(2,128)(2,1)}) fusion(bf16[4,2,128,2048]{2,1,0,3:T(2,128)(2,1)} %reshape_reshape.27, s32[]{:T(128)S(6)} %select_n.127, s32[]{:T(128)S(6)} %select_n.128), kind=kLoop, calls=%fused_computation.442 | loop fusion | bytes 8388616 | tf_op jit(solution)/shard_map/jit(dynamic_index_in_dim)/dynamic_slice | solution.py:480
  470.8 10.7 %copy.270 = bf16[4,1,128,2048]{3,2,0,1:T(8,128)(2,1)} copy(bf16[4,1,128,2048]{2,1,0,3:T(2,128)(2,1)} %get-tuple-element.333) | data formatting | bytes 4194304
  483.1 10.6 %copy.269 = bf16[4,1,128,2048]{3,2,0,1:T(8,128)(2,1)} copy(bf16[4,1,128,2048]{2,1,0,3:T(2,128)(2,1)} %get-tuple-element.332) | data formatting | bytes 4194304
  498.9 12.5 %collective-permute-done.38 = bf16[320,1024]{1,0:T(8,128)(2,1)S(1)} collective-permute-done((bf16[320,1024]{1,0:T(8,128)(2,1)S(1)}, bf16[320,1024]{1,0:T(8,128)(2,1)S(1)}, u32[]{:S(2)}, u32[]{:S(2)}) %collective-permute-start.38) | collective-permute-done | bytes 655392 | tf_op jit(solution)/shard_map/ppermute | solution.py:451
  559.0 13.7 %self_backward.2 = (bf16[1280,768]{1,0:T(8,128)(2,1)}, f32[4,320,320]{2,1,0:T(8,128)}) custom-call(s32[1]{0:T(128)} %bitcast.2.position_ref, bf16[1280,768]{1,0:T(8,128)(2,1)} %pad_maximum_fusion.11.qkv_ref, bf16[4,4,320,320]{3,2,1,0:T(8,128)(2,1)} %get-tuple-element.105.probs_ref, bf16[1280,256]{1,0:T(8,128)(2,1)} %pad_maximum_fusion.19.grad_ref), custom_call_target="tpu_custom_call" | custom-call | tf_op jit(solution)/shard_map/self_backward/pallas_call | solution.py:240
  586.9 17.1 %shard_map.637 = f32[128,64]{1,0:T(8,128)} custom-call(f32[4,320,320]{2,1,0:T(8,128)} %get-tuple-element.130.sum_ref, s32[320,320]{1,0:T(8,128)} %index_ref.5), custom_call_target="tpu_custom_call" | custom-call | tf_op jit(solution)/shard_map/pallas_call | solution.py:118
  605.7 8.8 constant_dynamic-slice_fusion.43
  651.0 8.6 constant_dynamic-slice_fusion.37
  712.9 11.6 %feed_backward.6 = (bf16[640,1024]{1,0:T(8,128)(2,1)}, bf16[320,1024]{1,0:T(8,128)(2,1)}, bf16[320,1024]{1,0:T(8,128)(2,1)}) custom-call(bf16[320,1024]{1,0:T(8,128)(2,1)} %multiply_convert_fusion.2.a_ref, bf16[320,1024]{1,0:T(8,128)(2,1)} %collective-permute-done.51.b_ref, bf16[640,1024]{1,0:T(8,128)(2,1)} %get-tuple-element.107.hidden_ref, ...), custom_call_target="tpu_custom_call" | custom-call | flops 2684354560 | bytes 7471104 | tf_op jit(solution)/shard_map/feed_backward/pallas_call | solution.py:414
  724.5 11.8 %feed_backward.7 = (bf16[640,1024]{1,0:T(8,128)(2,1)}, bf16[320,1024]{1,0:T(8,128)(2,1)}, bf16[320,1024]{1,0:T(8,128)(2,1)}) custom-call(bf16[320,1024]{1,0:T(8,128)(2,1)} %collective-permute-done.53.a_ref, bf16[320,1024]{1,0:T(8,128)(2,1)} %collective-permute-done.54.b_ref, bf16[640,1024]{1,0:T(8,128)(2,1)} %get-tuple-element.110.hidden_ref, ...), custom_call_target="tpu_custom_call" | custom-call | flops 2684354560 | bytes 7471104 | tf_op jit(solution)/shard_map/feed_backward/pallas_call | solution.py:414
  759.5 11.3 %constant_dynamic-slice_fusion.34 = (bf16[4,1,128,2048]{2,1,0,3:T(2,128)(2,1)}, bf16[4,1,128,2048]{2,1,0,3:T(2,128)(2,1)}) fusion(bf16[4,2,128,2048]{2,1,0,3:T(2,128)(2,1)} %reshape_reshape.26, s32[]{:T(128)S(6)} %select_n.127, s32[]{:T(128)S(6)} %select_n.128), kind=kLoop, calls=%fused_computation.445 | loop fusion | bytes 8388616 | tf_op jit(solution)/shard_map/jit(dynamic_index_in_dim)/dynamic_slice | solution.py:480
  770.8 10.6 %copy.268 = bf16[4,1,128,2048]{3,2,0,1:T(8,128)(2,1)} copy(bf16[4,1,128,2048]{2,1,0,3:T(2,128)(2,1)} %get-tuple-element.331) | data formatting | bytes 4194304
  782.5 11.1 %copy.267 = bf16[4,1,128,2048]{3,2,0,1:T(8,128)(2,1)} copy(bf16[4,1,128,2048]{2,1,0,3:T(2,128)(2,1)} %get-tuple-element.330) | data formatting | bytes 4194304
  822.9 8.9 collective-permute-done.79
  845.1 11.4 %self_backward.3 = (bf16[1280,768]{1,0:T(8,128)(2,1)}, f32[4,256,256]{2,1,0:T(8,128)}) custom-call(s32[1]{0:T(128)} %bitcast.2.position_ref, bf16[1280,768]{1,0:T(8,128)(2,1)} %pad_maximum_fusion.10.qkv_ref, bf16[5,4,256,256]{3,2,1,0:T(8,128)(2,1)} %get-tuple-element.115.probs_ref, bf16[1280,256]{1,0:T(8,128)(2,1)} %pad_maximum_fusion.20.grad_ref), custom_call_target="tpu_custom_call" | custom-call | tf_op jit(solution)/shard_map/self_backward/pallas_call | solution.py:240
  869.5 9.0 shard_map.636
  1007.9 12.2 %collective-permute-done.67 = f32[4,18,1024]{2,0,1:T(4,128)} collective-permute-done((f32[4,18,1024]{2,0,1:T(4,128)S(1)}, f32[4,18,1024]{2,0,1:T(4,128)}, u32[]{:S(2)}, u32[]{:S(2)}) %collective-permute-start.67) | collective-permute-done | bytes 294944 | tf_op jit(solution)/shard_map/ppermute | solution.py:451
  (1045 shorter events, 598.7 us)
Async XLA Ops:
  7.3 57.2 %all-gather.9.cloned.1.call-start = ((), (), s32[]{:S(2)}) async-start(), calls=%async_computation.1 | async-start | bytes 2359296 | tf_op jit(solution)/shard_map/all_gather | solution.py:517
  9.7 106.4 %all-gather.7.cloned.1.call-start = ((), (), s32[]{:S(2)}) async-start(), calls=%async_computation | async-start | bytes 2359296 | tf_op jit(solution)/shard_map/all_gather | solution.py:517
  11.4 179.0 %all-gather.11.cloned.1.call-start = ((), (), s32[]{:S(2)}) async-start(), calls=%async_computation.2 | async-start | bytes 4718592 | tf_op jit(solution)/shard_map/all_gather | solution.py:517
  16.4 226.0 %all-gather.15.cloned.1.call-start = ((), (), s32[]{:S(2)}) async-start(), calls=%async_computation.4 | async-start | bytes 2359296 | tf_op jit(solution)/shard_map/all_gather | solution.py:517
  17.2 276.6 %all-gather.13.cloned.1.call-start = ((), (), s32[]{:S(2)}) async-start(), calls=%async_computation.3 | async-start | bytes 2359296 | tf_op jit(solution)/shard_map/all_gather | solution.py:517
  26.1 96.2 %collective-permute-start = (bf16[320,1024]{1,0:T(8,128)(2,1)}, bf16[320,1024]{1,0:T(8,128)(2,1)}, u32[]{:S(2)}, u32[]{:S(2)}) collective-permute-start(bf16[320,1024]{1,0:T(8,128)(2,1)} %add_convert_fusion.17), channel_id=1, source_target_pairs={{0,1},{1,0},{2,3},{3,2},{4,5},{5,4},{6,7},{7,6},{8,9},{9,8},{10,11... | collective-permute-start | bytes 1966088 | tf_op jit(solution)/shard_map/ppermute | solution.py:451
  28.5 360.0 %all-gather.17.cloned.1.call-start = ((), (), s32[]{:S(2)}) async-start(), calls=%async_computation.5 | async-start | bytes 4718592 | tf_op jit(solution)/shard_map/all_gather | solution.py:517
  43.6 76.8 %collective-permute-start.2 = (bf16[320,1024]{1,0:T(8,128)(2,1)}, bf16[320,1024]{1,0:T(8,128)(2,1)}, u32[]{:S(2)}, u32[]{:S(2)}) collective-permute-start(bf16[320,1024]{1,0:T(8,128)(2,1)} %collective-permute-done.1), channel_id=1, source_target_pairs={{0,1},{1,0},{2,3},{3,2},{4,5},{5,4},{6,7},{7,6},{8,9},{9,8},{10,11... | collective-permute-start | bytes 1966088 | tf_op jit(solution)/shard_map/ppermute | solution.py:451
  66.9 75.1 %collective-permute-start.10 = (bf16[1024,512]{0,1:T(8,128)(2,1)}, bf16[1024,512]{0,1:T(8,128)(2,1)S(1)}, u32[]{:S(2)}, u32[]{:S(2)}) collective-permute-start(bf16[1024,512]{0,1:T(8,128)(2,1)} %slice.633), channel_id=1, source_target_pairs={{0,2},{1,3},{2,0},{3,1},{4,6},{5,7},{6,4},{7,5},{8,10},{9,11},{10,... | collective-permute-start | bytes 3145736 | tf_op jit(solution)/shard_map/ppermute | solution.py:451
  68.3 74.5 %collective-permute-start.9 = (bf16[1024,512]{0,1:T(8,128)(2,1)}, bf16[1024,512]{0,1:T(8,128)(2,1)}, u32[]{:S(2)}, u32[]{:S(2)}) collective-permute-start(bf16[1024,512]{0,1:T(8,128)(2,1)} %slice.633), channel_id=1, source_target_pairs={{0,1},{1,0},{2,3},{3,2},{4,5},{5,4},{6,7},{7,6},{8,9},{9,8},{10,11... | collective-permute-start | bytes 3145736 | tf_op jit(solution)/shard_map/ppermute | solution.py:451
  69.5 69.0 %collective-permute-start.13 = (bf16[128,512]{1,0:T(8,128)(2,1)}, bf16[128,512]{1,0:T(8,128)(2,1)S(1)}, u32[]{:S(2)}, u32[]{:S(2)}) collective-permute-start(bf16[128,512]{1,0:T(8,128)(2,1)} %convolution_convert_fusion.43), channel_id=1, source_target_pairs={{0,2},{1,3},{2,0},{3,1},{4,6},{5,7},{6,4},{7,5},{8,10},{9,11},{10,... | collective-permute-start | bytes 393224 | tf_op jit(solution)/shard_map/ppermute | solution.py:451
  244.7 70.5 %collective-permute-start.28 = (bf16[1024,512]{0,1:T(8,128)(2,1)}, bf16[1024,512]{0,1:T(8,128)(2,1)}, u32[]{:S(2)}, u32[]{:S(2)}) collective-permute-start(bf16[1024,512]{0,1:T(8,128)(2,1)} %slice.661), channel_id=1, source_target_pairs={{0,2},{1,3},{2,0},{3,1},{4,6},{5,7},{6,4},{7,5},{8,10},{9,11},{10,... | collective-permute-start | bytes 3145736 | tf_op jit(solution)/shard_map/ppermute | solution.py:451
  246.1 74.0 %collective-permute-start.27 = (bf16[1024,512]{0,1:T(8,128)(2,1)}, bf16[1024,512]{0,1:T(8,128)(2,1)}, u32[]{:S(2)}, u32[]{:S(2)}) collective-permute-start(bf16[1024,512]{0,1:T(8,128)(2,1)} %slice.661), channel_id=1, source_target_pairs={{0,1},{1,0},{2,3},{3,2},{4,5},{5,4},{6,7},{7,6},{8,9},{9,8},{10,11... | collective-permute-start | bytes 3145736 | tf_op jit(solution)/shard_map/ppermute | solution.py:451
  248.5 64.9 %collective-permute-start.30 = (bf16[128,512]{1,0:T(8,128)(2,1)S(1)}, bf16[128,512]{1,0:T(8,128)(2,1)}, u32[]{:S(2)}, u32[]{:S(2)}) collective-permute-start(bf16[128,512]{1,0:T(8,128)(2,1)S(1)} %convolution_convert_fusion.42), channel_id=1, source_target_pairs={{0,1},{1,0},{2,3},{3,2},{4,5},{5,4},{6,7},{7,6},{8,9},{9,8},{10,11... | collective-permute-start | bytes 393224 | tf_op jit(solution)/shard_map/ppermute | solution.py:451
  352.1 47.8 %collective-permute-start.39 = (bf16[320,1024]{1,0:T(8,128)(2,1)}, bf16[320,1024]{1,0:T(8,128)(2,1)}, u32[]{:S(2)}, u32[]{:S(2)}) collective-permute-start(bf16[320,1024]{1,0:T(8,128)(2,1)} %multiply_convert_fusion.5.a_ref), channel_id=1, source_target_pairs={{0,1},{1,0},{2,3},{3,2},{4,5},{5,4},{6,7},{7,6},{8,9},{9,8},{10,11... | collective-permute-start | bytes 1966088 | tf_op jit(solution)/shard_map/ppermute | solution.py:451
  399.8 99.1 %collective-permute-start.34 = (bf16[320,1024]{1,0:T(8,128)(2,1)}, bf16[320,1024]{1,0:T(8,128)(2,1)}, u32[]{:S(2)}, u32[]{:S(2)}) collective-permute-start(bf16[320,1024]{1,0:T(8,128)(2,1)} %get-tuple-element.94), channel_id=1, source_target_pairs={{0,1},{1,0},{2,3},{3,2},{4,5},{5,4},{6,7},{7,6},{8,9},{9,8},{10,11... | collective-permute-start | bytes 1966088 | tf_op jit(solution)/shard_map/ppermute | solution.py:451
  411.5 84.4 %collective-permute-start.40 = (bf16[320,1024]{1,0:T(8,128)(2,1)}, bf16[320,1024]{1,0:T(8,128)(2,1)}, u32[]{:S(2)}, u32[]{:S(2)}) collective-permute-start(bf16[320,1024]{1,0:T(8,128)(2,1)} %get-tuple-element.99), channel_id=1, source_target_pairs={{0,1},{1,0},{2,3},{3,2},{4,5},{5,4},{6,7},{7,6},{8,9},{9,8},{10,11... | collective-permute-start | bytes 1966088 | tf_op jit(solution)/shard_map/ppermute | solution.py:451
  423.6 70.0 %collective-permute-start.37 = (bf16[320,1024]{1,0:T(8,128)(2,1)}, bf16[320,1024]{1,0:T(8,128)(2,1)}, u32[]{:S(2)}, u32[]{:S(2)}) collective-permute-start(bf16[320,1024]{1,0:T(8,128)(2,1)} %get-tuple-element.96), channel_id=1, source_target_pairs={{0,1},{1,0},{2,3},{3,2},{4,5},{5,4},{6,7},{7,6},{8,9},{9,8},{10,11... | collective-permute-start | bytes 1966088 | tf_op jit(solution)/shard_map/ppermute | solution.py:451
  481.5 70.7 %collective-permute-start.95 = (bf16[4,128,2048]{2,1,0:T(8,128)(2,1)}, bf16[4,128,2048]{2,1,0:T(8,128)(2,1)}, u32[]{:S(2)}, u32[]{:S(2)}) collective-permute-start(bf16[4,128,2048]{2,1,0:T(8,128)(2,1)} %bitcast.326), channel_id=1, source_target_pairs={{0,4},{4,0},{8,12},{12,8},{16,20},{20,16},{24,28},{28,24},{1,5},{5... | collective-permute-start | bytes 6291464 | tf_op jit(solution)/shard_map/ppermute | solution.py:451
  549.0 92.1 %collective-permute-start.83 = (bf16[1024,512]{0,1:T(8,128)(2,1)}, bf16[1024,512]{0,1:T(8,128)(2,1)}, u32[]{:S(2)}, u32[]{:S(2)}) collective-permute-start(bf16[1024,512]{0,1:T(8,128)(2,1)} %pad_maximum_fusion.14), channel_id=1, source_target_pairs={{0,1},{1,0},{2,3},{3,2},{4,5},{5,4},{6,7},{7,6},{8,9},{9,8},{10,11... | collective-permute-start | bytes 3145736 | tf_op jit(solution)/shard_map/ppermute | solution.py:451
  555.8 77.2 %collective-permute-start.96 = (bf16[2,128,2048]{2,1,0:T(8,128)(2,1)}, bf16[2,128,2048]{2,1,0:T(8,128)(2,1)}, u32[]{:S(2)}, u32[]{:S(2)}) collective-permute-start(bf16[2,128,2048]{2,1,0:T(8,128)(2,1)} %dynamic-slice_bitcast_fusion), channel_id=1, source_target_pairs={{0,8},{4,12},{8,0},{12,4},{16,24},{20,28},{24,16},{28,20},{1,9},{5... | collective-permute-start | bytes 3145736 | tf_op jit(solution)/shard_map/ppermute | solution.py:451
  557.2 85.4 %collective-permute-start.85 = (bf16[1024,512]{0,1:T(8,128)(2,1)}, bf16[1024,512]{0,1:T(8,128)(2,1)}, u32[]{:S(2)}, u32[]{:S(2)}) collective-permute-start(bf16[1024,512]{0,1:T(8,128)(2,1)} %add_convert_fusion.1), channel_id=1, source_target_pairs={{0,2},{1,3},{2,0},{3,1},{4,6},{5,7},{6,4},{7,5},{8,10},{9,11},{10,... | collective-permute-start | bytes 3145736 | tf_op jit(solution)/shard_map/ppermute | solution.py:451
  575.5 61.0 %collective-permute-start.49 = (bf16[320,1024]{1,0:T(8,128)(2,1)}, bf16[320,1024]{1,0:T(8,128)(2,1)}, u32[]{:S(2)}, u32[]{:S(2)}) collective-permute-start(bf16[320,1024]{1,0:T(8,128)(2,1)} %convolution_convert_fusion.11), channel_id=1, source_target_pairs={{0,1},{1,0},{2,3},{3,2},{4,5},{5,4},{6,7},{7,6},{8,9},{9,8},{10,11... | collective-permute-start | bytes 1966088 | tf_op jit(solution)/shard_map/ppermute | solution.py:451
  724.5 69.9 %collective-permute-start.52 = (bf16[320,1024]{1,0:T(8,128)(2,1)}, bf16[320,1024]{1,0:T(8,128)(2,1)}, u32[]{:S(2)}, u32[]{:S(2)}) collective-permute-start(bf16[320,1024]{1,0:T(8,128)(2,1)} %get-tuple-element.109), channel_id=1, source_target_pairs={{0,1},{1,0},{2,3},{3,2},{4,5},{5,4},{6,7},{7,6},{8,9},{9,8},{10,11... | collective-permute-start | bytes 1966088 | tf_op jit(solution)/shard_map/ppermute | solution.py:451
  781.4 53.7 %collective-permute-start.92 = (bf16[4,128,2048]{2,1,0:T(8,128)(2,1)}, bf16[4,128,2048]{2,1,0:T(8,128)(2,1)}, u32[]{:S(2)}, u32[]{:S(2)}) collective-permute-start(bf16[4,128,2048]{2,1,0:T(8,128)(2,1)} %bitcast.327), channel_id=1, source_target_pairs={{0,4},{4,0},{8,12},{12,8},{16,20},{20,16},{24,28},{28,24},{1,5},{5... | collective-permute-start | bytes 6291464 | tf_op jit(solution)/shard_map/ppermute | solution.py:451
  831.8 80.9 %collective-permute-start.74 = (bf16[1024,512]{0,1:T(8,128)(2,1)}, bf16[1024,512]{0,1:T(8,128)(2,1)}, u32[]{:S(2)}, u32[]{:S(2)}) collective-permute-start(bf16[1024,512]{0,1:T(8,128)(2,1)} %pad_maximum_fusion.12), channel_id=1, source_target_pairs={{0,1},{1,0},{2,3},{3,2},{4,5},{5,4},{6,7},{7,6},{8,9},{9,8},{10,11... | collective-permute-start | bytes 3145736 | tf_op jit(solution)/shard_map/ppermute | solution.py:451
  838.6 65.0 %collective-permute-start.93 = (bf16[2,128,2048]{2,1,0:T(8,128)(2,1)}, bf16[2,128,2048]{2,1,0:T(8,128)(2,1)}, u32[]{:S(2)}, u32[]{:S(2)}) collective-permute-start(bf16[2,128,2048]{2,1,0:T(8,128)(2,1)} %dynamic-slice_bitcast_fusion.1), channel_id=1, source_target_pairs={{0,8},{4,12},{8,0},{12,4},{16,24},{20,28},{24,16},{28,20},{1,9},{5... | collective-permute-start | bytes 3145736 | tf_op jit(solution)/shard_map/ppermute | solution.py:451
  842.5 71.0 %collective-permute-start.76 = (bf16[1024,512]{0,1:T(8,128)(2,1)}, bf16[1024,512]{0,1:T(8,128)(2,1)}, u32[]{:S(2)}, u32[]{:S(2)}) collective-permute-start(bf16[1024,512]{0,1:T(8,128)(2,1)} %add_convert_fusion.3), channel_id=1, source_target_pairs={{0,2},{1,3},{2,0},{3,1},{4,6},{5,7},{6,4},{7,5},{8,10},{9,11},{10,... | collective-permute-start | bytes 3145736 | tf_op jit(solution)/shard_map/ppermute | solution.py:451
  859.2 47.8 %collective-permute-start.61 = (bf16[320,1024]{1,0:T(8,128)(2,1)}, bf16[320,1024]{1,0:T(8,128)(2,1)}, u32[]{:S(2)}, u32[]{:S(2)}) collective-permute-start(bf16[320,1024]{1,0:T(8,128)(2,1)} %convolution_convert_fusion.6), channel_id=1, source_target_pairs={{0,1},{1,0},{2,3},{3,2},{4,5},{5,4},{6,7},{7,6},{8,9},{9,8},{10,11... | collective-permute-start | bytes 1966088 | tf_op jit(solution)/shard_map/ppermute | solution.py:451
  902.9 54.1 %collective-permute-start.60 = (bf16[320,1024]{1,0:T(8,128)(2,1)}, bf16[320,1024]{1,0:T(8,128)(2,1)}, u32[]{:S(2)}, u32[]{:S(2)}) collective-permute-start(bf16[320,1024]{1,0:T(8,128)(2,1)} %convolution_convert_fusion.8), channel_id=1, source_target_pairs={{0,1},{1,0},{2,3},{3,2},{4,5},{5,4},{6,7},{7,6},{8,9},{9,8},{10,11... | collective-permute-start | bytes 1966088 | tf_op jit(solution)/shard_map/ppermute | solution.py:451
  903.6 49.4 %collective-permute-start.68 = (bf16[4,128,1024]{2,1,0:T(8,128)(2,1)}, bf16[4,128,1024]{2,1,0:T(8,128)(2,1)}, u32[]{:S(2)}, u32[]{:S(2)}) collective-permute-start(bf16[4,128,1024]{2,1,0:T(8,128)(2,1)} %bitcast.337), channel_id=1, source_target_pairs={{0,4},{4,0},{8,12},{12,8},{16,20},{20,16},{24,28},{28,24},{1,5},{5... | collective-permute-start | bytes 3145736 | tf_op jit(solution)/shard_map/ppermute | solution.py:451
  932.8 52.2 %collective-permute-start.80 = (bf16[4,128,1024]{2,1,0:T(8,128)(2,1)}, bf16[4,128,1024]{2,1,0:T(8,128)(2,1)}, u32[]{:S(2)}, u32[]{:S(2)}) collective-permute-start(bf16[4,128,1024]{2,1,0:T(8,128)(2,1)} %bitcast.336), channel_id=1, source_target_pairs={{0,4},{4,0},{8,12},{12,8},{16,20},{20,16},{24,28},{28,24},{1,5},{5... | collective-permute-start | bytes 3145736 | tf_op jit(solution)/shard_map/ppermute | solution.py:451
  (319 other events, 3418.0 us)
Sparse Core Ops, SparseCore 0:
  10.7 53.7 all-gather.8
  67.1 48.9 all-gather.6
  118.8 71.5 all-gather.10
  192.9 49.3 all-gather.14
  244.8 48.9 all-gather.12
  296.3 71.5 all-gather.16

commit v2 on v1

--- a/solution.py
+++ b/solution.py
@@ -59,7 +59,8 @@
     )
 
 
-VM=pltpu.CompilerParams(vmem_limit_bytes=56*1024*1024)
+VM = pltpu.CompilerParams(vmem_limit_bytes=56 * 1024 * 1024)
+LIGHT = pl.CostEstimate(flops=1, bytes_accessed=1, transcendentals=0)
 
 def bias_kernel(table_ref, index_ref, out_ref):
     heads, groups, _ = table_ref.shape
@@ -91,7 +92,7 @@
     index = jnp.pad(index, ((0, 0), (0, pad)))
     return pl.pallas_call(bias_kernel,
         out_shape=jax.ShapeDtypeStruct((heads, n, n + pad), jnp.bfloat16),
-        compiler_params=VM)(table.astype(jnp.float32).reshape(heads, reach // LANES, LANES), index)
+        cost_estimate=LIGHT, compiler_params=VM)(table.astype(jnp.float32).reshape(heads, reach // LANES, LANES), index)
 
 LOW=64
 def bucket_kernel(sum_ref, index_ref, out_ref):
@@ -117,7 +118,7 @@
     heads = summed.shape[0]
     out = pl.pallas_call(bucket_kernel,
         out_shape=jax.ShapeDtypeStruct((heads * (reach // LOW), LOW), jnp.float32),
-        compiler_params=VM)(summed, index)
+        cost_estimate=LIGHT, compiler_params=VM)(summed, index)
     return out.reshape(heads, reach)
 QUARTER=64
 NT=(((1,),(1,)),((),()))
@@ -191,7 +192,7 @@
                       pl.BlockSpec(bias.shape, lambda i, p: (0, 0, 0))],
             out_specs=[pl.BlockSpec((rows, width), lambda i, p: (0, 0)),
                        pl.BlockSpec((per, heads, size, size), lambda i, p: (i, 0, 0, 0))]),
-        compiler_params=VM,
+        cost_estimate=LIGHT, compiler_params=VM,
         name="self_forward",
     )(position, qkv, bias)
 
@@ -248,7 +249,7 @@
                       pl.BlockSpec(grad.shape, lambda i, p: (0, 0))],
             out_specs=[pl.BlockSpec(qkv.shape, lambda i, p: (0, 0)),
                        pl.BlockSpec((heads, size, size), lambda i, p: (0, 0, 0))]),
-        compiler_params=VM,
+        cost_estimate=LIGHT, compiler_params=VM,
         name="self_backward",
     )(position, qkv, probs, grad)
 PAD=128
@@ -279,7 +280,7 @@
                   pl.BlockSpec((1, PAD), lambda i: (0, 0))],
         out_specs=[pl.BlockSpec((rows, LANES), col), pl.BlockSpec((2, rows, PAD), lambda i: (i, 0, 0))],
         out_shape=[jax.ShapeDtypeStruct((rows, width), jnp.bfloat16), jax.ShapeDtypeStruct((2 * pairs, rows, PAD), jnp.bfloat16)],
-        compiler_params=VM, name="cross_forward")(q, k, v, bias)
+        cost_estimate=LIGHT, compiler_params=VM, name="cross_forward")(q, k, v, bias)
 
 def cross_backward_kernel(q_ref, k_ref, v_ref, probs_ref, grad_ref, dq_ref, dk_ref, dv_ref):
     rows = q_ref.shape[0]
@@ -315,183 +316,415 @@
         in_specs=[tok, txt, txt, pl.BlockSpec((2, rows, PAD), lambda i: (i, 0, 0)), tok],
         out_specs=[tok, txt, txt],
         out_shape=[jax.ShapeDtypeStruct((rows, width), jnp.bfloat16), jax.ShapeDtypeStruct((PAD, width), jnp.float32), jax.ShapeDtypeStruct((PAD, width), jnp.float32)],
-        compiler_params=VM, name="cross_backward")(q, k, v, probs, grad)
-
-def gelu_parts(u):
+        cost_estimate=LIGHT, compiler_params=VM, name="cross_backward")(q, k, v, probs, grad)
+
+
+def gelu_slope(u):
     inner = 0.7978845608028654 * (u + 0.044715 * u * u * u)
     th = jnp.tanh(inner)
-    slope = 0.5 * (1.0 + th) + 0.5 * u * (1.0 - th * th) * (0.7978845608028654 * (1.0 + 3.0 * 0.044715 * u * u))
-    return 0.5 * u * (1.0 + th), slope
-
-
-def feed_forward_kernel(a_ref, b_ref, up_ref, down_ref, hidden_ref, active_ref, pa_ref, pb_ref, acc_ref):
-    step = pl.program_id(0)
+    return 0.5 * (1.0 + th) + 0.5 * u * (1.0 - th * th) * (0.7978845608028654 * (1.0 + 3.0 * 0.044715 * u * u))
+
+
+FF_TILE = 256
+
+
+def feed_forward_kernel(a_ref, b_ref, up_ref, down_ref, hidden_ref, active_ref, pa_ref, pb_ref):
     rows = a_ref.shape[0]
+    units = up_ref.shape[1]
     for at, ref in ((0, a_ref), (rows, b_ref)):
-        u = dot(ref[...], up_ref[...])
-        hidden_ref[pl.ds(at, rows), :] = u.astype(jnp.bfloat16)
-        active = jax.nn.gelu(u, approximate=True).astype(jnp.bfloat16)
-        active_ref[pl.ds(at, rows), :] = active
-        part = dot(active, down_ref[...], NT)
-
-        @pl.when(step == 0)
-        def _():
-            acc_ref[pl.ds(at, rows), :] = part
-
-        @pl.when(step > 0)
-        def _():
-            acc_ref[pl.ds(at, rows), :] += part
-
-    @pl.when(step == pl.num_programs(0) - 1)
-    def _():
-        pa_ref[...] = acc_ref[pl.ds(0, rows), :].astype(jnp.bfloat16)
-        pb_ref[...] = acc_ref[pl.ds(rows, rows), :].astype(jnp.bfloat16)
-
-
-FF_TILE = 256
+        for t in range(0, units, FF_TILE):
+            u = dot(ref[...], up_ref[:, t : t + FF_TILE])
+            hidden_ref[pl.ds(at, rows), t : t + FF_TILE] = u.astype(jnp.bfloat16)
+            active_ref[pl.ds(at, rows), t : t + FF_TILE] = jax.nn.gelu(u, approximate=True).astype(jnp.bfloat16)
+    pa_ref[...] = dot(active_ref[pl.ds(0, rows), :], down_ref[...], NT).astype(jnp.bfloat16)
+    pb_ref[...] = dot(active_ref[pl.ds(rows, rows), :], down_ref[...], NT).astype(jnp.bfloat16)
+
+
+def half_columns(weights):
+    units = weights.shape[1] // 2
+    return [pl.BlockSpec((weights.shape[0], units), lambda i: (0, 0)), pl.BlockSpec((weights.shape[0], units), lambda i: (0, 1))]
 
 
 def feed_forward_call(a, b, weights):
     rows, width = a.shape
-    hidden = weights.shape[1] // 2
-    tiles = hidden // FF_TILE
+    units = weights.shape[1] // 2
     whole = pl.BlockSpec((rows, width), lambda i: (0, 0))
-    strip = pl.BlockSpec((2 * rows, FF_TILE), lambda i: (0, i))
+    wide = pl.BlockSpec((2 * rows, units), lambda i: (0, 0))
     return pl.pallas_call(
         feed_forward_kernel,
-        grid=(tiles,),
-        in_specs=[
-            whole,
-            whole,
-            pl.BlockSpec((width, FF_TILE), lambda i: (0, i)),
-            pl.BlockSpec((width, FF_TILE), lambda i: (0, tiles + i)),
-        ],
-        out_specs=[strip, strip, whole, whole],
+        grid=(1,),
+        in_specs=[whole, whole] + half_columns(weights),
+        out_specs=[wide, wide, whole, whole],
         out_shape=[
-            jax.ShapeDtypeStruct((2 * rows, hidden), jnp.bfloat16),
-            jax.ShapeDtypeStruct((2 * rows, hidden), jnp.bfloat16),
+            jax.ShapeDtypeStruct((2 * rows, units), jnp.bfloat16),
+            jax.ShapeDtypeStruct((2 * rows, units), jnp.bfloat16),
             jax.ShapeDtypeStruct((rows, width), jnp.bfloat16),
             jax.ShapeDtypeStruct((rows, width), jnp.bfloat16),
         ],
-        scratch_shapes=[pltpu.VMEM((2 * rows, width), jnp.float32)],
-        compiler_params=VM,
-        cost_estimate=pl.CostEstimate(
-            flops=8 * rows * width * hidden, bytes_accessed=4 * width * hidden + 12 * rows * width, transcendentals=2 * rows * hidden
-        ),
+        cost_estimate=LIGHT, compiler_params=VM,
         name="feed_forward",
     )(a, b, weights, weights)
 
 
-def feed_backward_kernel(a_ref, b_ref, hidden_ref, up_ref, down_ref, grad_ref, pa_ref, pb_ref, acc_ref):
-    step = pl.program_id(0)
+def feed_backward_kernel(a_ref, b_ref, hidden_ref, up_ref, down_ref, grad_ref, pa_ref, pb_ref):
     rows = a_ref.shape[0]
+    units = up_ref.shape[1]
     for at, ref in ((0, a_ref), (rows, b_ref)):
-        slope = gelu_parts(hidden_ref[pl.ds(at, rows), :].astype(jnp.float32))[1]
-        grad = (dot(ref[...], down_ref[...]) * slope).astype(jnp.bfloat16)
-        grad_ref[pl.ds(at, rows), :] = grad
-        part = dot(grad, up_ref[...], NT)
-
-        @pl.when(step == 0)
-        def _():
-            acc_ref[pl.ds(at, rows), :] = part
-
-        @pl.when(step > 0)
-        def _():
-            acc_ref[pl.ds(at, rows), :] += part
-
-    @pl.when(step == pl.num_programs(0) - 1)
-    def _():
-        pa_ref[...] = acc_ref[pl.ds(0, rows), :].astype(jnp.bfloat16)
-        pb_ref[...] = acc_ref[pl.ds(rows, rows), :].astype(jnp.bfloat16)
+        for t in range(0, units, FF_TILE):
+            slope = gelu_slope(hidden_ref[pl.ds(at, rows), t : t + FF_TILE].astype(jnp.float32))
+            grad_ref[pl.ds(at, rows), t : t + FF_TILE] = (dot(ref[...], down_ref[:, t : t + FF_TILE]) * slope).astype(jnp.bfloat16)
+    pa_ref[...] = dot(grad_ref[pl.ds(0, rows), :], up_ref[...], NT).astype(jnp.bfloat16)
+    pb_ref[...] = dot(grad_ref[pl.ds(rows, rows), :], up_ref[...], NT).astype(jnp.bfloat16)
 
 
 def feed_backward_call(a, b, hidden, weights):
     rows, width = a.shape
     units = weights.shape[1] // 2
-    tiles = units // FF_TILE
     whole = pl.BlockSpec((rows, width), lambda i: (0, 0))
-    strip = pl.BlockSpec((2 * rows, FF_TILE), lambda i: (0, i))
+    wide = pl.BlockSpec((2 * rows, units), lambda i: (0, 0))
     return pl.pallas_call(
         feed_backward_kernel,
-        grid=(tiles,),
-        in_specs=[
-            whole,
-            whole,
-            strip,
-            pl.BlockSpec((width, FF_TILE), lambda i: (0, i)),
-            pl.BlockSpec((width, FF_TILE), lambda i: (0, tiles + i)),
-        ],
-        out_specs=[strip, whole, whole],
+        grid=(1,),
+        in_specs=[whole, whole, wide] + half_columns(weights),
+        out_specs=[wide, whole, whole],
         out_shape=[
             jax.ShapeDtypeStruct((2 * rows, units), jnp.bfloat16),
             jax.ShapeDtypeStruct((rows, width), jnp.bfloat16),
             jax.ShapeDtypeStruct((rows, width), jnp.bfloat16),
         ],
-        scratch_shapes=[pltpu.VMEM((2 * rows, width), jnp.float32)],
-        compiler_params=VM,
-        cost_estimate=pl.CostEstimate(
-            flops=8 * rows * width * units, bytes_accessed=4 * width * units + 10 * rows * width, transcendentals=2 * rows * units
-        ),
+        cost_estimate=LIGHT, compiler_params=VM,
         name="feed_backward",
     )(a, b, hidden, weights, weights)
 
-def adam_update(master, first, second, grad, rate):
+
+def weight_grad_kernel(counts, splits, order_ref, *refs):
+    step = pl.program_id(0)
+    (ln_a, rn_a), (ln_b, rn_b) = splits
+    left = (refs[:ln_a], refs[ln_a : ln_a + ln_b])
+    refs = refs[ln_a + ln_b :]
+    right = (refs[:rn_a], refs[rn_a : rn_a + rn_b])
+    out_ref, turned_ref = refs[rn_a + rn_b :]
+    blocks = order_ref.shape[0]
+    width = turned_ref.shape[0] // blocks
+
+    def turn(pieces):
+        at = 0
+        for ref in pieces:
+            rows = ref.shape[0]
+            for p in range(blocks):
+                column = pl.multiple_of(order_ref[p] * width, width)
+                turned_ref[pl.ds(p * width, width), pl.ds(at, rows)] = ref[:, pl.ds(column, width)].T
+            at += rows
+
+    def product(pieces):
+        at = 0
+        total = None
+        for ref in pieces:
+            rows = ref.shape[0]
+            part = dot(turned_ref[:, pl.ds(at, rows)], ref[...])
+            total = part if total is None else total + part
+            at += rows
+        out_ref[...] = total.astype(jnp.bfloat16).reshape(out_ref.shape)
+
+    for n, begin in ((0, 0), (1, counts[0])):
+
+        @pl.when(step == begin)
+        def _():
+            turn(left[n])
+
+        @pl.when(jnp.logical_and(step >= begin, step < begin + counts[n]))
+        def _():
+            product(right[n])
+
+
+GRAD_TILE = 256
+
+
+def weight_grad_call(order, lefts, rights, out_shape, out_map):
+    counts = [sum_cols // GRAD_TILE for sum_cols in (rights[0][0][0].shape[1], rights[1][0][0].shape[1])]
+    splits = [(len(lefts[n]), len(rights[n])) for n in range(2)]
+    in_specs, operands = [], []
+    for n in range(2):
+        for item in lefts[n]:
+            in_specs.append(pl.BlockSpec(item.shape, lambda i, o: (0, 0)))
+            operands.append(item)
+    for n in range(2):
+        begin, count = (0, counts[0])[n], counts[n]
+        for item, rows, block in rights[n]:
+            in_specs.append(
+                pl.BlockSpec(
+                    (rows, GRAD_TILE),
+                    lambda i, o, begin=begin, count=count, block=block: (block, jnp.clip(i - begin, 0, count - 1)),
+                )
+            )
+            operands.append(item)
+    tokens = sum(item.shape[0] for item in lefts[0])
+    width = lefts[0][0].shape[1]
+    tiles = counts[0] + counts[1]
+    block_shape = out_shape[:-1] + (GRAD_TILE,) if len(out_shape) == 2 else (1, out_shape[1], GRAD_TILE)
+    return pl.pallas_call(
+        functools.partial(weight_grad_kernel, counts, splits),
+        grid_spec=pltpu.PrefetchScalarGridSpec(
+            num_scalar_prefetch=1,
+            grid=(tiles,),
+            in_specs=in_specs,
+            out_specs=pl.BlockSpec(block_shape, out_map),
+            scratch_shapes=[pltpu.VMEM((width, tokens), jnp.bfloat16)],
+        ),
+        out_shape=jax.ShapeDtypeStruct(out_shape, jnp.bfloat16),
+        cost_estimate=LIGHT, compiler_params=VM,
+        name="weight_grad",
+    )(order, *operands)
+
+
+def regroup(columns, outer, inner):
+    pieces = []
+    for i in range(inner):
+        for o in range(outer):
+            at = (o * inner + i) * HD
+            pieces.append(columns[:, at : at + HD])
+    return jnp.concatenate(pieces, axis=1)
+
+
+def prepare_kernel(qkv_ref, out_ref, cq_ref, ckv_ref, cout_ref, up_ref, down_ref, self_ref, pair_ref, text_ref, feed_ref):
+    wide = cq_ref.shape[2]
+    heads = wide // HD
+    units = up_ref.shape[2]
+    self_ref[0, :, : 3 * wide] = regroup(qkv_ref[0], heads, 3).astype(jnp.bfloat16)
+    self_ref[0, :, 3 * wide :] = out_ref[0].T.astype(jnp.bfloat16)
+    pair_ref[0, :, :wide] = cq_ref[0].astype(jnp.bfloat16)
+    pair_ref[0, :, wide:] = cout_ref[0].T.astype(jnp.bfloat16)
+    text_ref[0] = regroup(ckv_ref[0], heads, 2).astype(jnp.bfloat16)
+    feed_ref[0, :, :units] = up_ref[0].astype(jnp.bfloat16)
+    feed_ref[0, :, units:] = down_ref[0].T.astype(jnp.bfloat16)
+
+
+def layer_block(shape):
+    return pl.BlockSpec((1,) + tuple(shape[1:]), lambda i: (i, 0, 0))
+
+
+def prepare_call(masters):
+    layers, block, wide = masters[2].shape
+    units = masters[5].shape[2]
+    shapes = [(layers, block, 4 * wide), (layers, block, 2 * wide), (layers, block, 2 * wide), (layers, block, 2 * units)]
+    return pl.pallas_call(
+        prepare_kernel,
+        grid=(layers,),
+        in_specs=[layer_block(item.shape) for item in masters],
+        out_specs=[layer_block(shape) for shape in shapes],
+        out_shape=[jax.ShapeDtypeStruct(shape, jnp.bfloat16) for shape in shapes],
+        cost_estimate=LIGHT, compiler_params=VM,
+        name="prepare",
+    )(*masters)
+
+
+def adam_math(master, first, second, grad, rate):
     first_new = BETA_ONE * first + (1.0 - BETA_ONE) * grad
     second_new = BETA_TWO * second + (1.0 - BETA_TWO) * grad * grad
     step_size = (
-        first_new
-        / (1.0 - BETA_ONE**STEP)
-        / (jnp.sqrt(second_new / (1.0 - BETA_TWO**STEP)) + ADAM_EPS)
+        first_new / (1.0 - BETA_ONE**STEP) / (jnp.sqrt(second_new / (1.0 - BETA_TWO**STEP)) + ADAM_EPS)
     )
     master_new = master - rate * (step_size + DECAY_RATE * master)
     return (master_new, first_new, second_new, master_new.astype(jnp.bfloat16))
 
 
+def adam_kernel(plans, n_grads, *refs):
+    layer = pl.program_id(0)
+    count = len(plans)
+    sources = [jnp.where(layer == 0, refs[2 * n][...], refs[2 * n + 1][...]).astype(jnp.float32) for n in range(n_grads)]
+    refs = refs[2 * n_grads :]
+    for n, (source, begin, width, kind, rate) in enumerate(plans):
+        master, first, second = [refs[3 * n + m][0] for m in range(3)]
+        outs = refs[3 * count + 4 * n : 3 * count + 4 * n + 4]
+        grad = sources[source][:, begin : begin + width]
+        if kind == "turn":
+            grad = grad.T
+        elif kind:
+            grad = regroup(grad, kind, width // (kind * HD))
+        for ref, value in zip(outs, adam_math(master, first, second, grad, rate)):
+            ref[0] = value
+
+
+def adam_call(plans, grads, states):
+    in_specs, operands, out_specs, out_shape = [], [], [], []
+    for pair in grads:
+        for item in pair:
+            in_specs.append(pl.BlockSpec(item.shape, lambda i: (0, 0)))
+            operands.append(item)
+    for group in states:
+        for item in group:
+            in_specs.append(layer_block(item.shape))
+            operands.append(item)
+        shape = group[0].shape
+        for dtype in (jnp.float32, jnp.float32, jnp.float32, jnp.bfloat16):
+            out_specs.append(layer_block(shape))
+            out_shape.append(jax.ShapeDtypeStruct(shape, dtype))
+    result = pl.pallas_call(
+        functools.partial(adam_kernel, plans, len(grads)),
+        grid=(states[0][0].shape[0],),
+        in_specs=in_specs,
+        out_specs=out_specs,
+        out_shape=out_shape,
+        cost_estimate=LIGHT, compiler_params=VM,
+        name="adam",
+    )(*operands)
+    return [result[4 * n : 4 * n + 4] for n in range(len(states))]
+
+
 def exchange(value, axis, bit, size):
     return lax.ppermute(value, axis, [(i, i ^ bit) for i in range(size)])
 
 
-def share_rows(own):
+def after(value, *anchors):
+    return lax.optimization_barrier((value, anchors))[0]
+
+
+def share_rows(own, meanwhile):
+    far = exchange(own, "mp", 2, 4)
     near = exchange(own, "mp", 1, 4)
+    done = meanwhile(own, near)
+    far = after(far, done)
+    return (own, near, far, exchange(far, "mp", 1, 4)), done
+
+
+def share_small(own):
     far = exchange(own, "mp", 2, 4)
+    near = exchange(own, "mp", 1, 4)
     return (own, near, far, exchange(far, "mp", 1, 4))
 
 
-def collect_parts(parts):
+def collect_parts(parts, meanwhile=None):
     beside = exchange(parts[3], "mp", 1, 4)
-    crossing = (parts[2].astype(jnp.float32) + beside.astype(jnp.float32)).astype(jnp.bfloat16)
+    crossing = narrow(parts[2].astype(jnp.float32) + beside.astype(jnp.float32))
     far = exchange(crossing, "mp", 2, 4)
-    near = exchange(parts[1], "mp", 1, 4)
-    return parts[0].astype(jnp.float32) + near.astype(jnp.float32) + far.astype(jnp.float32)
+    near_part, done = parts[1], None
+    if meanwhile is not None:
+        done = meanwhile(crossing)
+        far = after(far, done)
+    near = exchange(after(parts[1], crossing), "mp", 1, 4)
+    total = parts[0].astype(jnp.float32) + near.astype(jnp.float32) + far.astype(jnp.float32)
+    return total if meanwhile is None else (total, done)
 
 
 def bits_of(size):
     return [1 << n for n in range(size.bit_length() - 1)]
 
 
-def halve_rows(total, size):
+class Flow:
+    def __init__(self, stages):
+        self.stages = stages
+        self.result = None
+        self.pending = next(stages)
+
+    def take(self, value):
+        try:
+            self.pending = self.stages.send(value)
+        except StopIteration as stop:
+            self.pending = None
+            self.result = stop.value
+
+    def finish(self):
+        while self.pending is not None:
+            self.take(self.pending)
+        return self.result
+
+
+def tick(anchor, *flows):
+    flows = [flow for flow in flows if flow is not None and flow.pending is not None]
+    if not flows:
+        return anchor
+    anchor, values = lax.optimization_barrier((anchor, [flow.pending for flow in flows]))
+    for flow, value in zip(flows, values):
+        flow.take(value)
+    return anchor
+
+
+def block_order(size):
+    me = lax.axis_index("dp").astype(jnp.int32)
+    if (D // size) % LANES:
+        return jnp.arange(D // LANES, dtype=jnp.int32), False
+    order = [0]
+    for bit in reversed(bits_of(size)):
+        order = order + [item | bit for item in order]
+    return jnp.array(order, jnp.int32) ^ me, True
+
+
+def halving(total, size, ordered):
     me = lax.axis_index("dp")
-    width = total.shape[1]
-    rows = total.shape[0] // size
-    blocks = total.reshape(size, rows, width)
+    rows, width = total.shape
+    if ordered:
+        for bit in bits_of(size):
+            half = total.shape[0] // 2
+            got = yield exchange(narrow(total[half:]), "dp", bit, size)
+            total = total[:half].astype(jnp.float32) + got.astype(jnp.float32)
+            if bit * 2 < size:
+                total = narrow(total)
+        return total
+    blocks = total.reshape(size, rows // size, width)
     for n, bit in enumerate(bits_of(size)):
-        pairs = blocks.reshape(blocks.shape[0] // 2, 2, rows, width)
+        pairs = blocks.reshape(blocks.shape[0] // 2, 2, rows // size, width)
         mine = (me >> n) & 1
         keep = lax.dynamic_index_in_dim(pairs, mine, 1, keepdims=False)
         send = lax.dynamic_index_in_dim(pairs, 1 - mine, 1, keepdims=False)
-        got = exchange(send, "dp", bit, size)
+        got = yield exchange(send, "dp", bit, size)
         total = keep.astype(jnp.float32) + got.astype(jnp.float32)
-        blocks = total.astype(jnp.bfloat16)
-    return total.reshape(rows, width)
-
-
-def gather_small(own, size):
+        blocks = narrow(total)
+    return total.reshape(rows // size, width)
+
+
+def doubling(own, size):
+    me = lax.axis_index("dp")
+    rows, width = own.shape
+    own = own[None, None]
+    for n, bit in reversed(list(enumerate(bits_of(size)))):
+        got = yield exchange(own, "dp", bit, size)
+        own = jnp.where(((me >> n) & 1) == 0, jnp.concatenate([own, got], axis=1), jnp.concatenate([got, own], axis=1))
+        own = own.reshape(own.shape[0] * 2, 1, rows, width)
+    return own.reshape(size * rows, width)
+
+
+def collecting(parts):
+    beside, near = yield (exchange(parts[3], "mp", 1, 4), exchange(parts[1], "mp", 1, 4))
+    crossing = narrow(parts[2].astype(jnp.float32) + beside.astype(jnp.float32))
+    far = yield exchange(crossing, "mp", 2, 4)
+    return parts[0].astype(jnp.float32) + near.astype(jnp.float32) + far.astype(jnp.float32)
+
+
+def collect_then_gather(parts, size):
+    total = yield from collecting(parts)
+    total = narrow(total)
+    got = yield exchange(total, "dp", 1, size)
+    slots = narrow(total.astype(jnp.float32) + got.astype(jnp.float32))[None, None]
+    me = lax.axis_index("dp")
+    for n, bit in reversed(list(enumerate(bits_of(size)))[1:]):
+        got = yield exchange(slots, "dp", bit, size)
+        slots = jnp.where(((me >> n) & 1) == 0, jnp.concatenate([slots, got], axis=1), jnp.concatenate([got, slots], axis=1))
+        slots = slots.reshape((slots.shape[0] * 2, 1) + slots.shape[2:])
+    return slots[:, 0]
+
+
+def pair_up(slots):
+    got = yield (exchange(slots[1], "mp", 1, 4), exchange(slots[3], "mp", 1, 4))
+    return jnp.concatenate([narrow(slots[2 * k].astype(jnp.float32) + got[k].astype(jnp.float32)) for k in range(2)], axis=1)
+
+
+def halve_then_cross(total, size, ordered, width):
+    total = yield from halving(total, size, ordered)
+    got = yield exchange(narrow(total[:, width : 2 * width]), "mp", 2, 4)
+    return total[:, :width] + got.astype(jnp.float32), total[:, 2 * width :]
+
+
+def gathering(own, size):
     me = lax.axis_index("dp")
     slots = own[None]
     for n, bit in enumerate(bits_of(size)):
-        got = exchange(slots, "dp", bit, size)
+        got = yield exchange(slots, "dp", bit, size)
         slots = jnp.where(((me >> n) & 1) == 0, jnp.concatenate([slots, got]), jnp.concatenate([got, slots]))
     return slots
+
+
+def gather_small(own, size):
+    return Flow(gathering(own, size)).finish()
 
 
 def modulate(latent, scale, shift):
@@ -499,22 +732,8 @@
     return (normed * (1.0 + scale) + shift).astype(jnp.bfloat16)
 
 
-def split_heads(columns, parts):
-    rows = columns.shape[0]
-    return columns.reshape(rows, -1, parts, HD).swapaxes(1, 2).reshape(rows, -1)
-
-
-def join_heads(columns, parts):
-    rows = columns.shape[0]
-    return columns.reshape(rows, parts, -1, HD).swapaxes(1, 2).reshape(rows, -1)
-
-
 def narrow(value):
     return value.astype(jnp.bfloat16)
-
-
-def gather_group(shards):
-    return lax.all_gather(jnp.concatenate(shards, axis=1), "dp", axis=0, tiled=True)
 
 
 def mm(a, b, dims=(((1,), (0,)), ((), ()))):
@@ -526,10 +745,30 @@
     masters, firsts, seconds = args[8:17], args[17:26], args[26:35]
     groups = lax.axis_size("dp")
     rates = learning_rates()
+    own = latents.shape[0]
+    half = 2 * own
+    wide = masters[1].shape[1]
+    index_tables = (rel_index_s, rel_index_t)
+    reaches = (masters[7].shape[1] * groups, masters[8].shape[1] * groups)
+
+    order, ordered = block_order(groups)
+
+    block = D // groups
+    self_shards, pair_shards, text_shards, feed_shards = prepare_call(masters[:7])
+    pair_shards = pair_shards.reshape(LAYERS * block, 2 * wide)
+    other = exchange(pair_shards, "mp", 2, 4)
+
+    def cross_shard(layer):
+        rows = slice(layer * block, (layer + 1) * block)
+        return [pair_shards[rows], other[rows], text_shards[layer]]
+
+    self_flow_0 = Flow(doubling(self_shards[0], groups))
+
     position = lax.axis_index("mp").astype(jnp.int32)[None]
     clip_index = lax.axis_index("dp") // 2
     text_rows = lax.dynamic_index_in_dim(text_embed, clip_index, 0, keepdims=False)
     texts = text_rows.shape[0]
+    texts_pad = -(-texts // 16) * 16
     text_rows = jnp.pad(text_rows, ((0, PAD - texts), (0, 0)))
     mask_row = lax.dynamic_index_in_dim(text_mask, clip_index, 0, keepdims=False)
     column = jnp.arange(PAD, dtype=jnp.int32)
@@ -538,6 +777,7 @@
     band_now = lax.dynamic_index_in_dim(band_ids, clip_index, 0, keepdims=False)
     selector = (jnp.arange(modulation.shape[0], dtype=jnp.int32) == band_now).astype(jnp.float32)
     mod_rows = lax.dynamic_index_in_dim(modulation, band_now, 0, keepdims=False)
+    text_columns = lax.dynamic_slice_in_dim(text_embed, lax.axis_index("dp") * (D // groups), D // groups, axis=2)
 
     tables = gather_small(jnp.concatenate([narrow(masters[7]), narrow(masters[8])], axis=1), groups)
     tables = tables.swapaxes(0, 1)
@@ -545,40 +785,50 @@
     table_s = tables[:, :, :cut].reshape(tables.shape[0], -1)
     table_t = tables[:, :, cut:].reshape(tables.shape[0], -1)
     biases = (make_bias(table_s, rel_index_s), make_bias(table_t, rel_index_t))
-    index_tables = (rel_index_s, rel_index_t)
-    reaches = (table_s.shape[1], table_t.shape[1])
-
+
+    latent = latents
+    saved = []
     weights = []
     for layer in range(LAYERS):
-        self_group = gather_group([split_heads(narrow(masters[0][layer]), 3), narrow(masters[1][layer]).T])
-        cross_group = gather_group(
-            [narrow(masters[2][layer]), narrow(masters[4][layer]).T, split_heads(narrow(masters[3][layer]), 2)]
-        )
-        feed_group = gather_group([narrow(masters[5][layer]), narrow(masters[6][layer]).T])
-        weights.append((self_group, cross_group, feed_group))
-
-    latent = latents
-    saved = []
-    wide = masters[1].shape[1]
-    for layer in range(LAYERS):
-        self_w, cross_w, feed_w = weights[layer]
         base = 9 * layer
         record = {"in": latent}
-        rows = share_rows(modulate(latent, mod_rows[base + 1], mod_rows[base]))
-        qkv = jnp.concatenate([narrow(mm(item, self_w[:, : 3 * wide])) for item in rows], axis=0)
+        sending = modulate(latent, mod_rows[base + 1], mod_rows[base])
+        if layer == 0:
+            cross_start = tick(jnp.concatenate(cross_shard(0), axis=1), self_flow_0)
+            cross_flow_0 = Flow(doubling(cross_start, groups))
+            biases = tick(biases, self_flow_0, cross_flow_0)
+            feed_start = tick(feed_shards[0], self_flow_0, cross_flow_0)
+            feed_flow_0 = Flow(doubling(feed_start, groups))
+            self_w = after(self_flow_0.finish(), feed_start, biases)
+        else:
+            self_w = self_flow_1.finish()
+        w_in = self_w[:, : 3 * wide]
+        rows, near_qkv = share_rows(sending, lambda one, two: (narrow(mm(one, w_in)), narrow(mm(two, w_in))))
+        qkv = jnp.concatenate(near_qkv + tuple(narrow(mm(item, w_in)) for item in rows[2:]), axis=0)
         mixed, probs = self_forward_call(layer, position, qkv, biases[layer])
         w_out = self_w[:, 3 * wide :]
-        own = latents.shape[0]
-        parts = [narrow(mm(mixed[k * own : (k + 1) * own], w_out, NT)) for k in range(4)]
-        branch = collect_parts(parts)
+        project = lambda k: narrow(mm(mixed[k * own : (k + 1) * own], w_out, NT))
+        p2, p3 = project(2), project(3)
+        p3 = tick(p3, feed_flow_0 if layer == 0 else feed_flow_1)
+        branch = collect_parts([project(0), project(1), p2, p3])
+        if layer == 0:
+            branch = tick(branch, feed_flow_0, cross_flow_0)
+            self_flow_1 = Flow(doubling(after(self_shards[1], branch), groups))
+        else:
+            branch = tick(branch, feed_flow_1, cross_flow_1)
         record["self"] = (rows, qkv, probs, mixed, branch)
         latent = latent + mod_rows[base + 2] * branch
         record["mid"] = latent
         normed = modulate(latent, mod_rows[base + 4], mod_rows[base + 3])
-        keyval = share_rows(narrow(mm(text_rows, cross_w[:, 2 * wide :])))
+        if layer == 0:
+            cross_w = cross_flow_0.finish()
+        else:
+            cross_w = cross_flow_1.finish()
+        keyval = share_small(narrow(mm(text_rows, cross_w[:, 4 * wide :])))
         keys = jnp.concatenate([item[:, :wide] for item in keyval], axis=1)
         values = jnp.concatenate([item[:, wide:] for item in keyval], axis=1)
-        cross_all = share_rows(cross_w[:, : 2 * wide])
+        across = exchange(cross_w[:, : 4 * wide], "mp", 1, 4)
+        cross_all = (cross_w[:, : 2 * wide], across[:, : 2 * wide], cross_w[:, 2 * wide : 4 * wide], across[:, 2 * wide :])
         w_cq = jnp.concatenate([item[:, :wide] for item in cross_all], axis=1)
         w_cout = jnp.concatenate([item[:, wide:] for item in cross_all], axis=1)
         queries = narrow(mm(normed, w_cq))
@@ -586,34 +836,58 @@
         branch = mm(mixed, w_cout, NT)
         record["cross"] = (normed, queries, keys, values, probs, mixed, branch, w_cq, w_cout)
         latent = latent + mod_rows[base + 5] * branch
+        if layer == 0:
+            latent = tick(latent, self_flow_1)
         record["late"] = latent
-        rows = share_rows(modulate(latent, mod_rows[base + 7], mod_rows[base + 6]))
-        hidden_near, active_near, p0, p1 = feed_forward_call(rows[0], rows[1], feed_w)
+        if layer == 0:
+            feed_w = tick(feed_flow_0.finish(), self_flow_1)
+            cross_flow_1 = Flow(doubling(after(jnp.concatenate(cross_shard(1), axis=1), feed_w), groups))
+        else:
+            feed_w = feed_flow_1.finish()
+        weights.append((self_w, feed_w))
+        rows, (hidden_near, active_near, p0, p1) = share_rows(
+            modulate(latent, mod_rows[base + 7], mod_rows[base + 6]), lambda one, two: feed_forward_call(one, two, feed_w)
+        )
         hidden_far, active_far, p2, p3 = feed_forward_call(rows[2], rows[3], feed_w)
+        if layer == 0:
+            p3 = tick(p3, cross_flow_1)
         branch = collect_parts([p0, p1, p2, p3])
+        if layer == 0:
+            branch = tick(branch, cross_flow_1, self_flow_1)
+            feed_flow_1 = Flow(doubling(after(feed_shards[1], branch), groups))
         record["feed"] = (rows, (hidden_near, hidden_far), (active_near, active_far), branch)
         latent = latent + mod_rows[base + 8] * branch
         saved.append(record)
 
     grad_latent = cotangent
     mod_grads = [None, None]
-    reduced = [None, None]
+    feed_flows, self_flows, cross_flows, tables_sent, kv_grads = [None] * 2, [None] * 2, [None] * 2, [None] * 2, [None] * 2
+    kv_flow = None
     for layer in reversed(range(LAYERS)):
-        self_w, cross_w, feed_w = weights[layer]
+        self_w, feed_w = weights[layer]
+        last = layer == 0
+        late = None if not last else self_flows[1]
         base = 9 * layer
         record = saved[layer]
         rows, hiddens, actives, branch = record["feed"]
         gate_m = jnp.sum(grad_latent * branch, axis=0)
-        grads = share_rows(narrow(mod_rows[base + 8] * grad_latent))
-        dh_near, p0, p1 = feed_backward_call(grads[0], grads[1], hiddens[0], feed_w)
+        grads, (dh_near, p0, p1) = share_rows(
+            narrow(mod_rows[base + 8] * grad_latent), lambda one, two: feed_backward_call(one, two, hiddens[0], feed_w)
+        )
         dh_far, p2, p3 = feed_backward_call(grads[2], grads[3], hiddens[1], feed_w)
-        grad_input = collect_parts([p0, p1, p2, p3])
-        grad_hidden = jnp.concatenate([dh_near, dh_far], axis=0)
-        active = jnp.concatenate(actives, axis=0)
-        all_rows = jnp.concatenate(rows, axis=0)
-        all_grads = jnp.concatenate(grads, axis=0)
-        feed_g = jnp.concatenate([narrow(mm(all_rows, grad_hidden, TN)), narrow(mm(all_grads, active, TN))], axis=1)
-        feed_sum = halve_rows(feed_g, groups)
+        units = dh_near.shape[1]
+        grad_input, feed_g = collect_parts(
+            [p0, p1, p2, p3],
+            lambda sent: weight_grad_call(
+                order,
+                (rows, grads),
+                (((after(dh_near, sent), half, 0), (dh_far, half, 0)), ((actives[0], half, 0), (actives[1], half, 0))),
+                (D, 2 * units),
+                lambda i, o: (0, i),
+            ),
+        )
+        feed_flows[layer] = Flow(halving(feed_g, groups, ordered))
+        grad_input = tick(grad_input, late)
         normed, inverse = layer_norm(record["late"])
         grad_latent, shift_m, scale_m = modulate_back(grad_latent, grad_input, normed, inverse, mod_rows[base + 7])
 
@@ -622,64 +896,125 @@
         grad_rows = narrow(mod_rows[base + 5] * grad_latent)
         grad_mixed = narrow(mm(grad_rows, w_cout))
         grad_query, grad_key, grad_value = cross_backward_call(queries, keys, values, probs, grad_mixed)
-        grad_input = mm(grad_query, w_cq, NT)
-        grad_cq = narrow(mm(hidden, grad_query, TN))
-        grad_cout = narrow(mm(grad_rows, mixed, TN))
-        cross_parts = [
-            jnp.concatenate([grad_cq[:, k * wide : (k + 1) * wide], grad_cout[:, k * wide : (k + 1) * wide]], axis=1) for k in range(4)
-        ]
-        cross_g = collect_parts(cross_parts)
-        kv_parts = [
-            narrow(jnp.concatenate([grad_key[:, k * wide : (k + 1) * wide], grad_value[:, k * wide : (k + 1) * wide]], axis=1))
+        kv_grads[layer] = [
+            narrow(
+                jnp.concatenate(
+                    [grad_key[:texts_pad, k * wide : (k + 1) * wide], grad_value[:texts_pad, k * wide : (k + 1) * wide]], axis=1
+                )
+            )
             for k in range(4)
         ]
-        grad_kv = narrow(collect_parts(kv_parts))
-        cross_g = jnp.concatenate([narrow(cross_g), narrow(mm(text_rows, grad_kv, TN))], axis=1)
-        cross_sum = halve_rows(cross_g, groups)
+        grad_input = mm(grad_query, w_cq, NT)
         normed, inverse = layer_norm(record["mid"])
         grad_latent, shift_c, scale_c = modulate_back(grad_latent, grad_input, normed, inverse, mod_rows[base + 4])
-
+        tiles = queries.shape[1] // GRAD_TILE
+        if last:
+            kv_flow = Flow(
+                collect_then_gather([jnp.concatenate([kv_grads[0][k], kv_grads[1][k]], axis=0) for k in range(4)], groups)
+            )
+        if last:
+            grad_latent = tick(grad_latent, late, feed_flows[0])
+        sending = narrow(mod_rows[base + 2] * grad_latent)
+        w_out = self_w[:, 3 * wide :]
+        grads, (cross_g, near_mixed) = share_rows(
+            sending,
+            lambda one, two: (
+                weight_grad_call(
+                    order,
+                    ((after(hidden, sending),), (grad_rows,)),
+                    (((grad_query, own, 0),), ((mixed, own, 0),)),
+                    (tiles, D, 2 * GRAD_TILE),
+                    lambda i, o: (i % tiles, 0, i // tiles),
+                ),
+                (narrow(mm(one, w_out)), narrow(mm(two, w_out))),
+            ),
+        )
         rows, qkv, probs, mixed, branch = record["self"]
         gate_a = jnp.sum(grad_latent * branch, axis=0)
-        grads = share_rows(narrow(mod_rows[base + 2] * grad_latent))
-        w_out = self_w[:, 3 * wide :]
-        grad_mixed = jnp.concatenate([narrow(mm(item, w_out)) for item in grads], axis=0)
+        grad_mixed = jnp.concatenate(near_mixed + tuple(narrow(mm(item, w_out)) for item in grads[2:]), axis=0)
+        pairing = Flow(pair_up(cross_g))
+        grad_mixed = tick(grad_mixed, kv_flow, None if last else feed_flows[1])
         grad_qkv, summed = self_backward_call(layer, position, qkv, probs, grad_mixed)
-        parts = [narrow(mm(grad_qkv[k * own : (k + 1) * own], self_w[:, : 3 * wide], NT)) for k in range(4)]
-        grad_input = collect_parts(parts)
-        all_rows = jnp.concatenate(rows, axis=0)
-        all_grads = jnp.concatenate(grads, axis=0)
-        self_g = jnp.concatenate([narrow(mm(all_rows, grad_qkv, TN)), narrow(mm(all_grads, mixed, TN))], axis=1)
-        self_sum = halve_rows(self_g, groups)
-        table_g = bucket_sum(summed, index_tables[layer], reaches[layer])
-        table_g = table_g.reshape(table_g.shape[0], groups, -1).swapaxes(0, 1).reshape(-1, reaches[layer] // groups)
-        table_sum = halve_rows(narrow(table_g), groups)
+        grad_qkv = tick(grad_qkv, pairing, kv_flow, late, feed_flows[layer])
+        if last:
+            cross_flows[0] = Flow(halve_then_cross(pairing.finish(), groups, ordered, 2 * wide))
+        back = lambda k: narrow(mm(grad_qkv[k * own : (k + 1) * own], self_w[:, : 3 * wide], NT))
+        p2, p3 = back(2), back(3)
+        grad_input, self_g = collect_parts(
+            [back(0), back(1), p2, p3],
+            lambda sent: weight_grad_call(
+                order,
+                (rows, grads),
+                (((after(grad_qkv, sent), half, 0), (grad_qkv, half, 1)), ((mixed, half, 0), (mixed, half, 1))),
+                (D, 4 * wide),
+                lambda i, o: (0, i),
+            ),
+        )
+        if last:
+            self_flows[0] = Flow(halving(self_g, groups, ordered))
+        else:
+            both = jnp.concatenate([pairing.finish(), self_g], axis=1)
+            self_flows[1] = Flow(halve_then_cross(both, groups, ordered, 2 * wide))
+        tables_sent[layer] = summed
+        if last:
+            grad_input = tick(grad_input, kv_flow, cross_flows[0], late, feed_flows[0])
         normed, inverse = layer_norm(record["in"])
         grad_latent, shift_a, scale_a = modulate_back(grad_latent, grad_input, normed, inverse, mod_rows[base + 1])
         mod_grads[layer] = [shift_a, scale_a, gate_a, shift_c, scale_c, gate_c, shift_m, scale_m, gate_m]
-        reduced[layer] = (
-            join_heads(self_sum[:, : 3 * wide], 3),
-            self_sum[:, 3 * wide :].T,
-            cross_sum[:, :wide],
-            join_heads(cross_sum[:, 2 * wide :], 2),
-            cross_sum[:, wide : 2 * wide].T,
-            feed_sum[:, : masters[5].shape[2]],
-            feed_sum[:, masters[5].shape[2] :].T,
-            table_sum,
-        )
+        if last:
+            grad_latent = tick(grad_latent, kv_flow, cross_flows[0])
+        else:
+            grad_latent = tick(grad_latent, feed_flows[1])
+
     mod_local = jnp.stack(mod_grads[0] + mod_grads[1], axis=0)
     for bit in (1, 2):
         mod_local = mod_local + exchange(mod_local, "mp", bit, 4)
     grad_modulation = selector[:, None, None] * mod_local[None]
     for bit in bits_of(groups):
         grad_modulation = grad_modulation + exchange(grad_modulation, "dp", bit, groups)
+
+    tables_sent = after(tables_sent, grad_latent)
+    table_grads = [bucket_sum(tables_sent[layer], index_tables[layer], reaches[layer]) for layer in range(LAYERS)]
+    table_rows = [item.reshape(item.shape[0], groups, -1).swapaxes(0, 1) for item in table_grads]
+    table_rows = jnp.concatenate(table_rows, axis=2)
+    me = lax.axis_index("dp")
+    blocks = table_rows
+    for n, bit in enumerate(bits_of(groups)):
+        pairs = blocks.reshape((blocks.shape[0] // 2, 2) + blocks.shape[1:])
+        mine = (me >> n) & 1
+        keep = lax.dynamic_index_in_dim(pairs, mine, 1, keepdims=False)
+        blocks = keep + exchange(lax.dynamic_index_in_dim(pairs, 1 - mine, 1, keepdims=False), "dp", bit, groups)
+    table_sum = blocks[0]
+
+    units = masters[5].shape[2]
+    state = lambda item: (masters[item], firsts[item], seconds[item])
+    updates = [None] * 9
+    updates[5], updates[6] = adam_call(
+        ((0, 0, units, None, rates[5]), (0, units, units, "turn", rates[6])), [[flow.finish() for flow in feed_flows]], [state(5), state(6)]
+    )
+    kv_all = kv_flow.finish()
+    kv_sums = []
+    for layer in range(LAYERS):
+        grad_kv = kv_all[:, layer * texts_pad : layer * texts_pad + texts]
+        kv_sums.append(
+            lax.dot_general(text_columns, grad_kv, (((0, 1), (0, 1)), ((), ())), preferred_element_type=jnp.float32)
+        )
+    cross_1, self_1 = self_flows[1].finish()
+    cross_sums = [cross_flows[0].finish()[0], cross_1]
+    updates[2], updates[3], updates[4] = adam_call(
+        ((0, 0, wide, None, rates[2]), (1, 0, 2 * wide, 2, rates[3]), (0, wide, wide, "turn", rates[4])),
+        [cross_sums, kv_sums],
+        [state(2), state(3), state(4)],
+    )
+    self_sums = [self_flows[0].finish(), self_1]
+    updates[0], updates[1] = adam_call(
+        ((0, 0, 3 * wide, 3, rates[0]), (0, 3 * wide, wide, "turn", rates[1])), [self_sums], [state(0), state(1)]
+    )
+    updates[7] = adam_math(masters[7], firsts[7], seconds[7], table_sum[:, :cut], rates[7])
+    updates[8] = adam_math(masters[8], firsts[8], seconds[8], table_sum[:, cut:], rates[8])
     results = [latent, grad_latent, grad_modulation]
-    for item in range(9):
-        if item < 7:
-            grad = jnp.stack([reduced[0][item], reduced[1][item]], axis=0)
-        else:
-            grad = reduced[item - 7][7]
-        results.extend(adam_update(masters[item], firsts[item], seconds[item], grad, rates[item]))
+    for item in updates:
+        results.extend(item)
     return tuple(results)
 
 

time: 1050 us -> 899 us (0.86)
  local copies, waits for them, and re-layouts: 264 us -> 54.2 us
  Pallas kernels: 205 us -> 264 us
  matrix products: 104 us -> 61.1 us
  waiting for transfers between devices: 263 us -> 302 us
  between operations: 20.3 us -> 5.76 us
    ppermute x104 -> x113, waiting for transfers between devices: 172 us -> 302 us  [exchange(): return lax.ppermute(value, axis, [(i, i ^ bit) for i in range(size)])]
    unnamed x532 -> x385, local copies, waits for them, and re-layouts: 141 us -> 14.6 us
    all_gather x6 -> x0, waiting for transfers between devices: 90.7 us -> none  [gather_group(): lax.all_gather(jnp.concatenate(shards, axis=1), 'dp', axis=0, tiled=True)]
    pallas_call x8 -> x18, Pallas kernels: 92.4 us -> 154 us  [the longest x6 74.8 us: weight_grad_call(): pl.pallas_call(functools.partial(weight_grad_kernel, counts, splits), gri...]
    dynamic_slice x7 -> x3, local copies, waits for them, and re-layouts: 52.7 us -> 0.09 us  [the longest x1 0.05 us: body(): keep = lax.dynamic_index_in_dim(pairs, mine, 1, keepdims=False)]
    dot_general x56 -> x42, matrix products: 104 us -> 59.2 us  [mm(): return lax.dot_general(a, b, dims, preferred_element_type=jnp.float32)]
    convert_element_type x33 -> x2, other arithmetic: 41.1 us -> 1.23 us  [adam_math(): return (master_new, first_new, second_new, master_new.astype(jnp.bfloat16))]
    select_n x2 -> x22, other arithmetic: 0.06 us -> 34.1 us  [the longest x18 32.9 us: doubling(): jnp.where(me >> n & 1 == 0, jnp.concatenate([own, got], axis=1), jnp.conc...]
  transfers between devices with their start and end apart: 110 -> 113, of which waited for: 30 -> 46; matrix products, arithmetic and copies ran while one was open for 44% -> 22% of each run, Pallas kernels for 20% -> 28%
where the time goes in v2:
time: 899 us; the launch traced here: 888 us
  waiting for transfers between devices  302 us (34%)
  Pallas kernels  264 us (29%)
  other arithmetic  117 us (13%)
  starting transfers between devices  83.6 us (9%)
  matrix products  61.1 us (7%)
  local copies, waits for them, and re-layouts  54.2 us (6%)
    ppermute x113, waiting for transfers between devices, exchange(): return lax.ppermute(value, axis, [(i, i ^ bit) for i in range(size)])  302 us
    ppermute x113, starting transfers between devices, exchange(): return lax.ppermute(value, axis, [(i, i ^ bit) for i in range(size)])  83.6 us
    pallas_call x6, Pallas kernels, weight_grad_call(): pl.pallas_call(functools.partial(weight_grad_kernel, counts, splits), gri...  74.8 us
    dot_general x42, matrix products, mm(): return lax.dot_general(a, b, dims, preferred_element_type=jnp.float32)  59.2 us
    select_n x18, other arithmetic, doubling(): jnp.where(me >> n & 1 == 0, jnp.concatenate([own, got], axis=1), jnp.conc...  32.9 us
    pallas_call x4, Pallas kernels, feed_backward_call(): pl.pallas_call(feed_backward_kernel, grid=(1,), in_specs=[whole, whole, w...  32.5 us
    convert_element_type x28, other arithmetic, narrow(): return value.astype(jnp.bfloat16)  30.8 us
    pallas_call x4, Pallas kernels, feed_forward_call(): pl.pallas_call(feed_forward_kernel, grid=(1,), in_specs=[whole, whole] +...  28 us
  transfers between devices with their start and end apart: 113, of which 46 were waited for; matrix products, arithmetic and copies ran while one was open for 22% of the time, Pallas kernels for 28%

profile of v2, /device:TPU:0, one launch (start us, length us, event | category | flops | bytes accessed | tf_op | source)
XLA Modules:
  0.0 887.6 jit_solution(16362666844877310905)
XLA Ops:
  58.3 13.2 %collective-permute-done.8 = bf16[2,1,128,1536]{3,2,1,0:T(8,128)(2,1)S(1)} collective-permute-done((bf16[2,1,128,1536]{3,2,1,0:T(8,128)(2,1)S(1)}, bf16[2,1,128,1536]{3,2,1,0:T(8,128)(2,1)S(1)}, u32[]{:S(2)}, u32[]{:S(2)}) %collective-permute-start.8) | collective-permute-done | bytes 786464 | tf_op jit(solution)/shard_map/ppermute | solution.py:575
  111.3 14.2 %collective-permute-done.15 = bf16[320,1024]{1,0:T(8,128)(2,1)S(1)} collective-permute-done((bf16[320,1024]{1,0:T(8,128)(2,1)S(1)}, bf16[320,1024]{1,0:T(8,128)(2,1)S(1)}, u32[]{:S(2)}, u32[]{:S(2)}) %collective-permute-start.15) | collective-permute-done | bytes 655392 | tf_op jit(solution)/shard_map/ppermute | solution.py:575
  164.5 23.0 %collective-permute-done.24 = bf16[4,1,128,2048]{3,2,1,0:T(8,128)(2,1)} collective-permute-done((bf16[4,1,128,2048]{3,2,1,0:T(8,128)(2,1)}, bf16[4,1,128,2048]{3,2,1,0:T(8,128)(2,1)}, u32[]{:S(2)}, u32[]{:S(2)}) %collective-permute-start.24) | collective-permute-done | bytes 2097184 | tf_op jit(solution)/shard_map/ppermute | solution.py:575
  211.7 10.6 %collective-permute-done.28 = bf16[1,1,128,1536]{3,2,1,0:T(8,128)(2,1)S(1)} collective-permute-done((bf16[1,1,128,1536]{3,2,1,0:T(8,128)(2,1)S(1)}, bf16[1,1,128,1536]{3,2,1,0:T(8,128)(2,1)S(1)}, u32[]{:S(2)}, u32[]{:S(2)}) %collective-permute-start.28) | collective-permute-done | bytes 393248 | tf_op jit(solution)/shard_map/ppermute | solution.py:575
  227.9 14.6 %collective-permute-done.31 = bf16[320,1024]{1,0:T(8,128)(2,1)S(1)} collective-permute-done((bf16[320,1024]{1,0:T(8,128)(2,1)S(1)}, bf16[320,1024]{1,0:T(8,128)(2,1)S(1)}, u32[]{:S(2)}, u32[]{:S(2)}) %collective-permute-start.31) | collective-permute-done | bytes 655392 | tf_op jit(solution)/shard_map/ppermute | solution.py:575
  254.7 13.7 %collective-permute-done.35.refs_2_ = bf16[320,1024]{1,0:T(8,128)(2,1)S(1)} collective-permute-done((bf16[320,1024]{1,0:T(8,128)(2,1)S(1)}, bf16[320,1024]{1,0:T(8,128)(2,1)S(1)}, u32[]{:S(2)}, u32[]{:S(2)}) %collective-permute-start.35) | collective-permute-done | bytes 655392 | tf_op jit(solution)/shard_map/ppermute | solution.py:575
  273.5 8.2 self_forward.3
  283.0 12.0 %collective-permute-done.37 = bf16[1,1,128,2048]{3,2,1,0:T(8,128)(2,1)} collective-permute-done((bf16[1,1,128,2048]{3,2,1,0:T(8,128)(2,1)S(1)}, bf16[1,1,128,2048]{3,2,1,0:T(8,128)(2,1)}, u32[]{:S(2)}, u32[]{:S(2)}) %collective-permute-start.37) | collective-permute-done | bytes 524320 | tf_op jit(solution)/shard_map/ppermute | solution.py:575
  300.6 15.1 %collective-permute-done.40 = bf16[320,1024]{1,0:T(8,128)(2,1)S(1)} collective-permute-done((bf16[320,1024]{1,0:T(8,128)(2,1)S(1)}, bf16[320,1024]{1,0:T(8,128)(2,1)S(1)}, u32[]{:S(2)}, u32[]{:S(2)}) %collective-permute-start.40) | collective-permute-done | bytes 655392 | tf_op jit(solution)/shard_map/ppermute | solution.py:575
  355.9 24.1 %collective-permute-done.48 = bf16[4,1,128,2048]{3,2,1,0:T(8,128)(2,1)} collective-permute-done((bf16[4,1,128,2048]{3,2,1,0:T(8,128)(2,1)}, bf16[4,1,128,2048]{3,2,1,0:T(8,128)(2,1)}, u32[]{:S(2)}, u32[]{:S(2)}) %collective-permute-start.48) | collective-permute-done | bytes 2097184 | tf_op jit(solution)/shard_map/ppermute | solution.py:575
  393.9 8.0 feed_backward.4
  410.2 8.4 feed_backward.5
  427.0 16.2 %weight_grad.6 = bf16[1024,2048]{1,0:T(8,128)(2,1)} custom-call(s32[8]{0:T(128)} %broadcast_xor_fusion.order_ref, bf16[320,1024]{1,0:T(8,128)(2,1)} %copy-done.34, bf16[320,1024]{1,0:T(8,128)(2,1)} %copy-done.49, bf16[320,1024]{1,0:T(8,128)(2,1)} %collective-permute-done.49.a_ref.refs_2_, bf16[320,1024]{1,0:T(8,128)(2,1)} %copy-done.50, ...), custom_call_target="tpu_custom_call" | custom-call | flops 1 | bytes 1 | tf_op jit(solution)/shard_map/weight_grad/pallas_call | solution.py:465
  462.4 8.4 cross_backward.2
  477.6 9.3 %weight_grad.7 = bf16[4,1024,512]{2,1,0:T(8,128)(2,1)} custom-call(s32[8]{0:T(128)} %broadcast_xor_fusion.order_ref, bf16[320,1024]{1,0:T(8,128)(2,1)} %copy-done.57, bf16[320,1024]{1,0:T(8,128)(2,1)} %copy-done.59, bf16[320,1024]{1,0:T(8,128)(2,1)} %get-tuple-element.280.refs_2_, bf16[320,1024]{1,0:T(8,128)(2,1)} %get-tuple-element.257.refs_3_), custom_call_target="tpu_custom_call" | custom-call | flops 1 | bytes 1 | tf_op jit(solution)/shard_map/weight_grad/pallas_call | solution.py:465
  504.4 13.5 %self_backward.2 = (bf16[1280,768]{1,0:T(8,128)(2,1)}, f32[4,320,320]{2,1,0:T(8,128)}) custom-call(s32[1]{0:T(128)} %bitcast.2.position_ref, bf16[1280,768]{1,0:T(8,128)(2,1)} %pad_maximum_fusion.6.qkv_ref, bf16[4,4,320,320]{3,2,1,0:T(8,128)(2,1)} %get-tuple-element.281.probs_ref, bf16[1280,256]{1,0:T(8,128)(2,1)} %pad_maximum_fusion.8.grad_ref), custom_call_target="tpu_custom_call" | custom-call | flops 1 | bytes 1 | tf_op jit(solution)/shard_map/self_backward/pallas_call | solution.py:241
  517.9 12.0 %collective-permute-done.66 = bf16[256,2048]{1,0:T(8,128)(2,1)S(1)} collective-permute-done((bf16[256,2048]{1,0:T(8,128)(2,1)}, bf16[256,2048]{1,0:T(8,128)(2,1)S(1)}, u32[]{:S(2)}, u32[]{:S(2)}) %collective-permute-start.66) | collective-permute-done | bytes 1048608 | tf_op jit(solution)/shard_map/ppermute | solution.py:575
  540.9 12.1 %weight_grad.8 = bf16[1024,1024]{1,0:T(8,128)(2,1)} custom-call(s32[8]{0:T(128)} %broadcast_xor_fusion.order_ref, bf16[320,1024]{1,0:T(8,128)(2,1)} %copy-done.52, bf16[320,1024]{1,0:T(8,128)(2,1)} %copy-done.75, bf16[320,1024]{1,0:T(8,128)(2,1)} %copy-done.76, bf16[320,1024]{1,0:T(8,128)(2,1)} %copy-done.77, bf16[320,1024]{1,0:T(8,128)(2,1)} %copy-done.55, ...), custom_call_target="tpu_custom_call" | custom-call | flops 1 | bytes 1 | tf_op jit(solution)/shard_map/weight_grad/pallas_call | solution.py:465
  559.2 8.0 collective-permute-done.70
  570.6 8.0 feed_backward.6
  608.0 16.3 %weight_grad.9 = bf16[1024,2048]{1,0:T(8,128)(2,1)} custom-call(s32[8]{0:T(128)} %broadcast_xor_fusion.order_ref, bf16[320,1024]{1,0:T(8,128)(2,1)} %copy-done.33, bf16[320,1024]{1,0:T(8,128)(2,1)} %copy-done.46, bf16[320,1024]{1,0:T(8,128)(2,1)} %copy-done.47, bf16[320,1024]{1,0:T(8,128)(2,1)} %copy-done.48, ...), custom_call_target="tpu_custom_call" | custom-call | flops 1 | bytes 1 | tf_op jit(solution)/shard_map/weight_grad/pallas_call | solution.py:465
  629.5 10.7 %collective-permute-done.77 = bf16[512,2048]{1,0:T(8,128)(2,1)} collective-permute-done((bf16[512,2048]{1,0:T(8,128)(2,1)}, bf16[512,2048]{1,0:T(8,128)(2,1)}, u32[]{:S(2)}, u32[]{:S(2)}) %collective-permute-start.77) | collective-permute-done | bytes 2097184 | tf_op jit(solution)/shard_map/ppermute | solution.py:575
  649.2 8.4 cross_backward.3
  665.3 8.2 collective-permute-done.78
  673.5 11.2 %collective-permute-done.79 = bf16[512,2048]{1,0:T(8,128)(2,1)} collective-permute-done((bf16[512,2048]{1,0:T(8,128)(2,1)}, bf16[512,2048]{1,0:T(8,128)(2,1)}, u32[]{:S(2)}, u32[]{:S(2)}) %collective-permute-start.79) | collective-permute-done | bytes 2097184 | tf_op jit(solution)/shard_map/ppermute | solution.py:575
  686.4 9.0 %weight_grad.10 = bf16[4,1024,512]{2,1,0:T(8,128)(2,1)} custom-call(s32[8]{0:T(128)} %broadcast_xor_fusion.order_ref, bf16[320,1024]{1,0:T(8,128)(2,1)} %copy-done.56, bf16[320,1024]{1,0:T(8,128)(2,1)} %copy-done.58, bf16[320,1024]{1,0:T(8,128)(2,1)} %get-tuple-element.309.refs_2_, bf16[320,1024]{1,0:T(8,128)(2,1)} %get-tuple-element.228.refs_3_), custom_call_target="tpu_custom_call" | custom-call | flops 1 | bytes 1 | tf_op jit(solution)/shard_map/weight_grad/pallas_call | solution.py:465
  714.9 11.4 %self_backward.3 = (bf16[1280,768]{1,0:T(8,128)(2,1)}, f32[4,256,256]{2,1,0:T(8,128)}) custom-call(s32[1]{0:T(128)} %bitcast.2.position_ref, bf16[1280,768]{1,0:T(8,128)(2,1)} %pad_maximum_fusion.5.qkv_ref, bf16[5,4,256,256]{3,2,1,0:T(8,128)(2,1)} %get-tuple-element.312.probs_ref, bf16[1280,256]{1,0:T(8,128)(2,1)} %pad_maximum_fusion.9.grad_ref), custom_call_target="tpu_custom_call" | custom-call | flops 1 | bytes 1 | tf_op jit(solution)/shard_map/self_backward/pallas_call | solution.py:241
  726.3 15.0 %collective-permute-done.88 = bf16[128,2048]{1,0:T(8,128)(2,1)} collective-permute-done((bf16[128,2048]{1,0:T(8,128)(2,1)S(1)}, bf16[128,2048]{1,0:T(8,128)(2,1)}, u32[]{:S(2)}, u32[]{:S(2)}) %collective-permute-start.88) | collective-permute-done | bytes 524320 | tf_op jit(solution)/shard_map/ppermute | solution.py:575
  761.9 11.8 %weight_grad.11 = bf16[1024,1024]{1,0:T(8,128)(2,1)} custom-call(s32[8]{0:T(128)} %broadcast_xor_fusion.order_ref, bf16[320,1024]{1,0:T(8,128)(2,1)} %copy-done.51, bf16[320,1024]{1,0:T(8,128)(2,1)} %copy-done.74, bf16[320,1024]{1,0:T(8,128)(2,1)} %collective-permute-done.10.refs_2_, bf16[320,1024]{1,0:T(8,128)(2,1)} %collective-permute-done.11.refs_3_, ...), custom_call_target="tpu_custom_call" | custom-call | flops 1 | bytes 1 | tf_op jit(solution)/shard_map/weight_grad/pallas_call | solution.py:465
  807.9 16.7 %shard_map.646 = f32[128,64]{1,0:T(8,128)} custom-call(f32[4,320,320]{2,1,0:T(8,128)} %get-tuple-element.374.sum_ref, s32[320,320]{1,0:T(8,128)} %index_ref.5), custom_call_target="tpu_custom_call" | custom-call | flops 1 | bytes 1 | tf_op jit(solution)/shard_map/pallas_call | solution.py:119
  824.6 9.1 %shard_map.645 = f32[64,64]{1,0:T(8,128)} custom-call(f32[4,256,256]{2,1,0:T(8,128)} %get-tuple-element.373.sum_ref, s32[256,256]{1,0:T(8,128)} %index_ref.4), custom_call_target="tpu_custom_call" | custom-call | flops 1 | bytes 1 | tf_op jit(solution)/shard_map/pallas_call | solution.py:119
  870.4 8.2 collective-permute-done.103
  (859 shorter events, 492.9 us)
Async XLA Ops:
  77.3 27.3 %collective-permute-start.12 = (bf16[1,1,128,2048]{3,2,1,0:T(8,128)(2,1)S(1)}, bf16[1,1,128,2048]{3,2,1,0:T(8,128)(2,1)}, u32[]{:S(2)}, u32[]{:S(2)}) collective-permute-start(bf16[1,1,128,2048]{3,2,1,0:T(8,128)(2,1)S(1)} %bitcast.246), channel_id=1, source_target_pairs={{0,16},{4,20},{8,24},{12,28},{16,0},{20,4},{24,8},{28,12},{1,17},{... | collective-permute-start | bytes 1572872 | tf_op jit(solution)/shard_map/ppermute | solution.py:575
  82.6 43.3 %collective-permute-start.17 = (bf16[4,1,128,1536]{3,2,1,0:T(8,128)(2,1)S(1)}, bf16[4,1,128,1536]{3,2,1,0:T(8,128)(2,1)}, u32[]{:S(2)}, u32[]{:S(2)}) collective-permute-start(bf16[4,1,128,1536]{3,2,1,0:T(8,128)(2,1)S(1)} %bitcast.236), channel_id=1, source_target_pairs={{0,4},{4,0},{8,12},{12,8},{16,20},{20,16},{24,28},{28,24},{1,5},{5... | collective-permute-start | bytes 4718600 | tf_op jit(solution)/shard_map/ppermute | solution.py:575
  139.6 47.9 %collective-permute-start.24 = (bf16[4,1,128,2048]{3,2,1,0:T(8,128)(2,1)}, bf16[4,1,128,2048]{3,2,1,0:T(8,128)(2,1)}, u32[]{:S(2)}, u32[]{:S(2)}) collective-permute-start(bf16[4,1,128,2048]{3,2,1,0:T(8,128)(2,1)} %bitcast.36), channel_id=1, source_target_pairs={{0,4},{4,0},{8,12},{12,8},{16,20},{20,16},{24,28},{28,24},{1,5},{5... | collective-permute-start | bytes 6291464 | tf_op jit(solution)/shard_map/ppermute | solution.py:575
  162.8 30.7 %collective-permute-start.23 = (bf16[320,1024]{1,0:T(8,128)(2,1)S(1)}, bf16[320,1024]{1,0:T(8,128)(2,1)S(1)}, u32[]{:S(2)}, u32[]{:S(2)}) collective-permute-start(bf16[320,1024]{1,0:T(8,128)(2,1)S(1)} %add_convert_fusion.16.a_ref.refs_0_), channel_id=1, source_target_pairs={{0,1},{1,0},{2,3},{3,2},{4,5},{5,4},{6,7},{7,6},{8,9},{9,8},{10,11... | collective-permute-start | bytes 1966088 | tf_op jit(solution)/shard_map/ppermute | solution.py:575
  162.9 38.4 %collective-permute-start.26 = (bf16[320,1024]{1,0:T(8,128)(2,1)S(1)}, bf16[320,1024]{1,0:T(8,128)(2,1)S(1)}, u32[]{:S(2)}, u32[]{:S(2)}) collective-permute-start(bf16[320,1024]{1,0:T(8,128)(2,1)S(1)} %add_convert_fusion.16.a_ref.refs_0_), channel_id=1, source_target_pairs={{0,2},{1,3},{2,0},{3,1},{4,6},{5,7},{6,4},{7,5},{8,10},{9,11},{10,... | collective-permute-start | bytes 1966088 | tf_op jit(solution)/shard_map/ppermute | solution.py:575
  164.0 29.4 %collective-permute-start.25 = (bf16[2,1,128,1024]{3,2,1,0:T(8,128)(2,1)S(1)}, bf16[2,1,128,1024]{3,2,1,0:T(8,128)(2,1)S(1)}, u32[]{:S(2)}, u32[]{:S(2)}) collective-permute-start(bf16[2,1,128,1024]{3,2,1,0:T(8,128)(2,1)S(1)} %maximum_select_fusion.18), channel_id=1, source_target_pairs={{0,8},{4,12},{8,0},{12,4},{16,24},{20,28},{24,16},{28,20},{1,9},{5... | collective-permute-start | bytes 1572872 | tf_op jit(solution)/shard_map/ppermute | solution.py:575
  268.4 26.6 %collective-permute-start.37 = (bf16[1,1,128,2048]{3,2,1,0:T(8,128)(2,1)S(1)}, bf16[1,1,128,2048]{3,2,1,0:T(8,128)(2,1)}, u32[]{:S(2)}, u32[]{:S(2)}) collective-permute-start(bf16[1,1,128,2048]{3,2,1,0:T(8,128)(2,1)S(1)} %bitcast.244), channel_id=1, source_target_pairs={{0,16},{4,20},{8,24},{12,28},{16,0},{20,4},{24,8},{28,12},{1,17},{... | collective-permute-start | bytes 1572872 | tf_op jit(solution)/shard_map/ppermute | solution.py:575
  272.9 43.1 %collective-permute-start.42 = (bf16[4,1,128,1536]{3,2,1,0:T(8,128)(2,1)}, bf16[4,1,128,1536]{3,2,1,0:T(8,128)(2,1)}, u32[]{:S(2)}, u32[]{:S(2)}) collective-permute-start(bf16[4,1,128,1536]{3,2,1,0:T(8,128)(2,1)} %bitcast.54), channel_id=1, source_target_pairs={{0,4},{4,0},{8,12},{12,8},{16,20},{20,16},{24,28},{28,24},{1,5},{5... | collective-permute-start | bytes 4718600 | tf_op jit(solution)/shard_map/ppermute | solution.py:575
  332.1 47.9 %collective-permute-start.48 = (bf16[4,1,128,2048]{3,2,1,0:T(8,128)(2,1)}, bf16[4,1,128,2048]{3,2,1,0:T(8,128)(2,1)}, u32[]{:S(2)}, u32[]{:S(2)}) collective-permute-start(bf16[4,1,128,2048]{3,2,1,0:T(8,128)(2,1)} %bitcast.65), channel_id=1, source_target_pairs={{0,4},{4,0},{8,12},{12,8},{16,20},{20,16},{24,28},{28,24},{1,5},{5... | collective-permute-start | bytes 6291464 | tf_op jit(solution)/shard_map/ppermute | solution.py:575
  352.3 41.5 %collective-permute-start.49 = (bf16[320,1024]{1,0:T(8,128)(2,1)S(1)}, bf16[320,1024]{1,0:T(8,128)(2,1)}, u32[]{:S(2)}, u32[]{:S(2)}) collective-permute-start(bf16[320,1024]{1,0:T(8,128)(2,1)S(1)} %add_convert_fusion.11.a_ref.refs_0_), channel_id=1, source_target_pairs={{0,2},{1,3},{2,0},{3,1},{4,6},{5,7},{6,4},{7,5},{8,10},{9,11},{10,... | collective-permute-start | bytes 1966088 | tf_op jit(solution)/shard_map/ppermute | solution.py:575
  352.9 33.1 %collective-permute-start.47 = (bf16[320,1024]{1,0:T(8,128)(2,1)S(1)}, bf16[320,1024]{1,0:T(8,128)(2,1)S(1)}, u32[]{:S(2)}, u32[]{:S(2)}) collective-permute-start(bf16[320,1024]{1,0:T(8,128)(2,1)S(1)} %add_convert_fusion.11.a_ref.refs_0_), channel_id=1, source_target_pairs={{0,1},{1,0},{2,3},{3,2},{4,5},{5,4},{6,7},{7,6},{8,9},{9,8},{10,11... | collective-permute-start | bytes 1966088 | tf_op jit(solution)/shard_map/ppermute | solution.py:575
  354.0 39.9 %collective-permute-start.54 = (bf16[320,1024]{1,0:T(8,128)(2,1)}, bf16[320,1024]{1,0:T(8,128)(2,1)}, u32[]{:S(2)}, u32[]{:S(2)}) collective-permute-start(bf16[320,1024]{1,0:T(8,128)(2,1)} %multiply_convert_fusion.5.a_ref.refs_4_), channel_id=1, source_target_pairs={{0,1},{1,0},{2,3},{3,2},{4,5},{5,4},{6,7},{7,6},{8,9},{9,8},{10,11... | collective-permute-start | bytes 1966088 | tf_op jit(solution)/shard_map/ppermute | solution.py:575
  354.4 47.5 %collective-permute-start.55 = (bf16[320,1024]{1,0:T(8,128)(2,1)}, bf16[320,1024]{1,0:T(8,128)(2,1)}, u32[]{:S(2)}, u32[]{:S(2)}) collective-permute-start(bf16[320,1024]{1,0:T(8,128)(2,1)} %multiply_convert_fusion.5.a_ref.refs_4_), channel_id=1, source_target_pairs={{0,2},{1,3},{2,0},{3,1},{4,6},{5,7},{6,4},{7,5},{8,10},{9,11},{10,... | collective-permute-start | bytes 1966088 | tf_op jit(solution)/shard_map/ppermute | solution.py:575
  425.3 29.0 %collective-permute-start.53 = (bf16[320,1024]{1,0:T(8,128)(2,1)}, bf16[320,1024]{1,0:T(8,128)(2,1)}, u32[]{:S(2)}, u32[]{:S(2)}) collective-permute-start(bf16[320,1024]{1,0:T(8,128)(2,1)} %add_convert_fusion.10), channel_id=1, source_target_pairs={{0,2},{1,3},{2,0},{3,1},{4,6},{5,7},{6,4},{7,5},{8,10},{9,11},{10,... | collective-permute-start | bytes 1966088 | tf_op jit(solution)/shard_map/ppermute | solution.py:575
  426.8 27.5 %collective-permute-start.52 = (bf16[320,1024]{1,0:T(8,128)(2,1)}, bf16[320,1024]{1,0:T(8,128)(2,1)}, u32[]{:S(2)}, u32[]{:S(2)}) collective-permute-start(bf16[320,1024]{1,0:T(8,128)(2,1)} %get-tuple-element.266), channel_id=1, source_target_pairs={{0,1},{1,0},{2,3},{3,2},{4,5},{5,4},{6,7},{7,6},{8,9},{9,8},{10,11... | collective-permute-start | bytes 1966088 | tf_op jit(solution)/shard_map/ppermute | solution.py:575
  446.5 54.1 %collective-permute-start.63 = (bf16[512,2048]{1,0:T(8,128)(2,1)}, bf16[512,2048]{1,0:T(8,128)(2,1)}, u32[]{:S(2)}, u32[]{:S(2)}) collective-permute-start(bf16[512,2048]{1,0:T(8,128)(2,1)} %slice.728), channel_id=1, source_target_pairs={{0,4},{4,0},{8,12},{12,8},{16,20},{20,16},{24,28},{28,24},{1,5},{5... | collective-permute-start | bytes 6291464 | tf_op jit(solution)/shard_map/ppermute | solution.py:575
  504.1 25.8 %collective-permute-start.66 = (bf16[256,2048]{1,0:T(8,128)(2,1)}, bf16[256,2048]{1,0:T(8,128)(2,1)S(1)}, u32[]{:S(2)}, u32[]{:S(2)}) collective-permute-start(bf16[256,2048]{1,0:T(8,128)(2,1)} %slice.732), channel_id=1, source_target_pairs={{0,8},{4,12},{8,0},{12,4},{16,24},{20,28},{24,16},{28,20},{1,9},{5... | collective-permute-start | bytes 3145736 | tf_op jit(solution)/shard_map/ppermute | solution.py:575
  540.9 26.3 %collective-permute-start.70 = (bf16[128,2048]{1,0:T(8,128)(2,1)}, bf16[128,2048]{1,0:T(8,128)(2,1)}, u32[]{:S(2)}, u32[]{:S(2)}) collective-permute-start(bf16[128,2048]{1,0:T(8,128)(2,1)} %slice.734), channel_id=1, source_target_pairs={{0,16},{4,20},{8,24},{12,28},{16,0},{20,4},{24,8},{28,12},{1,17},{... | collective-permute-start | bytes 1572872 | tf_op jit(solution)/shard_map/ppermute | solution.py:575
  591.5 48.8 %collective-permute-start.77 = (bf16[512,2048]{1,0:T(8,128)(2,1)}, bf16[512,2048]{1,0:T(8,128)(2,1)}, u32[]{:S(2)}, u32[]{:S(2)}) collective-permute-start(bf16[512,2048]{1,0:T(8,128)(2,1)} %slice.737), channel_id=1, source_target_pairs={{0,4},{4,0},{8,12},{12,8},{16,20},{20,16},{24,28},{28,24},{1,5},{5... | collective-permute-start | bytes 6291464 | tf_op jit(solution)/shard_map/ppermute | solution.py:575
  627.6 57.0 %collective-permute-start.79 = (bf16[512,2048]{1,0:T(8,128)(2,1)}, bf16[512,2048]{1,0:T(8,128)(2,1)}, u32[]{:S(2)}, u32[]{:S(2)}) collective-permute-start(bf16[512,2048]{1,0:T(8,128)(2,1)} %slice.740), channel_id=1, source_target_pairs={{0,4},{4,0},{8,12},{12,8},{16,20},{20,16},{24,28},{28,24},{1,5},{5... | collective-permute-start | bytes 6291464 | tf_op jit(solution)/shard_map/ppermute | solution.py:575
  661.9 46.1 %collective-permute-start.83 = (bf16[160,512]{1,0:T(8,128)(2,1)}, bf16[160,512]{1,0:T(8,128)(2,1)}, u32[]{:S(2)}, u32[]{:S(2)}) collective-permute-start(bf16[160,512]{1,0:T(8,128)(2,1)} %maximum_maximum_fusion), channel_id=1, source_target_pairs={{0,1},{1,0},{2,3},{3,2},{4,5},{5,4},{6,7},{7,6},{8,9},{9,8},{10,11... | collective-permute-start | bytes 491528 | tf_op jit(solution)/shard_map/ppermute | solution.py:575
  662.6 47.4 %collective-permute-start.84 = (bf16[160,512]{1,0:T(8,128)(2,1)}, bf16[160,512]{1,0:T(8,128)(2,1)}, u32[]{:S(2)}, u32[]{:S(2)}) collective-permute-start(bf16[160,512]{1,0:T(8,128)(2,1)} %maximum_maximum_fusion.1), channel_id=1, source_target_pairs={{0,1},{1,0},{2,3},{3,2},{4,5},{5,4},{6,7},{7,6},{8,9},{9,8},{10,11... | collective-permute-start | bytes 491528 | tf_op jit(solution)/shard_map/ppermute | solution.py:575
  698.4 42.9 %collective-permute-start.85 = (bf16[1024,512]{1,0:T(8,128)(2,1)}, bf16[1024,512]{1,0:T(8,128)(2,1)}, u32[]{:S(2)}, u32[]{:S(2)}) collective-permute-start(bf16[1024,512]{1,0:T(8,128)(2,1)} %get-tuple-element.424), channel_id=1, source_target_pairs={{0,1},{1,0},{2,3},{3,2},{4,5},{5,4},{6,7},{7,6},{8,9},{9,8},{10,11... | collective-permute-start | bytes 3145736 | tf_op jit(solution)/shard_map/ppermute | solution.py:575
  700.4 40.9 %collective-permute-start.86 = (bf16[1024,512]{1,0:T(8,128)(2,1)}, bf16[1024,512]{1,0:T(8,128)(2,1)}, u32[]{:S(2)}, u32[]{:S(2)}) collective-permute-start(bf16[1024,512]{1,0:T(8,128)(2,1)} %get-tuple-element.423), channel_id=1, source_target_pairs={{0,1},{1,0},{2,3},{3,2},{4,5},{5,4},{6,7},{7,6},{8,9},{9,8},{10,11... | collective-permute-start | bytes 3145736 | tf_op jit(solution)/shard_map/ppermute | solution.py:575
  706.7 36.8 %collective-permute-start.89 = (bf16[256,2048]{1,0:T(8,128)(2,1)}, bf16[256,2048]{1,0:T(8,128)(2,1)S(1)}, u32[]{:S(2)}, u32[]{:S(2)}) collective-permute-start(bf16[256,2048]{1,0:T(8,128)(2,1)} %slice.758), channel_id=1, source_target_pairs={{0,8},{4,12},{8,0},{12,4},{16,24},{20,28},{24,16},{28,20},{1,9},{5... | collective-permute-start | bytes 3145736 | tf_op jit(solution)/shard_map/ppermute | solution.py:575
  708.0 33.2 %collective-permute-start.88 = (bf16[128,2048]{1,0:T(8,128)(2,1)S(1)}, bf16[128,2048]{1,0:T(8,128)(2,1)}, u32[]{:S(2)}, u32[]{:S(2)}) collective-permute-start(bf16[128,2048]{1,0:T(8,128)(2,1)S(1)} %slice.756), channel_id=1, source_target_pairs={{0,16},{4,20},{8,24},{12,28},{16,0},{20,4},{24,8},{28,12},{1,17},{... | collective-permute-start | bytes 1572872 | tf_op jit(solution)/shard_map/ppermute | solution.py:575
  711.7 31.8 %collective-permute-start.87 = (bf16[160,512]{1,0:T(8,128)(2,1)}, bf16[160,512]{1,0:T(8,128)(2,1)S(1)}, u32[]{:S(2)}, u32[]{:S(2)}) collective-permute-start(bf16[160,512]{1,0:T(8,128)(2,1)} %add_convert_fusion.24), channel_id=1, source_target_pairs={{0,2},{1,3},{2,0},{3,1},{4,6},{5,7},{6,4},{7,5},{8,10},{9,11},{10,... | collective-permute-start | bytes 491528 | tf_op jit(solution)/shard_map/ppermute | solution.py:575
  752.5 32.1 %collective-permute-start.94 = (bf16[512,1024]{1,0:T(8,128)(2,1)}, bf16[512,1024]{1,0:T(8,128)(2,1)}, u32[]{:S(2)}, u32[]{:S(2)}) collective-permute-start(bf16[512,1024]{1,0:T(8,128)(2,1)} %fusion.20), channel_id=1, source_target_pairs={{0,4},{4,0},{8,12},{12,8},{16,20},{20,16},{24,28},{28,24},{1,5},{5... | collective-permute-start | bytes 3145736 | tf_op jit(solution)/shard_map/ppermute | solution.py:575
  758.4 26.2 %collective-permute-start.96 = (bf16[128,2048]{1,0:T(8,128)(2,1)S(1)}, bf16[128,2048]{1,0:T(8,128)(2,1)S(1)}, u32[]{:S(2)}, u32[]{:S(2)}) collective-permute-start(bf16[128,2048]{1,0:T(8,128)(2,1)S(1)} %slice.770), channel_id=1, source_target_pairs={{0,16},{4,20},{8,24},{12,28},{16,0},{20,4},{24,8},{28,12},{1,17},{... | collective-permute-start | bytes 1572872 | tf_op jit(solution)/shard_map/ppermute | solution.py:575
  777.0 28.4 %collective-permute-start.104 = (bf16[512,1024]{1,0:T(8,128)(2,1)}, bf16[512,1024]{1,0:T(8,128)(2,1)}, u32[]{:S(2)}, u32[]{:S(2)}) collective-permute-start(bf16[512,1024]{1,0:T(8,128)(2,1)} %slice.773), channel_id=1, source_target_pairs={{0,4},{4,0},{8,12},{12,8},{16,20},{20,16},{24,28},{28,24},{1,5},{5... | collective-permute-start | bytes 3145736 | tf_op jit(solution)/shard_map/ppermute | solution.py:575
  804.1 32.3 %collective-permute-start.101 = (f32[4,18,1024]{2,0,1:T(4,128)}, f32[4,18,1024]{2,0,1:T(4,128)S(1)}, u32[]{:S(2)}, u32[]{:S(2)}) collective-permute-start(f32[4,18,1024]{2,0,1:T(4,128)} %broadcast_multiply_fusion), channel_id=1, source_target_pairs={{0,4},{4,0},{8,12},{12,8},{16,20},{20,16},{24,28},{28,24},{1,5},{5... | collective-permute-start | bytes 884744 | tf_op jit(solution)/shard_map/ppermute | solution.py:575
  807.8 54.8 %collective-permute-start.105 = (bf16[256,1024]{1,0:T(8,128)(2,1)}, bf16[256,1024]{1,0:T(8,128)(2,1)}, u32[]{:S(2)}, u32[]{:S(2)}) collective-permute-start(bf16[256,1024]{1,0:T(8,128)(2,1)} %slice.775), channel_id=1, source_target_pairs={{0,8},{4,12},{8,0},{12,4},{16,24},{20,28},{24,16},{28,20},{1,9},{5... | collective-permute-start | bytes 1572872 | tf_op jit(solution)/shard_map/ppermute | solution.py:575
  (273 other events, 2680.7 us)

commit v3 on v2

--- a/solution.py
+++ b/solution.py
@@ -60,7 +60,11 @@
 
 
 VM = pltpu.CompilerParams(vmem_limit_bytes=56 * 1024 * 1024)
-LIGHT = pl.CostEstimate(flops=1, bytes_accessed=1, transcendentals=0)
+
+
+def cost(microseconds):
+    return pl.CostEstimate(flops=int(microseconds * 5e8), bytes_accessed=int(microseconds * 1.5e6), transcendentals=0)
+
 
 def bias_kernel(table_ref, index_ref, out_ref):
     heads, groups, _ = table_ref.shape
@@ -92,7 +96,7 @@
     index = jnp.pad(index, ((0, 0), (0, pad)))
     return pl.pallas_call(bias_kernel,
         out_shape=jax.ShapeDtypeStruct((heads, n, n + pad), jnp.bfloat16),
-        cost_estimate=LIGHT, compiler_params=VM)(table.astype(jnp.float32).reshape(heads, reach // LANES, LANES), index)
+        cost_estimate=cost(6), compiler_params=VM)(table.astype(jnp.float32).reshape(heads, reach // LANES, LANES), index)
 
 LOW=64
 def bucket_kernel(sum_ref, index_ref, out_ref):
@@ -118,7 +122,7 @@
     heads = summed.shape[0]
     out = pl.pallas_call(bucket_kernel,
         out_shape=jax.ShapeDtypeStruct((heads * (reach // LOW), LOW), jnp.float32),
-        cost_estimate=LIGHT, compiler_params=VM)(summed, index)
+        cost_estimate=cost(13), compiler_params=VM)(summed, index)
     return out.reshape(heads, reach)
 QUARTER=64
 NT=(((1,),(1,)),((),()))
@@ -192,7 +196,7 @@
                       pl.BlockSpec(bias.shape, lambda i, p: (0, 0, 0))],
             out_specs=[pl.BlockSpec((rows, width), lambda i, p: (0, 0)),
                        pl.BlockSpec((per, heads, size, size), lambda i, p: (i, 0, 0, 0))]),
-        cost_estimate=LIGHT, compiler_params=VM,
+        cost_estimate=cost(8), compiler_params=VM,
         name="self_forward",
     )(position, qkv, bias)
 
@@ -249,74 +253,83 @@
                       pl.BlockSpec(grad.shape, lambda i, p: (0, 0))],
             out_specs=[pl.BlockSpec(qkv.shape, lambda i, p: (0, 0)),
                        pl.BlockSpec((heads, size, size), lambda i, p: (0, 0, 0))]),
-        cost_estimate=LIGHT, compiler_params=VM,
+        cost_estimate=cost(13), compiler_params=VM,
         name="self_backward",
     )(position, qkv, probs, grad)
 PAD=128
+
+CROSS = 2 * LANES
+
 
 def cross_forward_kernel(q_ref, k_ref, v_ref, bias_ref, out_ref, probs_ref):
     rows = q_ref.shape[0]
     first = lax.broadcasted_iota(jnp.int32, (rows, LANES), 1) < HD
     vfirst = lax.broadcasted_iota(jnp.int32, (PAD, LANES), 1) < HD
     zero = jnp.bfloat16(0)
-    q = q_ref[...] * jnp.bfloat16(HD ** -0.5)
-    total = jnp.zeros((rows, LANES), jnp.float32)
-    for half in range(2):
-        s = dot(jnp.where(first == (half == 0), q, zero), k_ref[...], NT) + bias_ref[...]
-        s = s - jnp.max(s, axis=-1, keepdims=True)
-        e = jnp.exp(s)
-        p = (e * (1.0 / jnp.sum(e, axis=-1, keepdims=True))).astype(jnp.bfloat16)
-        probs_ref[half] = p
-        total = total + dot(p, jnp.where(vfirst == (half == 0), v_ref[...], zero))
-    out_ref[...] = total.astype(jnp.bfloat16)
+    for at in range(0, CROSS, LANES):
+        q = q_ref[:, at : at + LANES] * jnp.bfloat16(HD ** -0.5)
+        v = v_ref[:, at : at + LANES]
+        total = jnp.zeros((rows, LANES), jnp.float32)
+        for half in range(2):
+            s = dot(jnp.where(first == (half == 0), q, zero), k_ref[:, at : at + LANES], NT) + bias_ref[...]
+            s = s - jnp.max(s, axis=-1, keepdims=True)
+            e = jnp.exp(s)
+            p = (e * (1.0 / jnp.sum(e, axis=-1, keepdims=True))).astype(jnp.bfloat16)
+            probs_ref[at // HD + half] = p
+            total = total + dot(p, jnp.where(vfirst == (half == 0), v, zero))
+        out_ref[:, at : at + LANES] = total.astype(jnp.bfloat16)
+
 
 def cross_forward_call(q, k, v, bias):
     rows, width = q.shape
-    pairs = width // LANES
+    pairs = width // CROSS
     col = lambda i: (0, i)
     return pl.pallas_call(
         cross_forward_kernel, grid=(pairs,),
-        in_specs=[pl.BlockSpec((rows, LANES), col), pl.BlockSpec((PAD, LANES), col), pl.BlockSpec((PAD, LANES), col),
+        in_specs=[pl.BlockSpec((rows, CROSS), col), pl.BlockSpec((PAD, CROSS), col), pl.BlockSpec((PAD, CROSS), col),
                   pl.BlockSpec((1, PAD), lambda i: (0, 0))],
-        out_specs=[pl.BlockSpec((rows, LANES), col), pl.BlockSpec((2, rows, PAD), lambda i: (i, 0, 0))],
-        out_shape=[jax.ShapeDtypeStruct((rows, width), jnp.bfloat16), jax.ShapeDtypeStruct((2 * pairs, rows, PAD), jnp.bfloat16)],
-        cost_estimate=LIGHT, compiler_params=VM, name="cross_forward")(q, k, v, bias)
+        out_specs=[pl.BlockSpec((rows, CROSS), col), pl.BlockSpec((4, rows, PAD), lambda i: (i, 0, 0))],
+        out_shape=[jax.ShapeDtypeStruct((rows, width), jnp.bfloat16), jax.ShapeDtypeStruct((4 * pairs, rows, PAD), jnp.bfloat16)],
+        cost_estimate=cost(8), compiler_params=VM, name="cross_forward")(q, k, v, bias)
 
 def cross_backward_kernel(q_ref, k_ref, v_ref, probs_ref, grad_ref, dq_ref, dk_ref, dv_ref):
     rows = q_ref.shape[0]
     first = lax.broadcasted_iota(jnp.int32, (rows, LANES), 1) < HD
     kfirst = lax.broadcasted_iota(jnp.int32, (PAD, LANES), 1) < HD
     zero = jnp.bfloat16(0)
-    q = q_ref[...] * jnp.bfloat16(HD ** -0.5)
-    k = k_ref[...] * jnp.bfloat16(HD ** -0.5)
-    dq = jnp.zeros((rows, LANES), jnp.float32)
-    dk = jnp.zeros((PAD, LANES), jnp.float32)
-    dv = jnp.zeros((PAD, LANES), jnp.float32)
-    for half in range(2):
-        mine = first == (half == 0)
-        g = jnp.where(mine, grad_ref[...], zero)
-        p16 = probs_ref[half]
-        p = p16.astype(jnp.float32)
-        dp = dot(g, v_ref[...], NT)
-        ds = (p * (dp - jnp.sum(p * dp, axis=-1, keepdims=True))).astype(jnp.bfloat16)
-        dq = dq + dot(ds, jnp.where(kfirst == (half == 0), k, zero))
-        dk = dk + dot(ds, jnp.where(mine, q, zero), TN)
-        dv = dv + dot(p16, g, TN)
-    dq_ref[...] = dq.astype(jnp.bfloat16)
-    dk_ref[...] = dk
-    dv_ref[...] = dv
+    for at in range(0, CROSS, LANES):
+        q = q_ref[:, at : at + LANES] * jnp.bfloat16(HD ** -0.5)
+        k = k_ref[:, at : at + LANES] * jnp.bfloat16(HD ** -0.5)
+        grad = grad_ref[:, at : at + LANES]
+        dq = jnp.zeros((rows, LANES), jnp.float32)
+        dk = jnp.zeros((PAD, LANES), jnp.float32)
+        dv = jnp.zeros((PAD, LANES), jnp.float32)
+        for half in range(2):
+            mine = first == (half == 0)
+            g = jnp.where(mine, grad, zero)
+            p16 = probs_ref[at // HD + half]
+            p = p16.astype(jnp.float32)
+            dp = dot(g, v_ref[:, at : at + LANES], NT)
+            ds = (p * (dp - jnp.sum(p * dp, axis=-1, keepdims=True))).astype(jnp.bfloat16)
+            dq = dq + dot(ds, jnp.where(kfirst == (half == 0), k, zero))
+            dk = dk + dot(ds, jnp.where(mine, q, zero), TN)
+            dv = dv + dot(p16, g, TN)
+        dq_ref[:, at : at + LANES] = dq.astype(jnp.bfloat16)
+        dk_ref[:, at : at + LANES] = dk
+        dv_ref[:, at : at + LANES] = dv
+
 
 def cross_backward_call(q, k, v, probs, grad):
     rows, width = q.shape
-    pairs = width // LANES
+    pairs = width // CROSS
     col = lambda i: (0, i)
-    tok = pl.BlockSpec((rows, LANES), col); txt = pl.BlockSpec((PAD, LANES), col)
+    tok = pl.BlockSpec((rows, CROSS), col); txt = pl.BlockSpec((PAD, CROSS), col)
     return pl.pallas_call(
         cross_backward_kernel, grid=(pairs,),
-        in_specs=[tok, txt, txt, pl.BlockSpec((2, rows, PAD), lambda i: (i, 0, 0)), tok],
+        in_specs=[tok, txt, txt, pl.BlockSpec((4, rows, PAD), lambda i: (i, 0, 0)), tok],
         out_specs=[tok, txt, txt],
         out_shape=[jax.ShapeDtypeStruct((rows, width), jnp.bfloat16), jax.ShapeDtypeStruct((PAD, width), jnp.float32), jax.ShapeDtypeStruct((PAD, width), jnp.float32)],
-        cost_estimate=LIGHT, compiler_params=VM, name="cross_backward")(q, k, v, probs, grad)
+        cost_estimate=cost(9), compiler_params=VM, name="cross_backward")(q, k, v, probs, grad)
 
 
 def gelu_slope(u):
@@ -361,7 +374,7 @@
             jax.ShapeDtypeStruct((rows, width), jnp.bfloat16),
             jax.ShapeDtypeStruct((rows, width), jnp.bfloat16),
         ],
-        cost_estimate=LIGHT, compiler_params=VM,
+        cost_estimate=cost(7), compiler_params=VM,
         name="feed_forward",
     )(a, b, weights, weights)
 
@@ -392,7 +405,7 @@
             jax.ShapeDtypeStruct((rows, width), jnp.bfloat16),
             jax.ShapeDtypeStruct((rows, width), jnp.bfloat16),
         ],
-        cost_estimate=LIGHT, compiler_params=VM,
+        cost_estimate=cost(8), compiler_params=VM,
         name="feed_backward",
     )(a, b, hidden, weights, weights)
 
@@ -472,7 +485,7 @@
             scratch_shapes=[pltpu.VMEM((width, tokens), jnp.bfloat16)],
         ),
         out_shape=jax.ShapeDtypeStruct(out_shape, jnp.bfloat16),
-        cost_estimate=LIGHT, compiler_params=VM,
+        cost_estimate=cost(12), compiler_params=VM,
         name="weight_grad",
     )(order, *operands)
 
@@ -513,7 +526,7 @@
         in_specs=[layer_block(item.shape) for item in masters],
         out_specs=[layer_block(shape) for shape in shapes],
         out_shape=[jax.ShapeDtypeStruct(shape, jnp.bfloat16) for shape in shapes],
-        cost_estimate=LIGHT, compiler_params=VM,
+        cost_estimate=cost(3), compiler_params=VM,
         name="prepare",
     )(*masters)
 
@@ -565,7 +578,7 @@
         in_specs=in_specs,
         out_specs=out_specs,
         out_shape=out_shape,
-        cost_estimate=LIGHT, compiler_params=VM,
+        cost_estimate=cost(5), compiler_params=VM,
         name="adam",
     )(*operands)
     return [result[4 * n : 4 * n + 4] for n in range(len(states))]
@@ -599,7 +612,7 @@
     far = exchange(crossing, "mp", 2, 4)
     near_part, done = parts[1], None
     if meanwhile is not None:
-        done = meanwhile(crossing)
+        done = meanwhile((crossing, parts[0], parts[1]))
         far = after(far, done)
     near = exchange(after(parts[1], crossing), "mp", 1, 4)
     total = parts[0].astype(jnp.float32) + near.astype(jnp.float32) + far.astype(jnp.float32)
@@ -714,6 +727,30 @@
     return total[:, :width] + got.astype(jnp.float32), total[:, 2 * width :]
 
 
+def summing_rows(rows, size):
+    for bit in (1, 2):
+        got = yield exchange(narrow(rows), "mp", bit, 4)
+        rows = rows + got.astype(jnp.float32)
+    slots = narrow(rows)[None, None]
+    me = lax.axis_index("dp")
+    for n, bit in reversed(list(enumerate(bits_of(size)))[1:]):
+        got = yield exchange(slots, "dp", bit, size)
+        slots = jnp.where(((me >> n) & 1) == 0, jnp.concatenate([slots, got], axis=1), jnp.concatenate([got, slots], axis=1))
+        slots = slots.reshape((slots.shape[0] * 2, 1) + slots.shape[2:])
+    got = yield exchange(slots, "dp", 1, size)
+    return slots.astype(jnp.float32) + got.astype(jnp.float32)
+
+
+def halving_blocks(blocks, size):
+    me = lax.axis_index("dp")
+    for n, bit in enumerate(bits_of(size)):
+        pairs = blocks.reshape((blocks.shape[0] // 2, 2) + blocks.shape[1:])
+        mine = (me >> n) & 1
+        got = yield exchange(lax.dynamic_index_in_dim(pairs, 1 - mine, 1, keepdims=False), "dp", bit, size)
+        blocks = lax.dynamic_index_in_dim(pairs, mine, 1, keepdims=False) + got
+    return blocks[0]
+
+
 def gathering(own, size):
     me = lax.axis_index("dp")
     slots = own[None]
@@ -752,6 +789,7 @@
     reaches = (masters[7].shape[1] * groups, masters[8].shape[1] * groups)
 
     order, ordered = block_order(groups)
+    plain = jnp.arange(D // LANES, dtype=jnp.int32)
 
     block = D // groups
     self_shards, pair_shards, text_shards, feed_shards = prepare_call(masters[:7])
@@ -762,7 +800,16 @@
         rows = slice(layer * block, (layer + 1) * block)
         return [pair_shards[rows], other[rows], text_shards[layer]]
 
+    def gather(pieces):
+        return lax.all_gather(jnp.concatenate(pieces, axis=1), "dp", axis=0, tiled=True)
+
+    split = 4 * wide
     self_flow_0 = Flow(doubling(self_shards[0], groups))
+    first_all = gather(cross_shard(0) + [feed_shards[0]])
+    next_all = gather([self_shards[1]] + cross_shard(1))
+    feed_1 = lax.all_gather(feed_shards[1], "dp", axis=0, tiled=True)
+    cross_ws = (first_all[:, : 6 * wide], next_all[:, split:])
+    feed_ws = (first_all[:, 6 * wide :], feed_1)
 
     position = lax.axis_index("mp").astype(jnp.int32)[None]
     clip_index = lax.axis_index("dp") // 2
@@ -775,7 +822,6 @@
     valid = jnp.maximum(jnp.pad(mask_row, (0, PAD - texts)), (column == 0).astype(jnp.int32)).astype(jnp.float32)
     valid_bias = jnp.where(column < texts, (valid - 1.0) * 1000000000.0, -1e30)[None]
     band_now = lax.dynamic_index_in_dim(band_ids, clip_index, 0, keepdims=False)
-    selector = (jnp.arange(modulation.shape[0], dtype=jnp.int32) == band_now).astype(jnp.float32)
     mod_rows = lax.dynamic_index_in_dim(modulation, band_now, 0, keepdims=False)
     text_columns = lax.dynamic_slice_in_dim(text_embed, lax.axis_index("dp") * (D // groups), D // groups, axis=2)
 
@@ -794,14 +840,9 @@
         record = {"in": latent}
         sending = modulate(latent, mod_rows[base + 1], mod_rows[base])
         if layer == 0:
-            cross_start = tick(jnp.concatenate(cross_shard(0), axis=1), self_flow_0)
-            cross_flow_0 = Flow(doubling(cross_start, groups))
-            biases = tick(biases, self_flow_0, cross_flow_0)
-            feed_start = tick(feed_shards[0], self_flow_0, cross_flow_0)
-            feed_flow_0 = Flow(doubling(feed_start, groups))
-            self_w = after(self_flow_0.finish(), feed_start, biases)
+            self_w = after(self_flow_0.finish(), biases)
         else:
-            self_w = self_flow_1.finish()
+            self_w = next_all[:, :split]
         w_in = self_w[:, : 3 * wide]
         rows, near_qkv = share_rows(sending, lambda one, two: (narrow(mm(one, w_in)), narrow(mm(two, w_in))))
         qkv = jnp.concatenate(near_qkv + tuple(narrow(mm(item, w_in)) for item in rows[2:]), axis=0)
@@ -809,21 +850,12 @@
         w_out = self_w[:, 3 * wide :]
         project = lambda k: narrow(mm(mixed[k * own : (k + 1) * own], w_out, NT))
         p2, p3 = project(2), project(3)
-        p3 = tick(p3, feed_flow_0 if layer == 0 else feed_flow_1)
         branch = collect_parts([project(0), project(1), p2, p3])
-        if layer == 0:
-            branch = tick(branch, feed_flow_0, cross_flow_0)
-            self_flow_1 = Flow(doubling(after(self_shards[1], branch), groups))
-        else:
-            branch = tick(branch, feed_flow_1, cross_flow_1)
         record["self"] = (rows, qkv, probs, mixed, branch)
         latent = latent + mod_rows[base + 2] * branch
         record["mid"] = latent
         normed = modulate(latent, mod_rows[base + 4], mod_rows[base + 3])
-        if layer == 0:
-            cross_w = cross_flow_0.finish()
-        else:
-            cross_w = cross_flow_1.finish()
+        cross_w = cross_ws[layer]
         keyval = share_small(narrow(mm(text_rows, cross_w[:, 4 * wide :])))
         keys = jnp.concatenate([item[:, :wide] for item in keyval], axis=1)
         values = jnp.concatenate([item[:, wide:] for item in keyval], axis=1)
@@ -836,25 +868,14 @@
         branch = mm(mixed, w_cout, NT)
         record["cross"] = (normed, queries, keys, values, probs, mixed, branch, w_cq, w_cout)
         latent = latent + mod_rows[base + 5] * branch
-        if layer == 0:
-            latent = tick(latent, self_flow_1)
         record["late"] = latent
-        if layer == 0:
-            feed_w = tick(feed_flow_0.finish(), self_flow_1)
-            cross_flow_1 = Flow(doubling(after(jnp.concatenate(cross_shard(1), axis=1), feed_w), groups))
-        else:
-            feed_w = feed_flow_1.finish()
+        feed_w = feed_ws[layer]
         weights.append((self_w, feed_w))
         rows, (hidden_near, active_near, p0, p1) = share_rows(
             modulate(latent, mod_rows[base + 7], mod_rows[base + 6]), lambda one, two: feed_forward_call(one, two, feed_w)
         )
         hidden_far, active_far, p2, p3 = feed_forward_call(rows[2], rows[3], feed_w)
-        if layer == 0:
-            p3 = tick(p3, cross_flow_1)
         branch = collect_parts([p0, p1, p2, p3])
-        if layer == 0:
-            branch = tick(branch, cross_flow_1, self_flow_1)
-            feed_flow_1 = Flow(doubling(after(feed_shards[1], branch), groups))
         record["feed"] = (rows, (hidden_near, hidden_far), (active_near, active_far), branch)
         latent = latent + mod_rows[base + 8] * branch
         saved.append(record)
@@ -866,7 +887,6 @@
     for layer in reversed(range(LAYERS)):
         self_w, feed_w = weights[layer]
         last = layer == 0
-        late = None if not last else self_flows[1]
         base = 9 * layer
         record = saved[layer]
         rows, hiddens, actives, branch = record["feed"]
@@ -879,15 +899,16 @@
         grad_input, feed_g = collect_parts(
             [p0, p1, p2, p3],
             lambda sent: weight_grad_call(
-                order,
+                plain,
                 (rows, grads),
                 (((after(dh_near, sent), half, 0), (dh_far, half, 0)), ((actives[0], half, 0), (actives[1], half, 0))),
                 (D, 2 * units),
                 lambda i, o: (0, i),
             ),
         )
-        feed_flows[layer] = Flow(halving(feed_g, groups, ordered))
-        grad_input = tick(grad_input, late)
+        feed_flows[layer] = lax.psum_scatter(feed_g, "dp", scatter_dimension=0, tiled=True)
+        if last:
+            grad_input = after(grad_input, feed_flows[1])
         normed, inverse = layer_norm(record["late"])
         grad_latent, shift_m, scale_m = modulate_back(grad_latent, grad_input, normed, inverse, mod_rows[base + 7])
 
@@ -904,23 +925,23 @@
             )
             for k in range(4)
         ]
+        if last:
+            kv_flow = Flow(
+                collect_then_gather([jnp.concatenate([kv_grads[0][k], kv_grads[1][k]], axis=0) for k in range(4)], groups)
+            )
         grad_input = mm(grad_query, w_cq, NT)
         normed, inverse = layer_norm(record["mid"])
         grad_latent, shift_c, scale_c = modulate_back(grad_latent, grad_input, normed, inverse, mod_rows[base + 4])
         tiles = queries.shape[1] // GRAD_TILE
         if last:
-            kv_flow = Flow(
-                collect_then_gather([jnp.concatenate([kv_grads[0][k], kv_grads[1][k]], axis=0) for k in range(4)], groups)
-            )
-        if last:
-            grad_latent = tick(grad_latent, late, feed_flows[0])
+            grad_latent = tick(grad_latent, kv_flow)
         sending = narrow(mod_rows[base + 2] * grad_latent)
         w_out = self_w[:, 3 * wide :]
         grads, (cross_g, near_mixed) = share_rows(
             sending,
             lambda one, two: (
                 weight_grad_call(
-                    order,
+                    order if last else plain,
                     ((after(hidden, sending),), (grad_rows,)),
                     (((grad_query, own, 0),), ((mixed, own, 0),)),
                     (tiles, D, 2 * GRAD_TILE),
@@ -933,9 +954,9 @@
         gate_a = jnp.sum(grad_latent * branch, axis=0)
         grad_mixed = jnp.concatenate(near_mixed + tuple(narrow(mm(item, w_out)) for item in grads[2:]), axis=0)
         pairing = Flow(pair_up(cross_g))
-        grad_mixed = tick(grad_mixed, kv_flow, None if last else feed_flows[1])
+        grad_mixed = tick(grad_mixed, kv_flow)
         grad_qkv, summed = self_backward_call(layer, position, qkv, probs, grad_mixed)
-        grad_qkv = tick(grad_qkv, pairing, kv_flow, late, feed_flows[layer])
+        grad_qkv = tick(grad_qkv, pairing, kv_flow)
         if last:
             cross_flows[0] = Flow(halve_then_cross(pairing.finish(), groups, ordered, 2 * wide))
         back = lambda k: narrow(mm(grad_qkv[k * own : (k + 1) * own], self_w[:, : 3 * wide], NT))
@@ -943,7 +964,7 @@
         grad_input, self_g = collect_parts(
             [back(0), back(1), p2, p3],
             lambda sent: weight_grad_call(
-                order,
+                order if last else plain,
                 (rows, grads),
                 (((after(grad_qkv, sent), half, 0), (grad_qkv, half, 1)), ((mixed, half, 0), (mixed, half, 1))),
                 (D, 4 * wide),
@@ -953,45 +974,42 @@
         if last:
             self_flows[0] = Flow(halving(self_g, groups, ordered))
         else:
-            both = jnp.concatenate([pairing.finish(), self_g], axis=1)
-            self_flows[1] = Flow(halve_then_cross(both, groups, ordered, 2 * wide))
+            both = jnp.concatenate([pairing.finish(), after(self_g, grad_input)], axis=1)
+            upper = lax.psum_scatter(both, "dp", scatter_dimension=0, tiled=True)
+            from_pair = exchange(upper[:, 2 * wide : 4 * wide], "mp", 2, 4)
+            cross_1 = upper[:, : 2 * wide].astype(jnp.float32) + from_pair.astype(jnp.float32)
+            self_1 = upper[:, 4 * wide :]
         tables_sent[layer] = summed
         if last:
-            grad_input = tick(grad_input, kv_flow, cross_flows[0], late, feed_flows[0])
+            grad_input = tick(grad_input, kv_flow, cross_flows[0])
         normed, inverse = layer_norm(record["in"])
         grad_latent, shift_a, scale_a = modulate_back(grad_latent, grad_input, normed, inverse, mod_rows[base + 1])
         mod_grads[layer] = [shift_a, scale_a, gate_a, shift_c, scale_c, gate_c, shift_m, scale_m, gate_m]
         if last:
-            grad_latent = tick(grad_latent, kv_flow, cross_flows[0])
-        else:
-            grad_latent = tick(grad_latent, feed_flows[1])
+            grad_latent = after(grad_latent, upper)
 
     mod_local = jnp.stack(mod_grads[0] + mod_grads[1], axis=0)
-    for bit in (1, 2):
-        mod_local = mod_local + exchange(mod_local, "mp", bit, 4)
-    grad_modulation = selector[:, None, None] * mod_local[None]
-    for bit in bits_of(groups):
-        grad_modulation = grad_modulation + exchange(grad_modulation, "dp", bit, groups)
-
-    tables_sent = after(tables_sent, grad_latent)
-    table_grads = [bucket_sum(tables_sent[layer], index_tables[layer], reaches[layer]) for layer in range(LAYERS)]
+    mod_local = tick(mod_local, cross_flows[0])
+    mod_flow = Flow(summing_rows(mod_local, groups))
+    table_1 = bucket_sum(after(tables_sent[1], mod_local), index_tables[1], reaches[1])
+    table_1 = tick(table_1, mod_flow, cross_flows[0], self_flows[0], kv_flow)
+    table_0 = bucket_sum(after(tables_sent[0], table_1), index_tables[0], reaches[0])
+    table_0 = tick(table_0, mod_flow, self_flows[0], cross_flows[0])
+    table_grads = [table_0, table_1]
     table_rows = [item.reshape(item.shape[0], groups, -1).swapaxes(0, 1) for item in table_grads]
-    table_rows = jnp.concatenate(table_rows, axis=2)
-    me = lax.axis_index("dp")
-    blocks = table_rows
-    for n, bit in enumerate(bits_of(groups)):
-        pairs = blocks.reshape((blocks.shape[0] // 2, 2) + blocks.shape[1:])
-        mine = (me >> n) & 1
-        keep = lax.dynamic_index_in_dim(pairs, mine, 1, keepdims=False)
-        blocks = keep + exchange(lax.dynamic_index_in_dim(pairs, 1 - mine, 1, keepdims=False), "dp", bit, groups)
-    table_sum = blocks[0]
-
+    table_flow = Flow(halving_blocks(jnp.concatenate(table_rows, axis=2), groups))
     units = masters[5].shape[2]
     state = lambda item: (masters[item], firsts[item], seconds[item])
     updates = [None] * 9
     updates[5], updates[6] = adam_call(
-        ((0, 0, units, None, rates[5]), (0, units, units, "turn", rates[6])), [[flow.finish() for flow in feed_flows]], [state(5), state(6)]
+        ((0, 0, units, None, rates[5]), (0, units, units, "turn", rates[6])), [feed_flows], [state(5), state(6)]
     )
+    updates[5] = tick(updates[5], mod_flow, self_flows[0], cross_flows[0], table_flow)
+    mod_clips = mod_flow.finish()
+    bands = (band_ids[None, :] == jnp.arange(modulation.shape[0], dtype=jnp.int32)[:, None]).astype(jnp.float32)
+    grad_modulation = jnp.sum(bands[:, :, None, None] * mod_clips[None, :, 0], axis=1)
+
+    table_sum = table_flow.finish()
     kv_all = kv_flow.finish()
     kv_sums = []
     for layer in range(LAYERS):
@@ -999,7 +1017,6 @@
         kv_sums.append(
             lax.dot_general(text_columns, grad_kv, (((0, 1), (0, 1)), ((), ())), preferred_element_type=jnp.float32)
         )
-    cross_1, self_1 = self_flows[1].finish()
     cross_sums = [cross_flows[0].finish()[0], cross_1]
     updates[2], updates[3], updates[4] = adam_call(
         ((0, 0, wide, None, rates[2]), (1, 0, 2 * wide, 2, rates[3]), (0, wide, wide, "turn", rates[4])),

time: 899 us -> 769 us (0.86)
  waiting for transfers between devices: 302 us -> 205 us
  other arithmetic: 117 us -> 77.4 us
  starting transfers between devices: 83.6 us -> 65.4 us
  matrix products: 61.1 us -> 76.2 us
  between operations: 5.76 us -> 19.1 us
    ppermute x113 -> x89, waiting for transfers between devices: 302 us -> 198 us  [exchange(): return lax.ppermute(value, axis, [(i, i ^ bit) for i in range(size)])]
    select_n x18 -> x3, other arithmetic: 32.9 us -> 3.55 us  [doubling(): jnp.where(me >> n & 1 == 0, jnp.concatenate([own, got], axis=1), jnp.conc...]
    ppermute x113 -> x89, starting transfers between devices: 83.6 us -> 64.6 us  [exchange(): return lax.ppermute(value, axis, [(i, i ^ bit) for i in range(size)])]
    dot_general x42, matrix products: 59.2 us -> 74.3 us  [mm(): return lax.dot_general(a, b, dims, preferred_element_type=jnp.float32)]
    convert_element_type x28 -> x22, other arithmetic: 30.8 us -> 16.3 us  [narrow(): return value.astype(jnp.bfloat16)]
    slice x14 -> x5, local copies, waits for them, and re-layouts: 16.6 us -> 4.03 us  [halving(): got = (yield exchange(narrow(total[half:]), 'dp', bit, size))]
    unnamed x385 -> x335, local copies, waits for them, and re-layouts: 14.6 us -> 20.4 us
  transfers between devices with their start and end apart: 113 -> 95, of which waited for: 46 -> 40; matrix products, arithmetic and copies ran while one was open for 22% -> 25% of each run, Pallas kernels for 28% -> 33%
where the time goes in v3:
time: 769 us; the launch traced here: 757 us
  Pallas kernels  258 us (34%)
  waiting for transfers between devices  205 us (27%)
  other arithmetic  77.4 us (10%)
  matrix products  76.2 us (10%)
  starting transfers between devices  65.4 us (9%)
  local copies, waits for them, and re-layouts  56.1 us (7%)
  between operations  19.1 us (2%)
    ppermute x89, waiting for transfers between devices, exchange(): return lax.ppermute(value, axis, [(i, i ^ bit) for i in range(size)])  198 us
    pallas_call x6, Pallas kernels, weight_grad_call(): pl.pallas_call(functools.partial(weight_grad_kernel, counts, splits), gri...  75.1 us
    dot_general x42, matrix products, mm(): return lax.dot_general(a, b, dims, preferred_element_type=jnp.float32)  74.3 us
    ppermute x89, starting transfers between devices, exchange(): return lax.ppermute(value, axis, [(i, i ^ bit) for i in range(size)])  64.6 us
    pallas_call x4, Pallas kernels, feed_backward_call(): pl.pallas_call(feed_backward_kernel, grid=(1,), in_specs=[whole, whole, w...  32.9 us
    pallas_call x4, Pallas kernels, feed_forward_call(): pl.pallas_call(feed_forward_kernel, grid=(1,), in_specs=[whole, whole] +...  28.1 us
    pallas_call x2, Pallas kernels, bucket_sum(): pl.pallas_call(bucket_kernel, out_shape=jax.ShapeDtypeStruct((heads * (re...  25.9 us
    pallas_call x2, Pallas kernels, self_backward_call(): pl.pallas_call(functools.partial(self_backward_kernel, kind), out_shape=(...  25 us
  transfers between devices with their start and end apart: 95, of which 40 were waited for; matrix products, arithmetic and copies ran while one was open for 25% of the time, Pallas kernels for 33%

profile of v3, /device:TPU:0, one launch (start us, length us, event | category | flops | bytes accessed | tf_op | source)
XLA Modules:
  0.0 757.2 jit_solution(1627693126507051062)
XLA Ops:
  30.4 9.0 %collective-permute-done = bf16[1,1,128,1024]{3,2,1,0:T(8,128)(2,1)S(1)} collective-permute-done((bf16[1,1,128,1024]{3,2,1,0:T(8,128)(2,1)S(1)}, bf16[1,1,128,1024]{3,2,1,0:T(8,128)(2,1)S(1)}, u32[]{:S(2)}, u32[]{:S(2)}) %collective-permute-start) | collective-permute-done | bytes 262176 | tf_op jit(solution)/shard_map/ppermute | solution.py:588
  39.6 7.6 %collective-permute-start.1 = (bf16[2,1,128,1024]{3,2,1,0:T(8,128)(2,1)S(1)}, bf16[2,1,128,1024]{3,2,1,0:T(8,128)(2,1)}, u32[]{:S(2)}, u32[]{:S(2)}) collective-permute-start(bf16[2,1,128,1024]{3,2,1,0:T(8,128)(2,1)S(1)} %maximum_select_fusion.3), channel_id=1, source_target_pairs={{0,8},{4,12},{8,0},{12,4},{16,24},{20,28},{24,16},{28,20},{1,9},{5... | collective-permute-start | bytes 1572872 | tf_op jit(solution)/shard_map/ppermute | solution.py:588
  51.6 26.1 %collective-permute-done.4 = bf16[2,4,384]{2,0,1:T(2,128)(2,1)S(1)} collective-permute-done((bf16[2,4,384]{2,0,1:T(2,128)(2,1)S(1)}, bf16[2,4,384]{2,0,1:T(2,128)(2,1)S(1)}, u32[]{:S(2)}, u32[]{:S(2)}) %collective-permute-start.4) | collective-permute-done | bytes 6176 | tf_op jit(solution)/shard_map/ppermute | solution.py:588
  88.0 7.9 %shard_map.644.bias_ref = bf16[4,320,384]{2,1,0:T(8,128)(2,1)} custom-call(f32[4,16,128]{2,1,0:T(8,128)} %reshape.604.table_ref, s32[320,384]{1,0:T(8,128)} %pad.12.index_ref), custom_call_target="tpu_custom_call" | custom-call | flops 3000000000 | bytes 9000000 | tf_op jit(solution)/shard_map/pallas_call | solution.py:97
  95.8 32.9 %collective-permute-done.2 = bf16[4,1,128,1024]{3,2,1,0:T(8,128)(2,1)} collective-permute-done((bf16[4,1,128,1024]{3,2,1,0:T(8,128)(2,1)S(1)}, bf16[4,1,128,1024]{3,2,1,0:T(8,128)(2,1)}, u32[]{:S(2)}, u32[]{:S(2)}) %collective-permute-start.2) | collective-permute-done | bytes 1048608 | tf_op jit(solution)/shard_map/ppermute | solution.py:588
  140.6 7.7 %self_forward.2 = (bf16[1280,256]{1,0:T(8,128)(2,1)}, bf16[5,4,256,256]{3,2,1,0:T(8,128)(2,1)}) custom-call(s32[1]{0:T(128)} %bitcast.2.position_ref, bf16[1280,768]{1,0:T(8,128)(2,1)} %pad_maximum_fusion.5.qkv_ref, bf16[4,256,256]{2,1,0:T(8,128)(2,1)} %shard_map.643.bias_ref), custom_call_target="tpu_custom_call" | custom-call | flops 4000000000 | bytes 12000000 | tf_op jit(solution)/shard_map/self_forward/pallas_call | solution.py:189
  157.1 13.3 %collective-permute-done.11 = bf16[320,1024]{1,0:T(8,128)(2,1)S(1)} collective-permute-done((bf16[320,1024]{1,0:T(8,128)(2,1)}, bf16[320,1024]{1,0:T(8,128)(2,1)S(1)}, u32[]{:S(2)}, u32[]{:S(2)}) %collective-permute-start.11) | collective-permute-done | bytes 655392 | tf_op jit(solution)/shard_map/ppermute | solution.py:588
  205.4 7.1 feed_forward.4
  220.4 7.1 feed_forward.5
  232.6 15.4 %collective-permute-done.22 = bf16[320,1024]{1,0:T(8,128)(2,1)S(1)} collective-permute-done((bf16[320,1024]{1,0:T(8,128)(2,1)S(1)}, bf16[320,1024]{1,0:T(8,128)(2,1)S(1)}, u32[]{:S(2)}, u32[]{:S(2)}) %collective-permute-start.22) | collective-permute-done | bytes 655392 | tf_op jit(solution)/shard_map/ppermute | solution.py:588
  276.1 8.1 %self_forward.3 = (bf16[1280,256]{1,0:T(8,128)(2,1)}, bf16[4,4,320,320]{3,2,1,0:T(8,128)(2,1)}) custom-call(s32[1]{0:T(128)} %bitcast.2.position_ref, bf16[1280,768]{1,0:T(8,128)(2,1)} %pad_maximum_fusion.6.qkv_ref, bf16[4,320,384]{2,1,0:T(8,128)(2,1)} %shard_map.644.bias_ref), custom_call_target="tpu_custom_call" | custom-call | flops 4000000000 | bytes 12000000 | tf_op jit(solution)/shard_map/self_forward/pallas_call | solution.py:189
  293.6 13.0 %collective-permute-done.28 = bf16[320,1024]{1,0:T(8,128)(2,1)S(1)} collective-permute-done((bf16[320,1024]{1,0:T(8,128)(2,1)S(1)}, bf16[320,1024]{1,0:T(8,128)(2,1)S(1)}, u32[]{:S(2)}, u32[]{:S(2)}) %collective-permute-start.28) | collective-permute-done | bytes 655392 | tf_op jit(solution)/shard_map/ppermute | solution.py:588
  330.2 7.0 feed_forward.6
  341.2 8.0 %feed_backward.4 = (bf16[640,1024]{1,0:T(8,128)(2,1)}, bf16[320,1024]{1,0:T(8,128)(2,1)}, bf16[320,1024]{1,0:T(8,128)(2,1)}) custom-call(bf16[320,1024]{1,0:T(8,128)(2,1)} %multiply_convert_fusion.5.a_ref.refs_4_, bf16[320,1024]{1,0:T(8,128)(2,1)} %collective-permute-done.39.b_ref.refs_5_, bf16[640,1024]{1,0:T(8,128)(2,1)} %get-tuple-element.205.hidden_ref, ...), custom_call_target="tpu_custom_call" | custom-call | flops 4000000000 | bytes 12000000 | tf_op jit(solution)/shard_map/feed_backward/pallas_call | solution.py:398
  355.7 7.0 feed_forward.7
  363.5 8.5 %feed_backward.5 = (bf16[640,1024]{1,0:T(8,128)(2,1)}, bf16[320,1024]{1,0:T(8,128)(2,1)}, bf16[320,1024]{1,0:T(8,128)(2,1)}) custom-call(bf16[320,1024]{1,0:T(8,128)(2,1)} %collective-permute-done.40.a_ref.refs_6_, bf16[320,1024]{1,0:T(8,128)(2,1)} %copy-done.155, bf16[640,1024]{1,0:T(8,128)(2,1)} %get-tuple-element.215.hidden_ref, ...), custom_call_target="tpu_custom_call" | custom-call | flops 4000000000 | bytes 12000000 | tf_op jit(solution)/shard_map/feed_backward/pallas_call | solution.py:398
  380.7 16.2 %weight_grad.6 = bf16[1024,2048]{1,0:T(8,128)(2,1)} custom-call(s32[8]{0:T(128)} %iota.24.order_ref, bf16[320,1024]{1,0:T(8,128)(2,1)} %add_convert_fusion.5.a_ref.refs_0_, bf16[320,1024]{1,0:T(8,128)(2,1)} %collective-permute-done.33.b_ref.refs_1_, bf16[320,1024]{1,0:T(8,128)(2,1)} %collective-permute-done.34.a_ref.refs_2_, bf16[320,1024]{1,0:T(8,128)(2,1)} %copy-done.153, ...), custom_call_target="tpu_custom_call" | custom-call | flops 6000000000 | bytes 18000000 | tf_op jit(solution)/shard_map/weight_grad/pallas_call | solution.py:478
  400.5 7.7 %collective-permute-done.38 = bf16[320,1024]{1,0:T(8,128)(2,1)} collective-permute-done((bf16[320,1024]{1,0:T(8,128)(2,1)}, bf16[320,1024]{1,0:T(8,128)(2,1)}, u32[]{:S(2)}, u32[]{:S(2)}) %collective-permute-start.38) | collective-permute-done | bytes 655392 | tf_op jit(solution)/shard_map/ppermute | solution.py:588
  416.4 6.9 cross_backward.2
  430.0 9.1 %weight_grad.7 = bf16[4,1024,512]{2,1,0:T(8,128)(2,1)} custom-call(s32[8]{0:T(128)} %iota.25.order_ref, bf16[320,1024]{1,0:T(8,128)(2,1)} %copy-done.40, bf16[320,1024]{1,0:T(8,128)(2,1)} %copy-done.45, bf16[320,1024]{1,0:T(8,128)(2,1)} %get-tuple-element.224.refs_2_, bf16[320,1024]{1,0:T(8,128)(2,1)} %get-tuple-element.202.refs_3_), custom_call_target="tpu_custom_call" | custom-call | flops 6000000000 | bytes 18000000 | tf_op jit(solution)/shard_map/weight_grad/pallas_call | solution.py:478
  451.0 13.8 %self_backward.2 = (bf16[1280,768]{1,0:T(8,128)(2,1)}, f32[4,320,320]{2,1,0:T(8,128)}) custom-call(s32[1]{0:T(128)} %bitcast.2.position_ref, bf16[1280,768]{1,0:T(8,128)(2,1)} %pad_maximum_fusion.6.qkv_ref, bf16[4,4,320,320]{3,2,1,0:T(8,128)(2,1)} %get-tuple-element.225.probs_ref, bf16[1280,256]{1,0:T(8,128)(2,1)} %pad_maximum_fusion.10.grad_ref), custom_call_target="tpu_custom_call" | custom-call | flops 6499999744 | bytes 19500000 | tf_op jit(solution)/shard_map/self_backward/pallas_call | solution.py:245
  478.3 11.8 %weight_grad.8 = bf16[1024,1024]{1,0:T(8,128)(2,1)} custom-call(s32[8]{0:T(128)} %iota.26.order_ref, bf16[320,1024]{1,0:T(8,128)(2,1)} %add_convert_fusion.8.refs_0_, bf16[320,1024]{1,0:T(8,128)(2,1)} %collective-permute-done.23.refs_1_, bf16[320,1024]{1,0:T(8,128)(2,1)} %collective-permute-done.24.refs_2_, bf16[320,1024]{1,0:T(8,128)(2,1)} %copy-done.147, ...), custom_call_target="tpu_custom_call" | custom-call | flops 6000000000 | bytes 18000000 | tf_op jit(solution)/shard_map/weight_grad/pallas_call | solution.py:478
  505.9 8.0 %feed_backward.6 = (bf16[640,1024]{1,0:T(8,128)(2,1)}, bf16[320,1024]{1,0:T(8,128)(2,1)}, bf16[320,1024]{1,0:T(8,128)(2,1)}) custom-call(bf16[320,1024]{1,0:T(8,128)(2,1)} %copy-done.42, bf16[320,1024]{1,0:T(8,128)(2,1)} %copy-done.149, bf16[640,1024]{1,0:T(8,128)(2,1)} %get-tuple-element.193.hidden_ref, bf16[1024,2048]{1,0:T(8,128)(2,1)} %slice.651.up_ref.down_ref, ...), custom_call_target="tpu_custom_call" | custom-call | flops 4000000000 | bytes 12000000 | tf_op jit(solution)/shard_map/feed_backward/pallas_call | solution.py:398
  523.4 8.3 %feed_backward.7 = (bf16[640,1024]{1,0:T(8,128)(2,1)}, bf16[320,1024]{1,0:T(8,128)(2,1)}, bf16[320,1024]{1,0:T(8,128)(2,1)}) custom-call(bf16[320,1024]{1,0:T(8,128)(2,1)} %collective-permute-done.54.a_ref.refs_6_, bf16[320,1024]{1,0:T(8,128)(2,1)} %copy-done.151, bf16[640,1024]{1,0:T(8,128)(2,1)} %get-tuple-element.237.hidden_ref, ...), custom_call_target="tpu_custom_call" | custom-call | flops 4000000000 | bytes 12000000 | tf_op jit(solution)/shard_map/feed_backward/pallas_call | solution.py:398
  537.8 16.5 %weight_grad.9 = bf16[1024,2048]{1,0:T(8,128)(2,1)} custom-call(s32[8]{0:T(128)} %iota.27.order_ref, bf16[320,1024]{1,0:T(8,128)(2,1)} %copy-done.38, bf16[320,1024]{1,0:T(8,128)(2,1)} %copy-done.144, bf16[320,1024]{1,0:T(8,128)(2,1)} %copy-done.145, bf16[320,1024]{1,0:T(8,128)(2,1)} %copy-done.146, bf16[320,1024]{1,0:T(8,128)(2,1)} %copy-done.42, ...), custom_call_target="tpu_custom_call" | custom-call | flops 6000000000 | bytes 18000000 | tf_op jit(solution)/shard_map/weight_grad/pallas_call | solution.py:478
  577.4 9.4 %weight_grad.10 = bf16[4,1024,512]{2,1,0:T(8,128)(2,1)} custom-call(s32[8]{0:T(128)} %broadcast_xor_fusion.order_ref, bf16[320,1024]{1,0:T(8,128)(2,1)} %copy-done.37, bf16[320,1024]{1,0:T(8,128)(2,1)} %copy-done.44, bf16[320,1024]{1,0:T(8,128)(2,1)} %get-tuple-element.247.refs_2_, bf16[320,1024]{1,0:T(8,128)(2,1)} %get-tuple-element.190.refs_3_), custom_call_target="tpu_custom_call" | custom-call | flops 6000000000 | bytes 18000000 | tf_op jit(solution)/shard_map/weight_grad/pallas_call | solution.py:478
  602.5 11.2 %self_backward.3 = (bf16[1280,768]{1,0:T(8,128)(2,1)}, f32[4,256,256]{2,1,0:T(8,128)}) custom-call(s32[1]{0:T(128)} %bitcast.2.position_ref, bf16[1280,768]{1,0:T(8,128)(2,1)} %pad_maximum_fusion.5.qkv_ref, bf16[5,4,256,256]{3,2,1,0:T(8,128)(2,1)} %get-tuple-element.253.probs_ref, bf16[1280,256]{1,0:T(8,128)(2,1)} %pad_maximum_fusion.11.grad_ref), custom_call_target="tpu_custom_call" | custom-call | flops 6499999744 | bytes 19500000 | tf_op jit(solution)/shard_map/self_backward/pallas_call | solution.py:245
  623.3 12.0 %weight_grad.11 = bf16[1024,1024]{1,0:T(8,128)(2,1)} custom-call(s32[8]{0:T(128)} %broadcast_xor_fusion.order_ref, bf16[320,1024]{1,0:T(8,128)(2,1)} %add_convert_fusion.13.refs_0_, bf16[320,1024]{1,0:T(8,128)(2,1)} %collective-permute-done.6.refs_1_, bf16[320,1024]{1,0:T(8,128)(2,1)} %collective-permute-done.7.refs_2_, ...), custom_call_target="tpu_custom_call" | custom-call | flops 6000000000 | bytes 18000000 | tf_op jit(solution)/shard_map/weight_grad/pallas_call | solution.py:478
  669.9 16.8 %shard_map.645 = f32[128,64]{1,0:T(8,128)} custom-call(f32[4,320,320]{2,1,0:T(8,128)} %get-tuple-element.276.sum_ref, s32[320,320]{1,0:T(8,128)} %index_ref.4), custom_call_target="tpu_custom_call" | custom-call | flops 6499999744 | bytes 19500000 | tf_op jit(solution)/shard_map/pallas_call | solution.py:123
  687.7 7.1 collective-permute-done.75
  703.3 9.1 %shard_map.646 = f32[64,64]{1,0:T(8,128)} custom-call(f32[4,256,256]{2,1,0:T(8,128)} %get-tuple-element.282.sum_ref, s32[256,256]{1,0:T(8,128)} %index_ref.5), custom_call_target="tpu_custom_call" | custom-call | flops 6499999744 | bytes 19500000 | tf_op jit(solution)/shard_map/pallas_call | solution.py:123
  723.8 7.2 adam.3
  (748 shorter events, 381.3 us)
Async XLA Ops:
  7.2 167.6 %all-gather.5.cloned.1.call-start = ((), (), s32[]{:S(2)}) async-start(), calls=%async_computation.3 | async-start | bytes 8257536 | tf_op jit(solution)/shard_map/all_gather | solution.py:804
  21.9 234.0 %all-gather.7.cloned.1.call-start = ((), (), s32[]{:S(2)}) async-start(), calls=%async_computation.4 | async-start | bytes 5898240 | tf_op jit(solution)/shard_map/all_gather | solution.py:804
  25.8 23.0 %collective-permute-start.3 = (bf16[1,4,384]{2,0,1:T(2,128)(2,1)S(1)}, bf16[1,4,384]{2,0,1:T(2,128)(2,1)S(1)}, u32[]{:S(2)}, u32[]{:S(2)}) collective-permute-start(bf16[1,4,384]{2,0,1:T(2,128)(2,1)S(1)} %copy.101), channel_id=1, source_target_pairs={{0,4},{4,0},{8,12},{12,8},{16,20},{20,16},{24,28},{28,24},{1,5},{5... | collective-permute-start | bytes 9224 | tf_op jit(solution)/shard_map/ppermute | solution.py:588
  39.6 40.0 %collective-permute-start.1 = (bf16[2,1,128,1024]{3,2,1,0:T(8,128)(2,1)S(1)}, bf16[2,1,128,1024]{3,2,1,0:T(8,128)(2,1)}, u32[]{:S(2)}, u32[]{:S(2)}) collective-permute-start(bf16[2,1,128,1024]{3,2,1,0:T(8,128)(2,1)S(1)} %maximum_select_fusion.3), channel_id=1, source_target_pairs={{0,8},{4,12},{8,0},{12,4},{16,24},{20,28},{24,16},{28,20},{1,9},{5... | collective-permute-start | bytes 1572872 | tf_op jit(solution)/shard_map/ppermute | solution.py:588
  48.8 29.0 %collective-permute-start.4 = (bf16[2,4,384]{2,0,1:T(2,128)(2,1)S(1)}, bf16[2,4,384]{2,0,1:T(2,128)(2,1)S(1)}, u32[]{:S(2)}, u32[]{:S(2)}) collective-permute-start(bf16[2,4,384]{2,0,1:T(2,128)(2,1)S(1)} %broadcast_select_fusion), channel_id=1, source_target_pairs={{0,8},{4,12},{8,0},{12,4},{16,24},{20,28},{24,16},{28,20},{1,9},{5... | collective-permute-start | bytes 18440 | tf_op jit(solution)/shard_map/ppermute | solution.py:588
  50.1 84.7 %collective-permute-start.7 = (bf16[320,1024]{1,0:T(8,128)(2,1)}, bf16[320,1024]{1,0:T(8,128)(2,1)}, u32[]{:S(2)}, u32[]{:S(2)}) collective-permute-start(bf16[320,1024]{1,0:T(8,128)(2,1)} %add_convert_fusion.13.refs_0_), channel_id=1, source_target_pairs={{0,2},{1,3},{2,0},{3,1},{4,6},{5,7},{6,4},{7,5},{8,10},{9,11},{10,... | collective-permute-start | bytes 1966088 | tf_op jit(solution)/shard_map/ppermute | solution.py:588
  50.8 82.2 %collective-permute-start.6 = (bf16[320,1024]{1,0:T(8,128)(2,1)}, bf16[320,1024]{1,0:T(8,128)(2,1)}, u32[]{:S(2)}, u32[]{:S(2)}) collective-permute-start(bf16[320,1024]{1,0:T(8,128)(2,1)} %add_convert_fusion.13.refs_0_), channel_id=1, source_target_pairs={{0,1},{1,0},{2,3},{3,2},{4,5},{5,4},{6,7},{7,6},{8,9},{9,8},{10,11... | collective-permute-start | bytes 1966088 | tf_op jit(solution)/shard_map/ppermute | solution.py:588
  81.0 47.7 %collective-permute-start.2 = (bf16[4,1,128,1024]{3,2,1,0:T(8,128)(2,1)S(1)}, bf16[4,1,128,1024]{3,2,1,0:T(8,128)(2,1)}, u32[]{:S(2)}, u32[]{:S(2)}) collective-permute-start(bf16[4,1,128,1024]{3,2,1,0:T(8,128)(2,1)S(1)} %bitcast.186), channel_id=1, source_target_pairs={{0,4},{4,0},{8,12},{12,8},{16,20},{20,16},{24,28},{28,24},{1,5},{5... | collective-permute-start | bytes 3145736 | tf_op jit(solution)/shard_map/ppermute | solution.py:588
  157.0 173.2 %all-gather.9.cloned.1.call-start = ((), (), s32[]{:S(2)}) async-start(), calls=%async_computation.8 | async-start | bytes 4718592 | tf_op jit(solution)/shard_map/all_gather | solution.py:810
  250.9 306.1 %reduce-scatter.4.cloned.1.call-start = ((), (), s32[]{:S(2)}) async-start(), calls=%async_computation.5 | async-start | bytes 4718592 | tf_op jit(solution)/shard_map/reduce_scatter | solution.py:909
  251.1 17.9 %collective-permute-start.24 = (bf16[320,1024]{1,0:T(8,128)(2,1)}, bf16[320,1024]{1,0:T(8,128)(2,1)}, u32[]{:S(2)}, u32[]{:S(2)}) collective-permute-start(bf16[320,1024]{1,0:T(8,128)(2,1)} %add_convert_fusion.8.refs_0_), channel_id=1, source_target_pairs={{0,2},{1,3},{2,0},{3,1},{4,6},{5,7},{6,4},{7,5},{8,10},{9,11},{10,... | collective-permute-start | bytes 1966088 | tf_op jit(solution)/shard_map/ppermute | solution.py:588
  259.2 27.2 %collective-permute-start.30 = (bf16[128,512]{1,0:T(8,128)(2,1)S(1)}, bf16[128,512]{1,0:T(8,128)(2,1)S(1)}, u32[]{:S(2)}, u32[]{:S(2)}) collective-permute-start(bf16[128,512]{1,0:T(8,128)(2,1)S(1)} %convolution_convert_fusion.36), channel_id=1, source_target_pairs={{0,1},{1,0},{2,3},{3,2},{4,5},{5,4},{6,7},{7,6},{8,9},{9,8},{10,11... | collective-permute-start | bytes 393224 | tf_op jit(solution)/shard_map/ppermute | solution.py:588
  262.3 30.1 %collective-permute-start.29 = (bf16[1024,1024]{1,0:T(8,128)(2,1)}, bf16[1024,1024]{1,0:T(8,128)(2,1)S(1)}, u32[]{:S(2)}, u32[]{:S(2)}) collective-permute-start(bf16[1024,1024]{1,0:T(8,128)(2,1)} %slice.656), channel_id=1, source_target_pairs={{0,1},{1,0},{2,3},{3,2},{4,5},{5,4},{6,7},{7,6},{8,9},{9,8},{10,11... | collective-permute-start | bytes 6291464 | tf_op jit(solution)/shard_map/ppermute | solution.py:588
  271.4 19.6 %collective-permute-start.32 = (bf16[128,512]{1,0:T(8,128)(2,1)S(1)}, bf16[128,512]{1,0:T(8,128)(2,1)S(1)}, u32[]{:S(2)}, u32[]{:S(2)}) collective-permute-start(bf16[128,512]{1,0:T(8,128)(2,1)S(1)} %collective-permute-done.31), channel_id=1, source_target_pairs={{0,1},{1,0},{2,3},{3,2},{4,5},{5,4},{6,7},{7,6},{8,9},{9,8},{10,11... | collective-permute-start | bytes 393224 | tf_op jit(solution)/shard_map/ppermute | solution.py:588
  325.8 29.0 %collective-permute-start.40 = (bf16[320,1024]{1,0:T(8,128)(2,1)}, bf16[320,1024]{1,0:T(8,128)(2,1)}, u32[]{:S(2)}, u32[]{:S(2)}) collective-permute-start(bf16[320,1024]{1,0:T(8,128)(2,1)} %multiply_convert_fusion.5.a_ref.refs_4_), channel_id=1, source_target_pairs={{0,2},{1,3},{2,0},{3,1},{4,6},{5,7},{6,4},{7,5},{8,10},{9,11},{10,... | collective-permute-start | bytes 1966088 | tf_op jit(solution)/shard_map/ppermute | solution.py:588
  376.8 20.2 %collective-permute-start.44 = (bf16[320,1024]{1,0:T(8,128)(2,1)}, bf16[320,1024]{1,0:T(8,128)(2,1)}, u32[]{:S(2)}, u32[]{:S(2)}) collective-permute-start(bf16[320,1024]{1,0:T(8,128)(2,1)} %add_convert_fusion.3), channel_id=1, source_target_pairs={{0,2},{1,3},{2,0},{3,1},{4,6},{5,7},{6,4},{7,5},{8,10},{9,11},{10,... | collective-permute-start | bytes 1966088 | tf_op jit(solution)/shard_map/ppermute | solution.py:588
  378.1 18.9 %collective-permute-start.43 = (bf16[320,1024]{1,0:T(8,128)(2,1)}, bf16[320,1024]{1,0:T(8,128)(2,1)}, u32[]{:S(2)}, u32[]{:S(2)}) collective-permute-start(bf16[320,1024]{1,0:T(8,128)(2,1)} %get-tuple-element.218), channel_id=1, source_target_pairs={{0,1},{1,0},{2,3},{3,2},{4,5},{5,4},{6,7},{7,6},{8,9},{9,8},{10,11... | collective-permute-start | bytes 1966088 | tf_op jit(solution)/shard_map/ppermute | solution.py:588
  379.3 28.9 %collective-permute-start.38 = (bf16[320,1024]{1,0:T(8,128)(2,1)}, bf16[320,1024]{1,0:T(8,128)(2,1)}, u32[]{:S(2)}, u32[]{:S(2)}) collective-permute-start(bf16[320,1024]{1,0:T(8,128)(2,1)} %add_convert_fusion.4), channel_id=1, source_target_pairs={{0,2},{1,3},{2,0},{3,1},{4,6},{5,7},{6,4},{7,5},{8,10},{9,11},{10,... | collective-permute-start | bytes 1966088 | tf_op jit(solution)/shard_map/ppermute | solution.py:588
  380.0 28.2 %collective-permute-start.37 = (bf16[320,1024]{1,0:T(8,128)(2,1)}, bf16[320,1024]{1,0:T(8,128)(2,1)}, u32[]{:S(2)}, u32[]{:S(2)}) collective-permute-start(bf16[320,1024]{1,0:T(8,128)(2,1)} %get-tuple-element.210), channel_id=1, source_target_pairs={{0,1},{1,0},{2,3},{3,2},{4,5},{5,4},{6,7},{7,6},{8,9},{9,8},{10,11... | collective-permute-start | bytes 1966088 | tf_op jit(solution)/shard_map/ppermute | solution.py:588
  397.0 259.6 %reduce-scatter.6.cloned.1.call-start = ((), (), s32[]{:S(2)}) async-start(), calls=%async_computation.6 | async-start | bytes 4718592 | tf_op jit(solution)/shard_map/reduce_scatter | solution.py:978
  446.3 18.5 %collective-permute-start.48 = (bf16[1024,512]{1,0:T(8,128)(2,1)S(1)}, bf16[1024,512]{1,0:T(8,128)(2,1)S(1)}, u32[]{:S(2)}, u32[]{:S(2)}) collective-permute-start(bf16[1024,512]{1,0:T(8,128)(2,1)S(1)} %get-tuple-element.469), channel_id=1, source_target_pairs={{0,1},{1,0},{2,3},{3,2},{4,5},{5,4},{6,7},{7,6},{8,9},{9,8},{10,11... | collective-permute-start | bytes 3145736 | tf_op jit(solution)/shard_map/ppermute | solution.py:588
  446.8 18.0 %collective-permute-start.49 = (bf16[1024,512]{1,0:T(8,128)(2,1)S(1)}, bf16[1024,512]{1,0:T(8,128)(2,1)S(1)}, u32[]{:S(2)}, u32[]{:S(2)}) collective-permute-start(bf16[1024,512]{1,0:T(8,128)(2,1)S(1)} %get-tuple-element.468), channel_id=1, source_target_pairs={{0,1},{1,0},{2,3},{3,2},{4,5},{5,4},{6,7},{7,6},{8,9},{9,8},{10,11... | collective-permute-start | bytes 3145736 | tf_op jit(solution)/shard_map/ppermute | solution.py:588
  498.1 225.7 %reduce-scatter.8.cloned.1.call-start = ((), (), s32[]{:S(2)}) async-start(), calls=%async_computation.7 | async-start | bytes 4718592 | tf_op jit(solution)/shard_map/reduce_scatter | solution.py:909
  535.1 19.2 %collective-permute-start.58 = (bf16[320,1024]{1,0:T(8,128)(2,1)}, bf16[320,1024]{1,0:T(8,128)(2,1)S(1)}, u32[]{:S(2)}, u32[]{:S(2)}) collective-permute-start(bf16[320,1024]{1,0:T(8,128)(2,1)} %add_convert_fusion.2), channel_id=1, source_target_pairs={{0,2},{1,3},{2,0},{3,1},{4,6},{5,7},{6,4},{7,5},{8,10},{9,11},{10,... | collective-permute-start | bytes 1966088 | tf_op jit(solution)/shard_map/ppermute | solution.py:588
  536.6 18.6 %collective-permute-start.57 = (bf16[320,1024]{1,0:T(8,128)(2,1)}, bf16[320,1024]{1,0:T(8,128)(2,1)}, u32[]{:S(2)}, u32[]{:S(2)}) collective-permute-start(bf16[320,1024]{1,0:T(8,128)(2,1)} %get-tuple-element.240), channel_id=1, source_target_pairs={{0,1},{1,0},{2,3},{3,2},{4,5},{5,4},{6,7},{7,6},{8,9},{9,8},{10,11... | collective-permute-start | bytes 1966088 | tf_op jit(solution)/shard_map/ppermute | solution.py:588
  617.9 31.0 %collective-permute-start.72 = (bf16[512,1024]{1,0:T(8,128)(2,1)S(1)}, bf16[512,1024]{1,0:T(8,128)(2,1)}, u32[]{:S(2)}, u32[]{:S(2)}) collective-permute-start(bf16[512,1024]{1,0:T(8,128)(2,1)S(1)} %fusion.14), channel_id=1, source_target_pairs={{0,4},{4,0},{8,12},{12,8},{16,20},{20,16},{24,28},{28,24},{1,5},{5... | collective-permute-start | bytes 3145736 | tf_op jit(solution)/shard_map/ppermute | solution.py:588
  623.2 19.1 %collective-permute-start.71 = (bf16[1,1,160,512]{3,2,1,0:T(8,128)(2,1)S(1)}, bf16[1,1,160,512]{3,2,1,0:T(8,128)(2,1)S(1)}, u32[]{:S(2)}, u32[]{:S(2)}) collective-permute-start(bf16[1,1,160,512]{3,2,1,0:T(8,128)(2,1)S(1)} %fusion.49), channel_id=1, source_target_pairs={{0,16},{4,20},{8,24},{12,28},{16,0},{20,4},{24,8},{28,12},{1,17},{... | collective-permute-start | bytes 491528 | tf_op jit(solution)/shard_map/ppermute | solution.py:588
  637.7 50.0 %collective-permute-start.76 = (bf16[512,1024]{1,0:T(8,128)(2,1)}, bf16[512,1024]{1,0:T(8,128)(2,1)}, u32[]{:S(2)}, u32[]{:S(2)}) collective-permute-start(bf16[512,1024]{1,0:T(8,128)(2,1)} %slice.702), channel_id=1, source_target_pairs={{0,4},{4,0},{8,12},{12,8},{16,20},{20,16},{24,28},{28,24},{1,5},{5... | collective-permute-start | bytes 3145736 | tf_op jit(solution)/shard_map/ppermute | solution.py:588
  655.8 31.9 %collective-permute-start.77 = (bf16[2,1,160,512]{3,2,1,0:T(8,128)(2,1)}, bf16[2,1,160,512]{3,2,1,0:T(8,128)(2,1)}, u32[]{:S(2)}, u32[]{:S(2)}) collective-permute-start(bf16[2,1,160,512]{3,2,1,0:T(8,128)(2,1)} %maximum_select_fusion.4), channel_id=1, source_target_pairs={{0,8},{4,12},{8,0},{12,4},{16,24},{20,28},{24,16},{28,20},{1,9},{5... | collective-permute-start | bytes 983048 | tf_op jit(solution)/shard_map/ppermute | solution.py:588
  668.2 19.5 %collective-permute-start.74 = (bf16[18,1024]{1,0:T(8,128)(2,1)S(1)}, bf16[18,1024]{1,0:T(8,128)(2,1)S(1)}, u32[]{:S(2)}, u32[]{:S(2)}) collective-permute-start(bf16[18,1024]{1,0:T(8,128)(2,1)S(1)} %convert_element_type.640), channel_id=1, source_target_pairs={{0,1},{1,0},{2,3},{3,2},{4,5},{5,4},{6,7},{7,6},{8,9},{9,8},{10,11... | collective-permute-start | bytes 110600 | tf_op jit(solution)/shard_map/ppermute | solution.py:588
  669.5 25.3 %collective-permute-start.75 = (bf16[128,1024]{1,0:T(8,128)(2,1)S(1)}, bf16[128,1024]{1,0:T(8,128)(2,1)S(1)}, u32[]{:S(2)}, u32[]{:S(2)}) collective-permute-start(bf16[128,1024]{1,0:T(8,128)(2,1)S(1)} %slice.701), channel_id=1, source_target_pairs={{0,16},{4,20},{8,24},{12,28},{16,0},{20,4},{24,8},{28,12},{1,17},{... | collective-permute-start | bytes 786440 | tf_op jit(solution)/shard_map/ppermute | solution.py:588
  694.8 19.3 %collective-permute-start.78 = (bf16[18,1024]{1,0:T(8,128)(2,1)S(1)}, bf16[18,1024]{1,0:T(8,128)(2,1)S(1)}, u32[]{:S(2)}, u32[]{:S(2)}) collective-permute-start(bf16[18,1024]{1,0:T(8,128)(2,1)S(1)} %fusion.80), channel_id=1, source_target_pairs={{0,2},{1,3},{2,0},{3,1},{4,6},{5,7},{6,4},{7,5},{8,10},{9,11},{10,... | collective-permute-start | bytes 110600 | tf_op jit(solution)/shard_map/ppermute | solution.py:588
  (228 other events, 1840.5 us)
Sparse Core Ops, SparseCore 0:
  22.1 145.9 all-gather.4
  170.2 85.7 all-gather.6
  258.7 71.5 all-gather.8
  397.1 88.5 reduce-scatter.3
  498.2 88.5 reduce-scatter.5
  590.3 112.8 reduce-scatter.7

commit v4 on v3

--- a/solution.py
+++ b/solution.py
@@ -991,7 +991,9 @@
     mod_local = jnp.stack(mod_grads[0] + mod_grads[1], axis=0)
     mod_local = tick(mod_local, cross_flows[0])
     mod_flow = Flow(summing_rows(mod_local, groups))
-    table_1 = bucket_sum(after(tables_sent[1], mod_local), index_tables[1], reaches[1])
+    summed_1 = tick(tables_sent[1], mod_flow)
+    summed_1 = tick(summed_1, mod_flow)
+    table_1 = bucket_sum(summed_1, index_tables[1], reaches[1])
     table_1 = tick(table_1, mod_flow, cross_flows[0], self_flows[0], kv_flow)
     table_0 = bucket_sum(after(tables_sent[0], table_1), index_tables[0], reaches[0])
     table_0 = tick(table_0, mod_flow, self_flows[0], cross_flows[0])

time: 769 us -> 777 us (1.010)
  waiting for transfers between devices: 205 us -> 215 us
    ppermute x89, waiting for transfers between devices: 198 us -> 208 us  [exchange(): return lax.ppermute(value, axis, [(i, i ^ bit) for i in range(size)])]
    unnamed x335 -> x339, local copies, waits for them, and re-layouts: 20.4 us -> 20.9 us
  transfers between devices with their start and end apart: 95 -> 95, of which waited for: 40 -> 40; matrix products, arithmetic and copies ran while one was open for 25% -> 24% of each run, Pallas kernels for 33% -> 32%
where the time goes in v4:
time: 777 us; the launch traced here: 766 us
  Pallas kernels  258 us (33%)
  waiting for transfers between devices  215 us (28%)
  matrix products  76.2 us (10%)
  other arithmetic  75.9 us (10%)
  starting transfers between devices  65.9 us (8%)
  local copies, waits for them, and re-layouts  55.9 us (7%)
  between operations  19.2 us (2%)
    ppermute x89, waiting for transfers between devices, exchange(): return lax.ppermute(value, axis, [(i, i ^ bit) for i in range(size)])  208 us
    pallas_call x6, Pallas kernels, weight_grad_call(): pl.pallas_call(functools.partial(weight_grad_kernel, counts, splits), gri...  74.9 us
    dot_general x42, matrix products, mm(): return lax.dot_general(a, b, dims, preferred_element_type=jnp.float32)  74.3 us
    ppermute x89, starting transfers between devices, exchange(): return lax.ppermute(value, axis, [(i, i ^ bit) for i in range(size)])  65.1 us
    pallas_call x4, Pallas kernels, feed_backward_call(): pl.pallas_call(feed_backward_kernel, grid=(1,), in_specs=[whole, whole, w...  32.8 us
    pallas_call x4, Pallas kernels, feed_forward_call(): pl.pallas_call(feed_forward_kernel, grid=(1,), in_specs=[whole, whole] +...  28.3 us
    pallas_call x2, Pallas kernels, bucket_sum(): pl.pallas_call(bucket_kernel, out_shape=jax.ShapeDtypeStruct((heads * (re...  26 us
    pallas_call x2, Pallas kernels, self_backward_call(): pl.pallas_call(functools.partial(self_backward_kernel, kind), out_shape=(...  25 us
  transfers between devices with their start and end apart: 95, of which 40 were waited for; matrix products, arithmetic and copies ran while one was open for 24% of the time, Pallas kernels for 32%

profile of v4, /device:TPU:0, one launch (start us, length us, event | category | flops | bytes accessed | tf_op | source)
XLA Modules:
  0.0 765.9 jit_solution(2868109750120619799)
XLA Ops:
  30.4 9.0 %collective-permute-done = bf16[1,1,128,1024]{3,2,1,0:T(8,128)(2,1)S(1)} collective-permute-done((bf16[1,1,128,1024]{3,2,1,0:T(8,128)(2,1)S(1)}, bf16[1,1,128,1024]{3,2,1,0:T(8,128)(2,1)S(1)}, u32[]{:S(2)}, u32[]{:S(2)}) %collective-permute-start) | collective-permute-done | bytes 262176 | tf_op jit(solution)/shard_map/ppermute | solution.py:588
  39.6 7.6 collective-permute-start.1
  51.6 26.1 %collective-permute-done.4 = bf16[2,4,384]{2,0,1:T(2,128)(2,1)S(1)} collective-permute-done((bf16[2,4,384]{2,0,1:T(2,128)(2,1)S(1)}, bf16[2,4,384]{2,0,1:T(2,128)(2,1)S(1)}, u32[]{:S(2)}, u32[]{:S(2)}) %collective-permute-start.4) | collective-permute-done | bytes 6176 | tf_op jit(solution)/shard_map/ppermute | solution.py:588
  88.0 7.9 %shard_map.644.bias_ref = bf16[4,320,384]{2,1,0:T(8,128)(2,1)} custom-call(f32[4,16,128]{2,1,0:T(8,128)} %reshape.604.table_ref, s32[320,384]{1,0:T(8,128)} %pad.12.index_ref), custom_call_target="tpu_custom_call" | custom-call | flops 3000000000 | bytes 9000000 | tf_op jit(solution)/shard_map/pallas_call | solution.py:97
  95.8 33.0 %collective-permute-done.2 = bf16[4,1,128,1024]{3,2,1,0:T(8,128)(2,1)} collective-permute-done((bf16[4,1,128,1024]{3,2,1,0:T(8,128)(2,1)S(1)}, bf16[4,1,128,1024]{3,2,1,0:T(8,128)(2,1)}, u32[]{:S(2)}, u32[]{:S(2)}) %collective-permute-start.2) | collective-permute-done | bytes 1048608 | tf_op jit(solution)/shard_map/ppermute | solution.py:588
  140.7 7.7 %self_forward.2 = (bf16[1280,256]{1,0:T(8,128)(2,1)}, bf16[5,4,256,256]{3,2,1,0:T(8,128)(2,1)}) custom-call(s32[1]{0:T(128)} %bitcast.2.position_ref, bf16[1280,768]{1,0:T(8,128)(2,1)} %pad_maximum_fusion.5.qkv_ref, bf16[4,256,256]{2,1,0:T(8,128)(2,1)} %shard_map.643.bias_ref), custom_call_target="tpu_custom_call" | custom-call | flops 4000000000 | bytes 12000000 | tf_op jit(solution)/shard_map/self_forward/pallas_call | solution.py:189
  157.2 13.3 %collective-permute-done.11 = bf16[320,1024]{1,0:T(8,128)(2,1)S(1)} collective-permute-done((bf16[320,1024]{1,0:T(8,128)(2,1)}, bf16[320,1024]{1,0:T(8,128)(2,1)S(1)}, u32[]{:S(2)}, u32[]{:S(2)}) %collective-permute-start.11) | collective-permute-done | bytes 655392 | tf_op jit(solution)/shard_map/ppermute | solution.py:588
  205.5 7.2 feed_forward.4
  220.6 7.1 feed_forward.5
  232.6 15.5 %collective-permute-done.22 = bf16[320,1024]{1,0:T(8,128)(2,1)S(1)} collective-permute-done((bf16[320,1024]{1,0:T(8,128)(2,1)S(1)}, bf16[320,1024]{1,0:T(8,128)(2,1)S(1)}, u32[]{:S(2)}, u32[]{:S(2)}) %collective-permute-start.22) | collective-permute-done | bytes 655392 | tf_op jit(solution)/shard_map/ppermute | solution.py:588
  276.4 8.1 %self_forward.3 = (bf16[1280,256]{1,0:T(8,128)(2,1)}, bf16[4,4,320,320]{3,2,1,0:T(8,128)(2,1)}) custom-call(s32[1]{0:T(128)} %bitcast.2.position_ref, bf16[1280,768]{1,0:T(8,128)(2,1)} %pad_maximum_fusion.6.qkv_ref, bf16[4,320,384]{2,1,0:T(8,128)(2,1)} %shard_map.644.bias_ref), custom_call_target="tpu_custom_call" | custom-call | flops 4000000000 | bytes 12000000 | tf_op jit(solution)/shard_map/self_forward/pallas_call | solution.py:189
  293.7 13.1 %collective-permute-done.28 = bf16[320,1024]{1,0:T(8,128)(2,1)S(1)} collective-permute-done((bf16[320,1024]{1,0:T(8,128)(2,1)S(1)}, bf16[320,1024]{1,0:T(8,128)(2,1)S(1)}, u32[]{:S(2)}, u32[]{:S(2)}) %collective-permute-start.28) | collective-permute-done | bytes 655392 | tf_op jit(solution)/shard_map/ppermute | solution.py:588
  330.2 7.0 feed_forward.6
  341.4 8.0 %feed_backward.4 = (bf16[640,1024]{1,0:T(8,128)(2,1)}, bf16[320,1024]{1,0:T(8,128)(2,1)}, bf16[320,1024]{1,0:T(8,128)(2,1)}) custom-call(bf16[320,1024]{1,0:T(8,128)(2,1)} %multiply_convert_fusion.5.a_ref.refs_4_, bf16[320,1024]{1,0:T(8,128)(2,1)} %collective-permute-done.39.b_ref.refs_5_, bf16[640,1024]{1,0:T(8,128)(2,1)} %get-tuple-element.208.hidden_ref, ...), custom_call_target="tpu_custom_call" | custom-call | flops 4000000000 | bytes 12000000 | tf_op jit(solution)/shard_map/feed_backward/pallas_call | solution.py:398
  356.0 7.0 feed_forward.7
  363.8 8.5 %feed_backward.5 = (bf16[640,1024]{1,0:T(8,128)(2,1)}, bf16[320,1024]{1,0:T(8,128)(2,1)}, bf16[320,1024]{1,0:T(8,128)(2,1)}) custom-call(bf16[320,1024]{1,0:T(8,128)(2,1)} %collective-permute-done.40.a_ref.refs_6_, bf16[320,1024]{1,0:T(8,128)(2,1)} %copy-done.157, bf16[640,1024]{1,0:T(8,128)(2,1)} %get-tuple-element.218.hidden_ref, ...), custom_call_target="tpu_custom_call" | custom-call | flops 4000000000 | bytes 12000000 | tf_op jit(solution)/shard_map/feed_backward/pallas_call | solution.py:398
  381.0 16.2 %weight_grad.6 = bf16[1024,2048]{1,0:T(8,128)(2,1)} custom-call(s32[8]{0:T(128)} %iota.24.order_ref, bf16[320,1024]{1,0:T(8,128)(2,1)} %add_convert_fusion.5.a_ref.refs_0_, bf16[320,1024]{1,0:T(8,128)(2,1)} %collective-permute-done.33.b_ref.refs_1_, bf16[320,1024]{1,0:T(8,128)(2,1)} %collective-permute-done.34.a_ref.refs_2_, bf16[320,1024]{1,0:T(8,128)(2,1)} %copy-done.155, ...), custom_call_target="tpu_custom_call" | custom-call | flops 6000000000 | bytes 18000000 | tf_op jit(solution)/shard_map/weight_grad/pallas_call | solution.py:478
  400.8 7.7 %collective-permute-done.38 = bf16[320,1024]{1,0:T(8,128)(2,1)} collective-permute-done((bf16[320,1024]{1,0:T(8,128)(2,1)}, bf16[320,1024]{1,0:T(8,128)(2,1)}, u32[]{:S(2)}, u32[]{:S(2)}) %collective-permute-start.38) | collective-permute-done | bytes 655392 | tf_op jit(solution)/shard_map/ppermute | solution.py:588
  430.2 9.1 %weight_grad.7 = bf16[4,1024,512]{2,1,0:T(8,128)(2,1)} custom-call(s32[8]{0:T(128)} %iota.25.order_ref, bf16[320,1024]{1,0:T(8,128)(2,1)} %copy-done.41, bf16[320,1024]{1,0:T(8,128)(2,1)} %copy-done.46, bf16[320,1024]{1,0:T(8,128)(2,1)} %get-tuple-element.227.refs_2_, bf16[320,1024]{1,0:T(8,128)(2,1)} %get-tuple-element.205.refs_3_), custom_call_target="tpu_custom_call" | custom-call | flops 6000000000 | bytes 18000000 | tf_op jit(solution)/shard_map/weight_grad/pallas_call | solution.py:478
  451.3 13.7 %self_backward.2 = (bf16[1280,768]{1,0:T(8,128)(2,1)}, f32[4,320,320]{2,1,0:T(8,128)}) custom-call(s32[1]{0:T(128)} %bitcast.2.position_ref, bf16[1280,768]{1,0:T(8,128)(2,1)} %pad_maximum_fusion.6.qkv_ref, bf16[4,4,320,320]{3,2,1,0:T(8,128)(2,1)} %get-tuple-element.228.probs_ref, bf16[1280,256]{1,0:T(8,128)(2,1)} %pad_maximum_fusion.10.grad_ref), custom_call_target="tpu_custom_call" | custom-call | flops 6499999744 | bytes 19500000 | tf_op jit(solution)/shard_map/self_backward/pallas_call | solution.py:245
  478.3 11.8 %weight_grad.8 = bf16[1024,1024]{1,0:T(8,128)(2,1)} custom-call(s32[8]{0:T(128)} %iota.26.order_ref, bf16[320,1024]{1,0:T(8,128)(2,1)} %add_convert_fusion.8.refs_0_, bf16[320,1024]{1,0:T(8,128)(2,1)} %collective-permute-done.23.refs_1_, bf16[320,1024]{1,0:T(8,128)(2,1)} %collective-permute-done.24.refs_2_, bf16[320,1024]{1,0:T(8,128)(2,1)} %copy-done.149, ...), custom_call_target="tpu_custom_call" | custom-call | flops 6000000000 | bytes 18000000 | tf_op jit(solution)/shard_map/weight_grad/pallas_call | solution.py:478
  506.2 8.0 %feed_backward.6 = (bf16[640,1024]{1,0:T(8,128)(2,1)}, bf16[320,1024]{1,0:T(8,128)(2,1)}, bf16[320,1024]{1,0:T(8,128)(2,1)}) custom-call(bf16[320,1024]{1,0:T(8,128)(2,1)} %copy-done.43, bf16[320,1024]{1,0:T(8,128)(2,1)} %copy-done.151, bf16[640,1024]{1,0:T(8,128)(2,1)} %get-tuple-element.196.hidden_ref, bf16[1024,2048]{1,0:T(8,128)(2,1)} %slice.651.up_ref.down_ref, ...), custom_call_target="tpu_custom_call" | custom-call | flops 4000000000 | bytes 12000000 | tf_op jit(solution)/shard_map/feed_backward/pallas_call | solution.py:398
  523.6 8.3 %feed_backward.7 = (bf16[640,1024]{1,0:T(8,128)(2,1)}, bf16[320,1024]{1,0:T(8,128)(2,1)}, bf16[320,1024]{1,0:T(8,128)(2,1)}) custom-call(bf16[320,1024]{1,0:T(8,128)(2,1)} %collective-permute-done.54.a_ref.refs_6_, bf16[320,1024]{1,0:T(8,128)(2,1)} %copy-done.153, bf16[640,1024]{1,0:T(8,128)(2,1)} %get-tuple-element.240.hidden_ref, ...), custom_call_target="tpu_custom_call" | custom-call | flops 4000000000 | bytes 12000000 | tf_op jit(solution)/shard_map/feed_backward/pallas_call | solution.py:398
  537.7 16.5 %weight_grad.9 = bf16[1024,2048]{1,0:T(8,128)(2,1)} custom-call(s32[8]{0:T(128)} %iota.27.order_ref, bf16[320,1024]{1,0:T(8,128)(2,1)} %copy-done.39, bf16[320,1024]{1,0:T(8,128)(2,1)} %copy-done.146, bf16[320,1024]{1,0:T(8,128)(2,1)} %copy-done.147, bf16[320,1024]{1,0:T(8,128)(2,1)} %copy-done.148, bf16[320,1024]{1,0:T(8,128)(2,1)} %copy-done.43, ...), custom_call_target="tpu_custom_call" | custom-call | flops 6000000000 | bytes 18000000 | tf_op jit(solution)/shard_map/weight_grad/pallas_call | solution.py:478
  577.6 9.3 %weight_grad.10 = bf16[4,1024,512]{2,1,0:T(8,128)(2,1)} custom-call(s32[8]{0:T(128)} %broadcast_xor_fusion.order_ref, bf16[320,1024]{1,0:T(8,128)(2,1)} %copy-done.38, bf16[320,1024]{1,0:T(8,128)(2,1)} %copy-done.45, bf16[320,1024]{1,0:T(8,128)(2,1)} %get-tuple-element.250.refs_2_, bf16[320,1024]{1,0:T(8,128)(2,1)} %get-tuple-element.193.refs_3_), custom_call_target="tpu_custom_call" | custom-call | flops 6000000000 | bytes 18000000 | tf_op jit(solution)/shard_map/weight_grad/pallas_call | solution.py:478
  602.6 11.2 %self_backward.3 = (bf16[1280,768]{1,0:T(8,128)(2,1)}, f32[4,256,256]{2,1,0:T(8,128)}) custom-call(s32[1]{0:T(128)} %bitcast.2.position_ref, bf16[1280,768]{1,0:T(8,128)(2,1)} %pad_maximum_fusion.5.qkv_ref, bf16[5,4,256,256]{3,2,1,0:T(8,128)(2,1)} %get-tuple-element.256.probs_ref, bf16[1280,256]{1,0:T(8,128)(2,1)} %pad_maximum_fusion.11.grad_ref), custom_call_target="tpu_custom_call" | custom-call | flops 6499999744 | bytes 19500000 | tf_op jit(solution)/shard_map/self_backward/pallas_call | solution.py:245
  623.8 12.0 %weight_grad.11 = bf16[1024,1024]{1,0:T(8,128)(2,1)} custom-call(s32[8]{0:T(128)} %broadcast_xor_fusion.order_ref, bf16[320,1024]{1,0:T(8,128)(2,1)} %add_convert_fusion.13.refs_0_, bf16[320,1024]{1,0:T(8,128)(2,1)} %collective-permute-done.6.refs_1_, bf16[320,1024]{1,0:T(8,128)(2,1)} %collective-permute-done.7.refs_2_, ...), custom_call_target="tpu_custom_call" | custom-call | flops 6000000000 | bytes 18000000 | tf_op jit(solution)/shard_map/weight_grad/pallas_call | solution.py:478
  642.5 8.3 %collective-permute-done.72 = bf16[512,1024]{1,0:T(8,128)(2,1)} collective-permute-done((bf16[512,1024]{1,0:T(8,128)(2,1)}, bf16[512,1024]{1,0:T(8,128)(2,1)}, u32[]{:S(2)}, u32[]{:S(2)}) %collective-permute-start.72) | collective-permute-done | bytes 1048608 | tf_op jit(solution)/shard_map/ppermute | solution.py:588
  676.5 16.8 %shard_map.645 = f32[128,64]{1,0:T(8,128)} custom-call(f32[4,320,320]{2,1,0:T(8,128)} %get-tuple-element.282.sum_ref, s32[320,320]{1,0:T(8,128)} %index_ref.4), custom_call_target="tpu_custom_call" | custom-call | flops 6499999744 | bytes 19500000 | tf_op jit(solution)/shard_map/pallas_call | solution.py:123
  694.3 10.4 %collective-permute-done.76 = bf16[1,1,18,1024]{3,2,1,0:T(8,128)(2,1)S(1)} collective-permute-done((bf16[1,1,18,1024]{3,2,1,0:T(8,128)(2,1)S(1)}, bf16[1,1,18,1024]{3,2,1,0:T(8,128)(2,1)S(1)}, u32[]{:S(2)}, u32[]{:S(2)}) %collective-permute-start.76) | collective-permute-done | bytes 36896 | tf_op jit(solution)/shard_map/ppermute | solution.py:588
  705.3 9.2 %shard_map.646 = f32[64,64]{1,0:T(8,128)} custom-call(f32[4,256,256]{2,1,0:T(8,128)} %get-tuple-element.288.sum_ref, s32[256,256]{1,0:T(8,128)} %index_ref.5), custom_call_target="tpu_custom_call" | custom-call | flops 6499999744 | bytes 19500000 | tf_op jit(solution)/shard_map/pallas_call | solution.py:123
  739.6 7.2 adam.3
  (752 shorter events, 384.8 us)
Async XLA Ops:
  7.2 167.7 %all-gather.5.cloned.1.call-start = ((), (), s32[]{:S(2)}) async-start(), calls=%async_computation.3 | async-start | bytes 8257536 | tf_op jit(solution)/shard_map/all_gather | solution.py:804
  21.9 234.0 %all-gather.7.cloned.1.call-start = ((), (), s32[]{:S(2)}) async-start(), calls=%async_computation.4 | async-start | bytes 5898240 | tf_op jit(solution)/shard_map/all_gather | solution.py:804
  25.8 23.0 %collective-permute-start.3 = (bf16[1,4,384]{2,0,1:T(2,128)(2,1)S(1)}, bf16[1,4,384]{2,0,1:T(2,128)(2,1)S(1)}, u32[]{:S(2)}, u32[]{:S(2)}) collective-permute-start(bf16[1,4,384]{2,0,1:T(2,128)(2,1)S(1)} %copy.101), channel_id=1, source_target_pairs={{0,4},{4,0},{8,12},{12,8},{16,20},{20,16},{24,28},{28,24},{1,5},{5... | collective-permute-start | bytes 9224 | tf_op jit(solution)/shard_map/ppermute | solution.py:588
  39.6 40.0 %collective-permute-start.1 = (bf16[2,1,128,1024]{3,2,1,0:T(8,128)(2,1)S(1)}, bf16[2,1,128,1024]{3,2,1,0:T(8,128)(2,1)}, u32[]{:S(2)}, u32[]{:S(2)}) collective-permute-start(bf16[2,1,128,1024]{3,2,1,0:T(8,128)(2,1)S(1)} %maximum_select_fusion.3), channel_id=1, source_target_pairs={{0,8},{4,12},{8,0},{12,4},{16,24},{20,28},{24,16},{28,20},{1,9},{5... | collective-permute-start | bytes 1572872 | tf_op jit(solution)/shard_map/ppermute | solution.py:588
  48.8 29.0 %collective-permute-start.4 = (bf16[2,4,384]{2,0,1:T(2,128)(2,1)S(1)}, bf16[2,4,384]{2,0,1:T(2,128)(2,1)S(1)}, u32[]{:S(2)}, u32[]{:S(2)}) collective-permute-start(bf16[2,4,384]{2,0,1:T(2,128)(2,1)S(1)} %broadcast_select_fusion), channel_id=1, source_target_pairs={{0,8},{4,12},{8,0},{12,4},{16,24},{20,28},{24,16},{28,20},{1,9},{5... | collective-permute-start | bytes 18440 | tf_op jit(solution)/shard_map/ppermute | solution.py:588
  50.1 84.8 %collective-permute-start.7 = (bf16[320,1024]{1,0:T(8,128)(2,1)}, bf16[320,1024]{1,0:T(8,128)(2,1)}, u32[]{:S(2)}, u32[]{:S(2)}) collective-permute-start(bf16[320,1024]{1,0:T(8,128)(2,1)} %add_convert_fusion.13.refs_0_), channel_id=1, source_target_pairs={{0,2},{1,3},{2,0},{3,1},{4,6},{5,7},{6,4},{7,5},{8,10},{9,11},{10,... | collective-permute-start | bytes 1966088 | tf_op jit(solution)/shard_map/ppermute | solution.py:588
  50.8 82.3 %collective-permute-start.6 = (bf16[320,1024]{1,0:T(8,128)(2,1)}, bf16[320,1024]{1,0:T(8,128)(2,1)}, u32[]{:S(2)}, u32[]{:S(2)}) collective-permute-start(bf16[320,1024]{1,0:T(8,128)(2,1)} %add_convert_fusion.13.refs_0_), channel_id=1, source_target_pairs={{0,1},{1,0},{2,3},{3,2},{4,5},{5,4},{6,7},{7,6},{8,9},{9,8},{10,11... | collective-permute-start | bytes 1966088 | tf_op jit(solution)/shard_map/ppermute | solution.py:588
  81.1 47.8 %collective-permute-start.2 = (bf16[4,1,128,1024]{3,2,1,0:T(8,128)(2,1)S(1)}, bf16[4,1,128,1024]{3,2,1,0:T(8,128)(2,1)}, u32[]{:S(2)}, u32[]{:S(2)}) collective-permute-start(bf16[4,1,128,1024]{3,2,1,0:T(8,128)(2,1)S(1)} %bitcast.186), channel_id=1, source_target_pairs={{0,4},{4,0},{8,12},{12,8},{16,20},{20,16},{24,28},{28,24},{1,5},{5... | collective-permute-start | bytes 3145736 | tf_op jit(solution)/shard_map/ppermute | solution.py:588
  157.1 173.1 %all-gather.9.cloned.1.call-start = ((), (), s32[]{:S(2)}) async-start(), calls=%async_computation.8 | async-start | bytes 4718592 | tf_op jit(solution)/shard_map/all_gather | solution.py:810
  251.1 305.8 %reduce-scatter.4.cloned.1.call-start = ((), (), s32[]{:S(2)}) async-start(), calls=%async_computation.5 | async-start | bytes 4718592 | tf_op jit(solution)/shard_map/reduce_scatter | solution.py:909
  251.4 17.9 %collective-permute-start.24 = (bf16[320,1024]{1,0:T(8,128)(2,1)}, bf16[320,1024]{1,0:T(8,128)(2,1)}, u32[]{:S(2)}, u32[]{:S(2)}) collective-permute-start(bf16[320,1024]{1,0:T(8,128)(2,1)} %add_convert_fusion.8.refs_0_), channel_id=1, source_target_pairs={{0,2},{1,3},{2,0},{3,1},{4,6},{5,7},{6,4},{7,5},{8,10},{9,11},{10,... | collective-permute-start | bytes 1966088 | tf_op jit(solution)/shard_map/ppermute | solution.py:588
  259.1 27.5 %collective-permute-start.30 = (bf16[128,512]{1,0:T(8,128)(2,1)S(1)}, bf16[128,512]{1,0:T(8,128)(2,1)S(1)}, u32[]{:S(2)}, u32[]{:S(2)}) collective-permute-start(bf16[128,512]{1,0:T(8,128)(2,1)S(1)} %convolution_convert_fusion.36), channel_id=1, source_target_pairs={{0,1},{1,0},{2,3},{3,2},{4,5},{5,4},{6,7},{7,6},{8,9},{9,8},{10,11... | collective-permute-start | bytes 393224 | tf_op jit(solution)/shard_map/ppermute | solution.py:588
  262.3 30.3 %collective-permute-start.29 = (bf16[1024,1024]{1,0:T(8,128)(2,1)}, bf16[1024,1024]{1,0:T(8,128)(2,1)S(1)}, u32[]{:S(2)}, u32[]{:S(2)}) collective-permute-start(bf16[1024,1024]{1,0:T(8,128)(2,1)} %slice.656), channel_id=1, source_target_pairs={{0,1},{1,0},{2,3},{3,2},{4,5},{5,4},{6,7},{7,6},{8,9},{9,8},{10,11... | collective-permute-start | bytes 6291464 | tf_op jit(solution)/shard_map/ppermute | solution.py:588
  271.6 19.5 %collective-permute-start.32 = (bf16[128,512]{1,0:T(8,128)(2,1)S(1)}, bf16[128,512]{1,0:T(8,128)(2,1)S(1)}, u32[]{:S(2)}, u32[]{:S(2)}) collective-permute-start(bf16[128,512]{1,0:T(8,128)(2,1)S(1)} %collective-permute-done.31), channel_id=1, source_target_pairs={{0,1},{1,0},{2,3},{3,2},{4,5},{5,4},{6,7},{7,6},{8,9},{9,8},{10,11... | collective-permute-start | bytes 393224 | tf_op jit(solution)/shard_map/ppermute | solution.py:588
  323.6 17.8 %collective-permute-start.34 = (bf16[320,1024]{1,0:T(8,128)(2,1)}, bf16[320,1024]{1,0:T(8,128)(2,1)}, u32[]{:S(2)}, u32[]{:S(2)}) collective-permute-start(bf16[320,1024]{1,0:T(8,128)(2,1)} %add_convert_fusion.5.a_ref.refs_0_), channel_id=1, source_target_pairs={{0,2},{1,3},{2,0},{3,1},{4,6},{5,7},{6,4},{7,5},{8,10},{9,11},{10,... | collective-permute-start | bytes 1966088 | tf_op jit(solution)/shard_map/ppermute | solution.py:588
  326.0 29.1 %collective-permute-start.40 = (bf16[320,1024]{1,0:T(8,128)(2,1)}, bf16[320,1024]{1,0:T(8,128)(2,1)}, u32[]{:S(2)}, u32[]{:S(2)}) collective-permute-start(bf16[320,1024]{1,0:T(8,128)(2,1)} %multiply_convert_fusion.5.a_ref.refs_4_), channel_id=1, source_target_pairs={{0,2},{1,3},{2,0},{3,1},{4,6},{5,7},{6,4},{7,5},{8,10},{9,11},{10,... | collective-permute-start | bytes 1966088 | tf_op jit(solution)/shard_map/ppermute | solution.py:588
  377.1 20.3 %collective-permute-start.44 = (bf16[320,1024]{1,0:T(8,128)(2,1)}, bf16[320,1024]{1,0:T(8,128)(2,1)}, u32[]{:S(2)}, u32[]{:S(2)}) collective-permute-start(bf16[320,1024]{1,0:T(8,128)(2,1)} %add_convert_fusion.3), channel_id=1, source_target_pairs={{0,2},{1,3},{2,0},{3,1},{4,6},{5,7},{6,4},{7,5},{8,10},{9,11},{10,... | collective-permute-start | bytes 1966088 | tf_op jit(solution)/shard_map/ppermute | solution.py:588
  378.3 19.1 %collective-permute-start.43 = (bf16[320,1024]{1,0:T(8,128)(2,1)}, bf16[320,1024]{1,0:T(8,128)(2,1)}, u32[]{:S(2)}, u32[]{:S(2)}) collective-permute-start(bf16[320,1024]{1,0:T(8,128)(2,1)} %get-tuple-element.221), channel_id=1, source_target_pairs={{0,1},{1,0},{2,3},{3,2},{4,5},{5,4},{6,7},{7,6},{8,9},{9,8},{10,11... | collective-permute-start | bytes 1966088 | tf_op jit(solution)/shard_map/ppermute | solution.py:588
  379.5 29.0 %collective-permute-start.38 = (bf16[320,1024]{1,0:T(8,128)(2,1)}, bf16[320,1024]{1,0:T(8,128)(2,1)}, u32[]{:S(2)}, u32[]{:S(2)}) collective-permute-start(bf16[320,1024]{1,0:T(8,128)(2,1)} %add_convert_fusion.4), channel_id=1, source_target_pairs={{0,2},{1,3},{2,0},{3,1},{4,6},{5,7},{6,4},{7,5},{8,10},{9,11},{10,... | collective-permute-start | bytes 1966088 | tf_op jit(solution)/shard_map/ppermute | solution.py:588
  380.3 28.2 %collective-permute-start.37 = (bf16[320,1024]{1,0:T(8,128)(2,1)}, bf16[320,1024]{1,0:T(8,128)(2,1)}, u32[]{:S(2)}, u32[]{:S(2)}) collective-permute-start(bf16[320,1024]{1,0:T(8,128)(2,1)} %get-tuple-element.213), channel_id=1, source_target_pairs={{0,1},{1,0},{2,3},{3,2},{4,5},{5,4},{6,7},{7,6},{8,9},{9,8},{10,11... | collective-permute-start | bytes 1966088 | tf_op jit(solution)/shard_map/ppermute | solution.py:588
  397.3 261.3 %reduce-scatter.6.cloned.1.call-start = ((), (), s32[]{:S(2)}) async-start(), calls=%async_computation.6 | async-start | bytes 4718592 | tf_op jit(solution)/shard_map/reduce_scatter | solution.py:978
  446.5 18.5 %collective-permute-start.48 = (bf16[1024,512]{1,0:T(8,128)(2,1)S(1)}, bf16[1024,512]{1,0:T(8,128)(2,1)S(1)}, u32[]{:S(2)}, u32[]{:S(2)}) collective-permute-start(bf16[1024,512]{1,0:T(8,128)(2,1)S(1)} %get-tuple-element.475), channel_id=1, source_target_pairs={{0,1},{1,0},{2,3},{3,2},{4,5},{5,4},{6,7},{7,6},{8,9},{9,8},{10,11... | collective-permute-start | bytes 3145736 | tf_op jit(solution)/shard_map/ppermute | solution.py:588
  447.1 18.0 %collective-permute-start.49 = (bf16[1024,512]{1,0:T(8,128)(2,1)S(1)}, bf16[1024,512]{1,0:T(8,128)(2,1)S(1)}, u32[]{:S(2)}, u32[]{:S(2)}) collective-permute-start(bf16[1024,512]{1,0:T(8,128)(2,1)S(1)} %get-tuple-element.474), channel_id=1, source_target_pairs={{0,1},{1,0},{2,3},{3,2},{4,5},{5,4},{6,7},{7,6},{8,9},{9,8},{10,11... | collective-permute-start | bytes 3145736 | tf_op jit(solution)/shard_map/ppermute | solution.py:588
  498.4 241.2 %reduce-scatter.8.cloned.1.call-start = ((), (), s32[]{:S(2)}) async-start(), calls=%async_computation.7 | async-start | bytes 4718592 | tf_op jit(solution)/shard_map/reduce_scatter | solution.py:909
  535.4 18.9 %collective-permute-start.58 = (bf16[320,1024]{1,0:T(8,128)(2,1)}, bf16[320,1024]{1,0:T(8,128)(2,1)S(1)}, u32[]{:S(2)}, u32[]{:S(2)}) collective-permute-start(bf16[320,1024]{1,0:T(8,128)(2,1)} %add_convert_fusion.2), channel_id=1, source_target_pairs={{0,2},{1,3},{2,0},{3,1},{4,6},{5,7},{6,4},{7,5},{8,10},{9,11},{10,... | collective-permute-start | bytes 1966088 | tf_op jit(solution)/shard_map/ppermute | solution.py:588
  536.5 18.6 %collective-permute-start.57 = (bf16[320,1024]{1,0:T(8,128)(2,1)}, bf16[320,1024]{1,0:T(8,128)(2,1)}, u32[]{:S(2)}, u32[]{:S(2)}) collective-permute-start(bf16[320,1024]{1,0:T(8,128)(2,1)} %get-tuple-element.243), channel_id=1, source_target_pairs={{0,1},{1,0},{2,3},{3,2},{4,5},{5,4},{6,7},{7,6},{8,9},{9,8},{10,11... | collective-permute-start | bytes 1966088 | tf_op jit(solution)/shard_map/ppermute | solution.py:588
  619.0 31.8 %collective-permute-start.72 = (bf16[512,1024]{1,0:T(8,128)(2,1)}, bf16[512,1024]{1,0:T(8,128)(2,1)}, u32[]{:S(2)}, u32[]{:S(2)}) collective-permute-start(bf16[512,1024]{1,0:T(8,128)(2,1)} %fusion.14), channel_id=1, source_target_pairs={{0,4},{4,0},{8,12},{12,8},{16,20},{20,16},{24,28},{28,24},{1,5},{5... | collective-permute-start | bytes 3145736 | tf_op jit(solution)/shard_map/ppermute | solution.py:588
  623.7 18.8 %collective-permute-start.71 = (bf16[1,1,160,512]{3,2,1,0:T(8,128)(2,1)S(1)}, bf16[1,1,160,512]{3,2,1,0:T(8,128)(2,1)S(1)}, u32[]{:S(2)}, u32[]{:S(2)}) collective-permute-start(bf16[1,1,160,512]{3,2,1,0:T(8,128)(2,1)S(1)} %fusion.49), channel_id=1, source_target_pairs={{0,16},{4,20},{8,24},{12,28},{16,0},{20,4},{24,8},{28,12},{1,17},{... | collective-permute-start | bytes 491528 | tf_op jit(solution)/shard_map/ppermute | solution.py:588
  638.2 56.1 %collective-permute-start.78 = (bf16[512,1024]{1,0:T(8,128)(2,1)}, bf16[512,1024]{1,0:T(8,128)(2,1)}, u32[]{:S(2)}, u32[]{:S(2)}) collective-permute-start(bf16[512,1024]{1,0:T(8,128)(2,1)} %slice.702), channel_id=1, source_target_pairs={{0,4},{4,0},{8,12},{12,8},{16,20},{20,16},{24,28},{28,24},{1,5},{5... | collective-permute-start | bytes 3145736 | tf_op jit(solution)/shard_map/ppermute | solution.py:588
  658.5 35.7 %collective-permute-start.79 = (bf16[2,1,160,512]{3,2,1,0:T(8,128)(2,1)}, bf16[2,1,160,512]{3,2,1,0:T(8,128)(2,1)}, u32[]{:S(2)}, u32[]{:S(2)}) collective-permute-start(bf16[2,1,160,512]{3,2,1,0:T(8,128)(2,1)} %maximum_select_fusion.4), channel_id=1, source_target_pairs={{0,8},{4,12},{8,0},{12,4},{16,24},{20,28},{24,16},{28,20},{1,9},{5... | collective-permute-start | bytes 983048 | tf_op jit(solution)/shard_map/ppermute | solution.py:588
  673.4 31.2 %collective-permute-start.77 = (bf16[128,1024]{1,0:T(8,128)(2,1)S(1)}, bf16[128,1024]{1,0:T(8,128)(2,1)S(1)}, u32[]{:S(2)}, u32[]{:S(2)}) collective-permute-start(bf16[128,1024]{1,0:T(8,128)(2,1)S(1)} %slice.701), channel_id=1, source_target_pairs={{0,16},{4,20},{8,24},{12,28},{16,0},{20,4},{24,8},{28,12},{1,17},{... | collective-permute-start | bytes 786440 | tf_op jit(solution)/shard_map/ppermute | solution.py:588
  676.3 28.3 %collective-permute-start.76 = (bf16[1,1,18,1024]{3,2,1,0:T(8,128)(2,1)S(1)}, bf16[1,1,18,1024]{3,2,1,0:T(8,128)(2,1)S(1)}, u32[]{:S(2)}, u32[]{:S(2)}) collective-permute-start(bf16[1,1,18,1024]{3,2,1,0:T(8,128)(2,1)S(1)} %fusion.81), channel_id=1, source_target_pairs={{0,16},{4,20},{8,24},{12,28},{16,0},{20,4},{24,8},{28,12},{1,17},{... | collective-permute-start | bytes 110600 | tf_op jit(solution)/shard_map/ppermute | solution.py:588
  (230 other events, 1871.1 us)
Sparse Core Ops, SparseCore 0:
  22.1 145.9 all-gather.4
  170.2 85.6 all-gather.6
  258.6 71.5 all-gather.8
  397.4 88.6 reduce-scatter.3
  498.5 88.3 reduce-scatter.5
  590.4 118.3 reduce-scatter.7
